TPU v7x, 128 devices: a whole 4x4x4 slice. The times are simulated.
128 devices in a mesh: dp: 16 (over x, y), expert: 8 (over z, core).
Axes of the slice: x: 4, y: 4, z: 4, core: 2. Of those that a mesh axis runs over, the one named last changes fastest.
Arguments:
- residual: bfloat16 [1024, 4096], P('dp', 'expert'), may hold values from -6 to 6
- queries: bfloat16 [1024, 4096], P('dp', 'expert'), may hold values from -25 to 25
- cache_keys: bfloat16 [36864, 1024], P('dp', 'expert'), may hold values from -5 to 5
- cache_values: bfloat16 [36864, 1024], P('dp', 'expert'), may hold values from -18 to 18
- node_of_position: int32 [36864], P('dp'), may hold values from -1 to 36, as said below
- parent: int32 [37], replicated, may hold values from 0 to 4, as said below
- leaf_ids: int32 [1024], P('dp'), may hold values from 5 to 36
- routes: int32 [1024, 2], P('dp'), may hold values from 0 to 7, all different within a row; in each aligned block of 64 rows (0 to 63, 64 to 127, ...) at most 32 rows name the same one
- gate_weights: bfloat16 [1024, 2], P('dp'), may hold values from 0.19921875 to 0.796875
- norm_gain: bfloat16 [4096], replicated, may hold values from 0.5 to 1.5
- w_gate: bfloat16 [8, 4096, 14336], P('expert', None, 'dp'), may hold values from -0.09375 to 0.09375
- w_up: bfloat16 [8, 4096, 14336], P('expert', None, 'dp'), may hold values from -0.09375 to 0.09375
- w_down: bfloat16 [8, 14336, 4096], P('expert', 'dp'), may hold values from -0.046875 to 0.046875
Outputs:
- attention_out: bfloat16 [1024, 4096], P('dp', 'expert')
- layer_out: bfloat16 [1024, 4096], P('dp', 'expert')
Inputs may be any that keep to these rules, and one draw needn't show every extreme that they name: `node_of_position`: each block of 2304 positions begins with 256 positions of node 0, the root; the rest come in blocks of 128 positions, each holding one non-root node on a leading run of one or more positions and -1 after it; every non-root node holds one or more blocks. Node 0 is the root and its own parent; nodes 1 to 4 have parent 0; the other nodes are leaves with a parent among nodes 1 to 4. `leaf_ids`: every request sits at a leaf. `routes`: the two experts of a request differ; among the 64 requests of one index of dp no expert is named more than 32 times.
All inputs are finite; a program needn't handle non-finite values.
Results may differ from a plain program's by a relative error of at most 0.012.
Values may be sent and summed in bfloat16 or wider, within the bound.
No kernel may reach another device: no remote copies, remote signals or barrier semaphores. Data moves between devices by JAX's collectives and lax.ppermute only.
A program may use at most 128 MiB of HBM per device.

v0:
```python
import math

import jax
import jax.numpy as jnp
from jax import lax
from jax.sharding import PartitionSpec as P

Q_HEADS = 32
KV_HEADS = 8
HEAD_DIM = 128
EXPERTS = 8
CAP = 32


eps = 1e-05


def ancestor_nodes(leaf_nodes, parent):
    node_range = jnp.arange(parent.shape[0], dtype=jnp.int32)
    leaf_hot = (leaf_nodes[:, None] == node_range[None, :]).astype(jnp.int32)
    middle = jnp.sum(leaf_hot * parent[None, :], axis=1)
    middle_hot = (middle[:, None] == node_range[None, :]).astype(jnp.int32)
    upper = jnp.sum(middle_hot * parent[None, :], axis=1)
    return jnp.stack([leaf_nodes, middle, upper], axis=1)


def route_matrix(routes, weights, capacity, expert_count):
    row_total = routes.shape[0]
    flat_routes = routes.reshape(-1)
    expert_range = jnp.arange(expert_count, dtype=jnp.int32)
    expert_hot = (flat_routes[:, None] == expert_range[None, :]).astype(jnp.int32)
    slot_ranks = jnp.cumsum(expert_hot, axis=0) - expert_hot
    slot_ids = jnp.sum(slot_ranks * expert_hot, axis=1)
    target = slot_ids * expert_count + flat_routes
    column = jnp.arange(capacity * expert_count, dtype=jnp.int32)
    weighted = (target[:, None] == column[None, :]).astype(jnp.float32) * weights.reshape(-1)[
        :, None
    ].astype(jnp.float32)
    return jnp.sum(weighted.reshape(row_total, 2, capacity * expert_count), axis=1)


def body(
    residual,
    queries,
    cache_keys,
    cache_values,
    node_of_position,
    parent,
    leaf_ids,
    routes,
    gate_weights,
    norm_gain,
    w_gate,
    w_up,
    w_down,
):
    row_count = queries.shape[0]
    feature_count = queries.shape[1]
    dp_ways = lax.axis_size("dp")
    expert_ways = lax.axis_size("expert")
    group_size = Q_HEADS // KV_HEADS
    kv_local = cache_keys.shape[1] // HEAD_DIM
    head_local = kv_local * group_size
    local_experts = w_gate.shape[0]
    model_width = w_down.shape[2]
    capacity = CAP
    score_scale = 1.0 / math.sqrt(HEAD_DIM)
    all_queries, all_leaves, all_routes, all_weights = (
        lax.all_gather(queries, "dp", axis=0, tiled=True),
        lax.all_gather(leaf_ids, "dp", axis=0, tiled=True),
        lax.all_gather(routes, "dp", axis=0, tiled=True),
        lax.all_gather(gate_weights, "dp", axis=0, tiled=True),
    )
    total_rows = all_queries.shape[0]
    block_rows = min(total_rows, 512)
    block_count = total_rows // block_rows
    ancestors = ancestor_nodes(all_leaves, parent).reshape(block_count, block_rows, 3)
    query_blocks = all_queries.reshape(block_count, block_rows, kv_local, group_size, HEAD_DIM)
    key_heads = cache_keys.reshape(-1, kv_local, HEAD_DIM)
    value_heads = cache_values.reshape(-1, kv_local, HEAD_DIM)

    def attend(packed):
        query_block, ancestor_block = packed
        visible = jnp.any(node_of_position[None, :, None] == ancestor_block[:, None, :], axis=2)
        scores = (
            jnp.einsum("tkgd,pkd->tkgp", query_block, key_heads, preferred_element_type=jnp.float32)
            * score_scale
        )
        scores = jnp.where(visible[:, None, None, :], scores, -jnp.inf)
        local_max = jnp.max(scores, axis=3)
        exponent = jnp.exp(scores - local_max[..., None])
        local_total = jnp.sum(exponent, axis=3)
        local_out = jnp.einsum(
            "tkgp,pkd->tkgd",
            exponent.astype(jnp.bfloat16),
            value_heads,
            preferred_element_type=jnp.float32,
        )
        return (local_max, local_total, local_out)

    maxima, totals, outputs = lax.map(attend, (query_blocks, ancestors))
    maxima = maxima.reshape(total_rows, head_local)
    totals = totals.reshape(total_rows, head_local)
    outputs = outputs.reshape(total_rows, head_local * HEAD_DIM)
    got_out, got_max, got_total = (
        lax.all_to_all(outputs, "dp", split_axis=0, concat_axis=0, tiled=True),
        lax.all_to_all(maxima, "dp", split_axis=0, concat_axis=0, tiled=True),
        lax.all_to_all(totals, "dp", split_axis=0, concat_axis=0, tiled=True),
    )
    got_out = got_out.reshape(dp_ways, row_count, head_local, HEAD_DIM)
    got_max = got_max.reshape(dp_ways, row_count, head_local)
    got_total = got_total.reshape(dp_ways, row_count, head_local)
    global_max = jnp.max(got_max, axis=0)
    factor = jnp.exp(got_max - global_max[None])
    attention = (
        jnp.sum(factor[..., None] * got_out, axis=0)
        / jnp.sum(factor * got_total, axis=0)[..., None]
    )
    attention = attention.reshape(row_count, feature_count)
    attention_out = attention.astype(jnp.bfloat16)
    stream = (residual.astype(jnp.float32) + attention).astype(jnp.bfloat16)
    dispatch = route_matrix(routes, jnp.ones_like(gate_weights), capacity, EXPERTS).astype(
        jnp.bfloat16
    )
    slot_data = jnp.einsum(
        "rs,rf->sf", dispatch, stream, preferred_element_type=jnp.float32
    ).astype(jnp.bfloat16)
    slot_data = slot_data.reshape(capacity, EXPERTS, feature_count)
    gain_wide = norm_gain.astype(jnp.float32)
    gathered = lax.all_gather(slot_data, "dp", axis=0, tiled=True)
    rows_wide = lax.all_to_all(gathered, "expert", split_axis=1, concat_axis=2, tiled=True).astype(
        jnp.float32
    )
    inverse = lax.rsqrt(jnp.mean(rows_wide * rows_wide, axis=2, keepdims=True) + eps)
    normed = (rows_wide * inverse * gain_wide).astype(jnp.bfloat16)
    gate_val = jnp.einsum("rxd,xdf->rxf", normed, w_gate, preferred_element_type=jnp.float32)
    up_val = jnp.einsum("rxd,xdf->rxf", normed, w_up, preferred_element_type=jnp.float32)
    hidden = (jax.nn.silu(gate_val) * up_val).astype(jnp.bfloat16)
    expert_y = jnp.einsum("rxf,xfd->rxd", hidden, w_down, preferred_element_type=jnp.float32)
    expert_y = expert_y.reshape(dp_ways, capacity, local_experts, model_width)

    def block_matrix(block_routes, block_weights):
        return route_matrix(block_routes, block_weights, capacity, EXPERTS)

    row_mix = jax.vmap(block_matrix)(
        all_routes.reshape(dp_ways, row_count, 2), all_weights.reshape(dp_ways, row_count, 2)
    )
    row_mix = row_mix.reshape(dp_ways, row_count, capacity, EXPERTS)
    row_mix = lax.dynamic_slice_in_dim(
        row_mix, lax.axis_index("expert") * local_experts, local_experts, 3
    )
    row_mix = row_mix.reshape(dp_ways, row_count, capacity * local_experts)

    def one_pair(pair_index):
        row_block = pair_index // expert_ways
        feature_block = pair_index % expert_ways
        mixing = lax.dynamic_index_in_dim(row_mix, row_block, 0, keepdims=False)
        outs_block = lax.dynamic_index_in_dim(expert_y, row_block, 0, keepdims=False)
        columns = lax.dynamic_slice_in_dim(
            outs_block, feature_block * feature_count, feature_count, 2
        )
        return jnp.dot(
            mixing,
            columns.reshape(capacity * local_experts, feature_count),
            precision=lax.Precision.HIGHEST,
            preferred_element_type=jnp.float32,
        )

    pair_list = jnp.arange(
        row_count * lax.axis_size(("dp", "expert")) // row_count, dtype=jnp.int32
    )
    mixture = lax.psum_scatter(
        lax.map(one_pair, pair_list).reshape(
            row_count * lax.axis_size(("dp", "expert")), feature_count
        ),
        ("dp", "expert"),
        scatter_dimension=0,
        tiled=True,
    )
    layer_out = (stream.astype(jnp.float32) + mixture).astype(jnp.bfloat16)
    return (attention_out, layer_out)


def solution(mesh):
    in_specs = (
        P("dp", "expert"),
        P("dp", "expert"),
        P("dp", "expert"),
        P("dp", "expert"),
        P("dp"),
        P(),
        P("dp"),
        P("dp", None),
        P("dp", None),
        P(),
        P("expert", None, "dp"),
        P("expert", None, "dp"),
        P("expert", "dp", None),
    )
    out_specs = (P("dp", "expert"), P("dp", "expert"))
    return jax.shard_map(body, mesh=mesh, in_specs=in_specs, out_specs=out_specs, check_vma=False)
```

profile of v0, /device:TPU:1, one launch (start us, length us, event | category | flops | bytes accessed | tf_op | source)
XLA Modules:
  0.0 1619.1 jit_solution(6109415715800916081)
XLA Ops:
  10.7 13.8 all-reduce
  26.1 28.5 %all-gather.5.cloned.1.call-done = bf16[1024,512]{1,0:T(8,128)(2,1)} async-done(((bf16[64,512]{1,0:T(8,128)(2,1)}), bf16[1024,512]{1,0:T(8,128)(2,1)}) %all-gather.5.cloned.1.call-update) | async-done | bytes 1048592 | tf_op jit(solution)/shard_map/all_gather | solution.py:69
  55.9 36.9 %while.27 = (s32[]{:T(128)}, f32[2,512,1,4]{1,0,3,2:T(2,128)S(1)}, f32[2,512,1,4]{1,0,3,2:T(2,128)S(1)}, f32[2,512,1,4,128]{4,3,1,0,2:T(4,128)S(1)}, s32[2304]{0...) while((s32[]{:T(128)}, f32[2,512,1,4]{1,0,3,2:T(2,128)S(1)}, ...), condition=%wide.region_6.7_spmd, body=%wide.region_2.6_spmd.sunk | while | flops 2473717760 | bytes 69725344 | solution.py:101
  58.6 4.9 fusion.67
  63.6 5.0 fusion.69
  69.3 4.9 fusion.68
  77.1 4.9 fusion.67
  82.0 5.0 fusion.69
  87.8 4.9 fusion.68
  93.6 5.0 all-to-all-start
  99.4 5.6 all-to-all-done
  110.5 4.5 all-to-all-done.2
  126.3 17.9 %all-to-all-done.1 = f32[16,64,512]{2,1,0:T(8,128)} async-done(((f32[16,64,512]{2,1,0:T(8,128)}), f32[16,64,512]{2,1,0:T(8,128)}, u32[]{:S(2)}, u32[]{:S(2)}) %all-to-all-start.1) | async-done | bytes 2097184 | tf_op jit(solution)/shard_map/all_to_all | solution.py:106
  147.9 55.5 %all-gather.7.cloned.1.call-done = bf16[512,8,512]{2,1,0:T(8,128)(2,1)} async-done(((bf16[32,8,512]{2,1,0:T(8,128)(2,1)}), bf16[512,8,512]{2,1,0:T(8,128)(2,1)}) %all-gather.7.cloned.1.call-update) | async-done | bytes 4194320 | tf_op jit(solution)/shard_map/all_gather | solution.py:130
  203.4 5.6 copy.124
  209.0 5.1 all-to-all-start.3
  214.1 19.0 %all-gather = s32[16,64,2]{1,2,0:T(2,128)S(1)} all-gather(s32[1,64,2]{1,2,0:T(2,128)S(1)} %bitcast.222), channel_id=1, replica_groups=mesh['dp'=16,'expert'=8] {'dp'}, dimensions={0}, use_global_device_ids=true | all-gather | bytes 8704 | tf_op jit(solution)/shard_map/all_gather | solution.py:71
  236.1 16.0 all-gather.1
  253.8 9.2 all-to-all-done.3
  263.0 6.5 copy.125
  272.6 9.0 fusion.25
  281.6 18.7 %fusion.21 = f32[512,4096]{1,0:T(8,128)} fusion(bf16[1,896,4096]{2,1,0:T(8,128)(2,1)} %param.29, bf16[1,4096,896]{2,1,0:T(8,128)(2,1)} %param.28, f32[512,896]{1,0:T(8,128)S(1)} %fusion.25, f32[4096]{0:T(1024)S(1)} %convert_element_type.126, f32[512]{0:T(512)S(1)} %add_rsqrt_fusion, bf16[512,1,1,1,1,1,4096]{0,6,5,4,3,2,1:T(8,128)(2,1)} %bitcast.207), kind=kOutput, calls=%fused_computation.28 | convolution fusion | flops 7527333888 | bytes 29116416 | tf_op jit(solution)/shard_map/rxf,xfd->rxd/dot_general | solution.py:139
  300.3 652.6 %while.28 = (s32[]{:T(128)}, f32[128,64,512]{2,1,0:T(8,128)}, s32[128]{0:T(128)S(1)}, f32[16,64,32]{1,2,0:T(8,128)S(1)}, f32[16,32,1,4096]{3,1,0,2:T(8,128)}, /*...) while((s32[]{:T(128)}, f32[128,64,512]{2,1,0:T(8,128)}, ...), condition=%wide.region_18.19_spmd, body=%wide.region_17.18_spmd.sunk | while | flops 12582942 | bytes 213976 | solution.py:173
  952.9 658.1 %reduce-scatter.2.cloned.1.call-done = f32[64,512]{1,0:T(8,128)} async-done(((f32[8192,512]{1,0:T(8,128)}), f32[64,512]{1,0:T(8,128)}) %reduce-scatter.2.cloned.1.call-update) | async-done | bytes 131088 | tf_op jit(solution)/shard_map/reduce_scatter | solution.py:172
  (349 shorter events, 360.8 us)
Async XLA Ops:
  7.2 47.4 %all-gather.5.cloned.1.call-start = ((), (), s32[]{:S(2)}) async-start(), calls=%async_computation.5 | async-start | bytes 1114112 | tf_op jit(solution)/shard_map/all_gather | solution.py:69
  58.6 4.9 copy-start.4
  77.1 4.9 copy-start.4
  92.8 26.8 %copy-start.1 = (s32[64,2]{0,1:T(2,128)S(1)}, s32[64,2]{0,1:T(2,128)}, u32[]{:S(2)}) copy-start(s32[64,2]{0,1:T(2,128)} %param.24) | copy-start | bytes 1540
  93.6 11.4 all-to-all-start
  105.1 9.9 all-to-all-start.2
  115.0 29.1 %all-to-all-start.1 = ((f32[16,64,512]{2,1,0:T(8,128)}), f32[16,64,512]{2,1,0:T(8,128)}, u32[]{:S(2)}, u32[]{:S(2)}) async-start(f32[16,64,512]{2,1,0:T(8,128)} %all_to_all.27), calls=%async_computation.1 | async-start | bytes 4194304 | tf_op jit(solution)/shard_map/all_to_all | solution.py:106
  119.4 27.5 %copy-start = (bf16[64,512]{1,0:T(8,128)(2,1)S(1)}, bf16[64,512]{1,0:T(8,128)(2,1)}, u32[]{:S(2)}) copy-start(bf16[64,512]{1,0:T(8,128)(2,1)} %param.17) | copy-start | bytes 196612
  119.4 84.0 %all-gather.7.cloned.1.call-start = ((), (), s32[]{:S(2)}) async-start(), calls=%async_computation.6 | async-start | bytes 4456448 | tf_op jit(solution)/shard_map/all_gather | solution.py:130
  147.9 66.2 %copy-start.2 = (bf16[4096]{0:T(1024)(128)(2,1)S(1)}, bf16[4096]{0:T(1024)(128)(2,1)}, u32[]{:S(2)}) copy-start(bf16[4096]{0:T(1024)(128)(2,1)} %param.26) | copy-start | bytes 24580
  147.9 88.2 %copy-start.3 = (bf16[64,2]{0,1:T(2,128)(2,1)S(1)}, bf16[64,2]{0,1:T(2,128)(2,1)}, u32[]{:S(2)}) copy-start(bf16[64,2]{0,1:T(2,128)(2,1)} %param.25) | copy-start | bytes 772
  209.0 54.0 %all-to-all-start.3 = ((bf16[512,8,512]{2,0,1:T(8,128)(2,1)}), bf16[512,8,512]{2,0,1:T(8,128)(2,1)}, u32[]{:S(2)}, u32[]{:S(2)}) async-start(bf16[512,8,512]{2,0,1:T(8,128)(2,1)} %copy.124), calls=%async_computation.3 | async-start | bytes 8388608 | tf_op jit(solution)/shard_map/all_to_all | solution.py:131
  214.1 1396.9 %reduce-scatter.2.cloned.1.call-start = ((), (), s32[]{:S(2)}) async-start(), calls=%async_computation.7 | async-start | bytes 16908288 | tf_op jit(solution)/shard_map/reduce_scatter | solution.py:172
Sparse Core Ops, SparseCore 0:
  10.1 44.3 all-gather.4
  148.0 55.3 all-gather.6
  953.0 657.9 reduce-scatter.1
where the time goes:
time: 1640 us; the launch traced here: 1620 us
  waiting for transfers between devices  780 us (48%)
  loops' own time  336 us (20%)
  matrix products  291 us (18%)
  local copies, waits for them, and re-layouts  101 us (6%)
  blocking collectives  48.9 us (3%)
  other arithmetic  29.3 us (2%)
  starting transfers between devices  18.3 us (1%)
    reduce_scatter x1, waiting for transfers between devices, body(): lax.psum_scatter(lax.map(one_pair, pair_list).reshape(row_count * lax.axi...  658 us
    another operation x1, loops' own time, body(): lax.map(one_pair, pair_list)  336 us
    dot_general x128, matrix products, one_pair(): jnp.dot(mixing, columns.reshape(capacity * local_experts, feature_count),...  242 us
    dynamic_slice x128, local copies, waits for them, and re-layouts, body(): lax.map(one_pair, pair_list)  74.5 us
    all_gather x1, waiting for transfers between devices, body(): gathered = lax.all_gather(slot_data, 'dp', axis=0, tiled=True)  55.5 us
  transfers between devices with their start and end apart: 7, of which 7 were waited for; matrix products, arithmetic and copies ran while one was open for 1% of the time, Pallas kernels for 0%

commit v1 on v0

v1 whole, which is shorter than its diff:
```python
import functools
import math

import jax
import jax.numpy as jnp
from jax import lax
from jax.experimental import pallas as pl
from jax.experimental.pallas import tpu as pltpu
from jax.sharding import PartitionSpec as P

HEAD_DIM = 128
EXPERTS = 8
CAP = 32
EPS = 1e-05
HIDE = -1e30
SCALE2 = math.log2(math.e) / math.sqrt(HEAD_DIM)
BF = jnp.bfloat16
F32 = jnp.float32


def ring_pairs(axis, shift):
    pairs = []
    for a in range(4):
        for b in range(4):
            if axis == 0:
                pairs.append((4 * a + b, 4 * ((a + shift) % 4) + b))
            else:
                pairs.append((4 * a + b, 4 * a + (b + shift) % 4))
    return pairs


def shift_dp(value, axis, shift):
    return lax.ppermute(value, "dp", ring_pairs(axis, shift))


def attend_kernel(order_ref, q0, q1, q2, q3, kt_ref, v_ref, out_ref, q_scr):
    step = pl.program_id(0)
    for k, ref in enumerate((q0, q1, q2, q3)):

        @pl.when(step // 4 == k)
        def _(ref=ref):
            q_scr[...] = ref[step % 4]

    bias = q_scr[:, 512:640]
    rows = [
        jnp.concatenate([q_scr[:, 128 * h : 128 * h + 128], bias], axis=1) for h in range(4)
    ]
    q_wide = jnp.concatenate(rows, axis=0)
    scores = jnp.dot(q_wide, kt_ref[...], preferred_element_type=F32)
    top = jnp.max(scores, axis=1, keepdims=True) * SCALE2
    top = top.astype(BF).astype(F32)
    probs = jnp.exp2(scores * SCALE2 - top).astype(BF)
    both = jnp.dot(probs, v_ref[...], preferred_element_type=F32)
    lane = lax.broadcasted_iota(jnp.int32, (64, 128), 1)
    stats = jnp.zeros((64, 128), F32)
    for h in range(4):
        part = both[64 * h : 64 * h + 64]
        out_ref[0, :, 128 * h : 128 * h + 128] = part[:, :128].astype(BF)
        total = part[:, 128:256]
        high = total.astype(BF).astype(F32)
        low = total - high
        stats = jnp.where(lane == h, top[64 * h : 64 * h + 64], stats)
        stats = jnp.where(lane == 4 + h, high, stats)
        stats = jnp.where(lane == 8 + h, low, stats)
    out_ref[0, :, 512:640] = stats.astype(BF)


def attend(order, blocks, kt_wide, v_wide):
    whole = lambda shape: pl.BlockSpec(shape, lambda g, order: tuple(0 for _ in shape))
    return pl.pallas_call(
        attend_kernel,
        out_shape=jax.ShapeDtypeStruct((16, 64, 640), BF),
        grid_spec=pltpu.PrefetchScalarGridSpec(
            num_scalar_prefetch=1,
            grid=(16,),
            in_specs=[whole((4, 64, 640)) for _ in range(4)]
            + [whole(kt_wide.shape), whole(v_wide.shape)],
            out_specs=pl.BlockSpec((1, 64, 640), lambda g, order: (order[g], 0, 0)),
            scratch_shapes=[pltpu.VMEM((64, 640), BF)],
        ),
        compiler_params=pltpu.CompilerParams(vmem_limit_bytes=40 << 20),
        name="attend",
    )(order, *blocks, kt_wide, v_wide)


def combine_kernel(got_ref, res_ref, disp_ref, att_ref, stream_ref, slot_ref):
    stats = got_ref[:, :, 512:640].astype(F32)
    top = jnp.max(stats, axis=0)
    factor = jnp.exp2(stats - top[None])
    for h in range(4):
        weight = factor[:, :, h : h + 1]
        total = stats[:, :, 4 + h : 5 + h] + stats[:, :, 8 + h : 9 + h]
        part = got_ref[:, :, 128 * h : 128 * h + 128].astype(F32)
        upper = jnp.sum(part * weight, axis=0)
        lower = jnp.sum(total * weight, axis=0)
        att = upper / lower
        cols = slice(128 * h, 128 * h + 128)
        att_ref[:, cols] = att.astype(BF)
        stream_ref[:, cols] = (res_ref[:, cols].astype(F32) + att).astype(BF)
    slot_ref[...] = jnp.dot(
        disp_ref[...], stream_ref[...], preferred_element_type=F32
    ).astype(BF)


def combine(got, residual, disp):
    return pl.pallas_call(
        combine_kernel,
        out_shape=(
            jax.ShapeDtypeStruct((64, 512), BF),
            jax.ShapeDtypeStruct((64, 512), BF),
            jax.ShapeDtypeStruct((256, 512), BF),
        ),
        name="combine",
    )(got, residual, disp)


def norm_kernel(x_ref, gain_ref, out_ref):
    total = jnp.zeros((32, 512), F32)
    for f in range(8):
        wide = x_ref[f].astype(F32)
        total = total + wide * wide
    mean = jnp.sum(total, axis=1, keepdims=True) * (1.0 / 4096.0)
    inverse = lax.rsqrt(mean + EPS)
    for f in range(8):
        cols = slice(512 * f, 512 * f + 512)
        out_ref[:, cols] = (x_ref[f].astype(F32) * inverse * gain_ref[:, cols].astype(F32)).astype(BF)


def norm(x, gain):
    return pl.pallas_call(
        norm_kernel,
        out_shape=jax.ShapeDtypeStruct((32, 4096), BF),
        name="norm",
    )(x, gain)


def moe_kernel(x_ref, wg_ref, wu_ref, wd_ref, out_ref, gate_acc, up_acc, hid):
    step = pl.program_id(0)

    @pl.when(step < 8)
    def _():
        x = x_ref[...]
        gate = jnp.dot(x, wg_ref[0], preferred_element_type=F32)
        up = jnp.dot(x, wu_ref[0], preferred_element_type=F32)

        @pl.when(step == 0)
        def _():
            gate_acc[...] = gate
            up_acc[...] = up

        @pl.when(step > 0)
        def _():
            gate_acc[...] += gate
            up_acc[...] += up

        @pl.when(step == 7)
        def _():
            g = gate_acc[...]
            hid[...] = (g / (1.0 + jnp.exp(-g)) * up_acc[...]).astype(BF)

    @pl.when(step >= 8)
    def _():
        out_ref[...] = jnp.dot(hid[...], wd_ref[0], preferred_element_type=F32).astype(BF)


def moe(x, w_gate, w_up, w_down):
    return pl.pallas_call(
        moe_kernel,
        out_shape=jax.ShapeDtypeStruct((512, 4096), BF),
        grid=(16,),
        in_specs=[
            pl.BlockSpec((512, 512), lambda i: (0, jnp.minimum(i, 7))),
            pl.BlockSpec((1, 512, 896), lambda i: (0, jnp.minimum(i, 7), 0)),
            pl.BlockSpec((1, 512, 896), lambda i: (0, jnp.minimum(i, 7), 0)),
            pl.BlockSpec((1, 896, 512), lambda i: (0, 0, jnp.maximum(i - 8, 0))),
        ],
        out_specs=pl.BlockSpec((512, 512), lambda i: (0, jnp.maximum(i - 8, 0))),
        scratch_shapes=[
            pltpu.VMEM((512, 896), F32),
            pltpu.VMEM((512, 896), F32),
            pltpu.VMEM((512, 896), BF),
        ],
        compiler_params=pltpu.CompilerParams(vmem_limit_bytes=40 << 20),
        name="moe",
    )(x, w_gate, w_up, w_down)


def add_kernel(x_ref, out_ref):
    total = jnp.zeros((32, 512), F32)
    for j in range(16):
        total = total + x_ref[j].astype(F32)
    out_ref[0] = total.astype(BF)


def add_up(x):
    return pl.pallas_call(
        add_kernel,
        out_shape=jax.ShapeDtypeStruct((8, 32, 512), BF),
        grid=(8,),
        in_specs=[pl.BlockSpec((16, 32, 512), lambda f: (0, 0, f))],
        out_specs=pl.BlockSpec((1, 32, 512), lambda f: (f, 0, 0)),
        name="add_up",
    )(x)


def finish_kernel(mix_ref, y_ref, stream_ref, out_ref):
    mixture = jnp.dot(mix_ref[...], y_ref[...], preferred_element_type=F32)
    out_ref[...] = (stream_ref[...].astype(F32) + mixture).astype(BF)


def finish(mix, y, stream):
    return pl.pallas_call(
        finish_kernel, out_shape=jax.ShapeDtypeStruct((64, 512), BF), name="finish"
    )(mix, y, stream)


def body(
    residual,
    queries,
    cache_keys,
    cache_values,
    node_of_position,
    parent,
    leaf_ids,
    routes,
    gate_weights,
    norm_gain,
    w_gate,
    w_up,
    w_down,
):
    rows = queries.shape[0]
    node_count = parent.shape[0]
    lane = jnp.arange(128, dtype=jnp.int32)
    leaf_hot = leaf_ids[:, None] == jnp.arange(node_count, dtype=jnp.int32)[None, :]
    middle = jnp.sum(jnp.where(leaf_hot, parent[None, :], 0), axis=1)
    middle_hot = middle[:, None] == jnp.arange(node_count, dtype=jnp.int32)[None, :]
    upper = jnp.sum(jnp.where(middle_hot, parent[None, :], 0), axis=1)
    seen = (
        (lane[None, :] == leaf_ids[:, None])
        | (lane[None, :] == middle[:, None])
        | (lane[None, :] == upper[:, None])
    )
    bias = jnp.where(seen, 0.0, HIDE).astype(BF)
    q_own = jnp.concatenate([queries, bias], axis=1)[None]
    stage = jnp.concatenate([q_own] + [shift_dp(q_own, 1, s) for s in (1, 2, 3)], axis=0)
    blocks = [stage] + [shift_dp(stage, 0, s) for s in (1, 2, 3)]

    kt_hot = (
        jnp.where(node_of_position < 0, 127, node_of_position)[None, :] == lane[:, None]
    ).astype(BF)
    kt_wide = jnp.concatenate([cache_keys.T, kt_hot], axis=0)
    v_wide = jnp.concatenate([cache_values, jnp.ones_like(cache_values)], axis=1)

    expert_range = jnp.arange(EXPERTS, dtype=jnp.int32)
    hot = routes[:, :, None] == expert_range[None, None, :]
    weight = jnp.sum(jnp.where(hot, gate_weights.astype(F32)[:, :, None], 0.0), axis=1)
    named = jnp.any(hot, axis=1)
    row = jnp.arange(rows, dtype=jnp.int32)
    before = (row[None, :] < row[:, None]).astype(BF)
    rank = jnp.dot(before, named.astype(BF), preferred_element_type=F32).astype(jnp.int32)
    slot = jnp.arange(CAP, dtype=jnp.int32)
    place = named.T[:, None, :] & (rank.T[:, None, :] == slot[None, :, None])
    disp = place.reshape(EXPERTS * CAP, rows).astype(BF)
    place_t = named[:, :, None] & (rank[:, :, None] == slot[None, None, :])
    mix = jnp.where(place_t, weight[:, :, None], 0.0).reshape(rows, EXPERTS * CAP).astype(BF)

    me = lax.axis_index("dp")
    rel = jnp.arange(16, dtype=jnp.int32)
    order = ((me // 4 - rel // 4) % 4) * 4 + (me % 4 - rel % 4) % 4
    partial = attend(order, blocks, kt_wide, v_wide)
    got = lax.all_to_all(partial, "dp", split_axis=0, concat_axis=0, tiled=True)
    attention_out, stream, slots = combine(got, residual, disp)

    mine = lax.all_to_all(slots.reshape(8, 32, 512), "expert", split_axis=0, concat_axis=0, tiled=True)
    normed = norm(mine, norm_gain[None, :])
    gathered = lax.all_gather(normed, "dp", axis=0, tiled=True)
    expert_y = moe(gathered, w_gate, w_up, w_down)
    spread = lax.all_to_all(
        expert_y.reshape(16, 32, 4096), "dp", split_axis=0, concat_axis=0, tiled=True
    )
    summed = add_up(spread)
    back = lax.all_to_all(summed, "expert", split_axis=0, concat_axis=0, tiled=True)
    layer_out = finish(mix, back.reshape(256, 512), stream)
    return (attention_out, layer_out)


def solution(mesh):
    in_specs = (
        P("dp", "expert"),
        P("dp", "expert"),
        P("dp", "expert"),
        P("dp", "expert"),
        P("dp"),
        P(),
        P("dp"),
        P("dp", None),
        P("dp", None),
        P(),
        P("expert", None, "dp"),
        P("expert", None, "dp"),
        P("expert", "dp", None),
    )
    out_specs = (P("dp", "expert"), P("dp", "expert"))
    return jax.shard_map(body, mesh=mesh, in_specs=in_specs, out_specs=out_specs, check_vma=False)
```

time: 1640 us -> 283 us (0.17); the launches traced: 1620 us -> 279 us
  waiting for transfers between devices: 780 us -> 149 us
  loops' own time: 336 us -> 0 us
  matrix products: 291 us -> 0.13 us
  local copies, waits for them, and re-layouts: 101 us -> 9.04 us
  Pallas kernels: 0 us -> 62.3 us
  blocking collectives: 48.9 us -> 0 us
  other arithmetic: 29.3 us -> 5.51 us
  starting transfers between devices: 18.3 us -> 38.7 us
    reduce_scatter x1 -> x0, waiting for transfers between devices: 658 us -> none  [body(): lax.psum_scatter(lax.map(one_pair, pair_list).reshape(row_count * lax.axi...]
    another operation x2 -> x0, loops' own time: 336 us -> none  [the longest x1 336 us: body(): lax.map(one_pair, pair_list)]
    dot_general x135 -> x1, matrix products: 291 us -> 0.13 us  [body(): jnp.dot(before, named.astype(BF), preferred_element_type=F32)]
    dynamic_slice x131 -> x0, local copies, waits for them, and re-layouts: 75.1 us -> none  [the longest x128 74.5 us: body(): lax.map(one_pair, pair_list)]
    pallas_call x0 -> x6, Pallas kernels: none -> 62.3 us  [the longest x1 26.3 us: attend(): pl.pallas_call(attend_kernel, out_shape=jax.ShapeDtypeStruct((16, 64, 640...]
    all_to_all x4, waiting for transfers between devices: 37.2 us -> 89.7 us  [the longest x1 61.5 us: body(): lax.all_to_all(expert_y.reshape(16, 32, 4096), 'dp', split_axis=0, concat...]
    all_gather x2 -> x1, waiting for transfers between devices: 84 us -> 47.5 us  [body(): gathered = lax.all_gather(normed, 'dp', axis=0, tiled=True)]
    all_gather x2 -> x0, blocking collectives: 35 us -> none  [the longest x1 19 us: body(): lax.all_gather(routes, 'dp', axis=0, tiled=True)]
  transfers between devices with their start and end apart: 7 -> 11, of which waited for: 7 -> 8; matrix products, arithmetic and copies ran while one was open for 1% -> 2% of each run, Pallas kernels for 0% -> 0%
where the time goes in v1:
time: 283 us; the launch traced here: 279 us
  waiting for transfers between devices  149 us (53%)
  Pallas kernels  62.3 us (22%)
  starting transfers between devices  38.7 us (14%)
  between operations  14.2 us (5%)
  local copies, waits for them, and re-layouts  9.04 us (3%)
  other arithmetic  5.51 us (2%)
    all_to_all x1, waiting for transfers between devices, body(): lax.all_to_all(expert_y.reshape(16, 32, 4096), 'dp', split_axis=0, concat...  61.5 us
    all_gather x1, waiting for transfers between devices, body(): gathered = lax.all_gather(normed, 'dp', axis=0, tiled=True)  47.5 us
    pallas_call x1, Pallas kernels, attend(): pl.pallas_call(attend_kernel, out_shape=jax.ShapeDtypeStruct((16, 64, 640...  26.3 us
    pallas_call x1, Pallas kernels, moe(): pl.pallas_call(moe_kernel, out_shape=jax.ShapeDtypeStruct((512, 4096), BF...  23.4 us
    all_to_all x1, waiting for transfers between devices, body(): got = lax.all_to_all(partial, 'dp', split_axis=0, concat_axis=0, tiled=True)  16.8 us
    ppermute x6, waiting for transfers between devices, shift_dp(): return lax.ppermute(value, 'dp', ring_pairs(axis, shift))  12.1 us
    ppermute x6, starting transfers between devices, shift_dp(): return lax.ppermute(value, 'dp', ring_pairs(axis, shift))  11.1 us
    all_to_all x1, starting transfers between devices, body(): lax.all_to_all(slots.reshape(8, 32, 512), 'expert', split_axis=0, concat_...  9.26 us
  transfers between devices with their start and end apart: 11, of which 8 were waited for; matrix products, arithmetic and copies ran while one was open for 2% of the time, Pallas kernels for 0%

profile of v1, /device:TPU:1, one launch (start us, length us, event | category | flops | bytes accessed | tf_op | source)
XLA Modules:
  0.0 279.2 jit_solution(4498249175986193638)
XLA Ops:
  10.3 2.1 collective-permute-start
  12.5 2.6 collective-permute-start.1
  17.0 1.3 copy.26
  18.5 1.6 collective-permute-start.3
  20.2 2.5 collective-permute-start.4
  23.9 3.2 %collective-permute-done.3.q1 = bf16[4,64,640]{2,1,0:T(8,128)(2,1)S(1)} collective-permute-done((bf16[4,64,640]{2,1,0:T(8,128)(2,1)S(1)}, bf16[4,64,640]{2,1,0:T(8,128)(2,1)S(1)}, u32[]{:S(2)}, u32[]{:S(2)}) %collective-permute-start.3) | collective-permute-done | bytes 327712 | tf_op jit(solution)/shard_map/ppermute | solution.py:33
  27.1 8.4 %collective-permute-done.4.q2 = bf16[4,64,640]{2,1,0:T(8,128)(2,1)S(1)} collective-permute-done((bf16[4,64,640]{2,1,0:T(8,128)(2,1)S(1)}, bf16[4,64,640]{2,1,0:T(8,128)(2,1)S(1)}, u32[]{:S(2)}, u32[]{:S(2)}) %collective-permute-start.4) | collective-permute-done | bytes 327712 | tf_op jit(solution)/shard_map/ppermute | solution.py:33
  35.9 26.3 %attend.1 = bf16[16,64,640]{2,1,0:T(8,128)(2,1)} custom-call(s32[16]{0:T(128)S(1)} %fusion.7.order_ref, bf16[4,64,640]{2,1,0:T(8,128)(2,1)S(1)} %pad_maximum_fusion.1.q0, bf16[4,64,640]{2,1,0:T(8,128)(2,1)S(1)} %collective-permute-done.3.q1, bf16[4,64,640]{2,1,0:T(8,128)(2,1)S(1)} %collective-permute-done.4.q2, ...), custom_call_target="tpu_custom_call" | custom-call | tf_op jit(solution)/shard_map/attend/pallas_call | solution.py:70
  62.2 6.6 %all-to-all-start = ((bf16[16,64,640]{2,1,0:T(8,128)(2,1)}), bf16[16,64,640]{2,1,0:T(8,128)(2,1)S(1)}, u32[]{:S(2)}, u32[]{:S(2)}) async-start(bf16[16,64,640]{2,1,0:T(8,128)(2,1)} %attend.1), calls=%async_computation | async-start | bytes 2621440 | tf_op jit(solution)/shard_map/all_to_all | solution.py:272
  69.8 16.8 %all-to-all-done.got_ref = bf16[16,64,640]{2,1,0:T(8,128)(2,1)S(1)} async-done(((bf16[16,64,640]{2,1,0:T(8,128)(2,1)}), bf16[16,64,640]{2,1,0:T(8,128)(2,1)S(1)}, u32[]{:S(2)}, u32[]{:S(2)}) %all-to-all-start) | async-done | bytes 1310752 | tf_op jit(solution)/shard_map/all_to_all | solution.py:272
  87.7 3.2 %combine.1 = (bf16[64,512]{1,0:T(8,128)(2,1)}, bf16[64,512]{1,0:T(8,128)(2,1)}, bf16[256,512]{1,0:T(8,128)(2,1)}) custom-call(bf16[16,64,640]{2,1,0:T(8,128)(2,1)} %copy-done.2, bf16[64,512]{1,0:T(8,128)(2,1)} %res_ref.1, bf16[256,64]{1,0:T(8,128)(2,1)} %fusion.2.disp_ref), custom_call_target="tpu_custom_call" | custom-call | tf_op jit(solution)/shard_map/combine/pallas_call | solution.py:106
  90.9 9.3 %all-to-all-start.1 = ((bf16[8,32,512]{2,1,0:T(8,128)(2,1)}), bf16[8,32,512]{2,1,0:T(8,128)(2,1)S(1)}, u32[]{:S(2)}, u32[]{:S(2)}) async-start(bf16[8,32,512]{2,1,0:T(8,128)(2,1)} %bitcast.24), calls=%async_computation.1 | async-start | bytes 524288 | tf_op jit(solution)/shard_map/all_to_all | solution.py:275
  100.8 5.9 %all-to-all-done.1.x_ref = bf16[8,32,512]{2,1,0:T(8,128)(2,1)S(1)} async-done(((bf16[8,32,512]{2,1,0:T(8,128)(2,1)}), bf16[8,32,512]{2,1,0:T(8,128)(2,1)S(1)}, u32[]{:S(2)}, u32[]{:S(2)}) %all-to-all-start.1) | async-done | bytes 262176 | tf_op jit(solution)/shard_map/all_to_all | solution.py:275
  107.4 1.8 norm.1
  109.2 47.5 %all-gather.2.cloned.1.call-done.x_ref = bf16[512,4096]{1,0:T(8,128)(2,1)} async-done(((bf16[32,4096]{1,0:T(8,128)(2,1)}), bf16[512,4096]{1,0:T(8,128)(2,1)}) %all-gather.2.cloned.1.call-update) | async-done | bytes 4194320 | tf_op jit(solution)/shard_map/all_gather | solution.py:277
  156.7 2.2 copy-done.1
  158.9 23.4 %moe.1 = bf16[512,4096]{1,0:T(8,128)(2,1)S(1)} custom-call(bf16[512,4096]{1,0:T(8,128)(2,1)S(1)} %copy-done.1, bf16[1,4096,896]{2,1,0:T(8,128)(2,1)} %wg_ref.1, bf16[1,4096,896]{2,1,0:T(8,128)(2,1)} %wu_ref.1, bf16[1,896,4096]{2,1,0:T(8,128)(2,1)} %wd_ref.1), custom_call_target="tpu_custom_call" | custom-call | tf_op jit(solution)/shard_map/moe/pallas_call | solution.py:167
  182.4 2.0 copy-done
  184.3 5.2 %all-to-all-start.2 = ((bf16[16,32,4096]{2,1,0:T(8,128)(2,1)}), bf16[16,32,4096]{2,1,0:T(8,128)(2,1)}, u32[]{:S(2)}, u32[]{:S(2)}) async-start(bf16[16,32,4096]{2,1,0:T(8,128)(2,1)} %bitcast.20), calls=%async_computation.2 | async-start | bytes 8388608 | tf_op jit(solution)/shard_map/all_to_all | solution.py:279
  189.5 61.5 %all-to-all-done.2.x_ref = bf16[16,32,4096]{2,1,0:T(8,128)(2,1)} async-done(((bf16[16,32,4096]{2,1,0:T(8,128)(2,1)}), bf16[16,32,4096]{2,1,0:T(8,128)(2,1)}, u32[]{:S(2)}, u32[]{:S(2)}) %all-to-all-start.2) | async-done | bytes 4194336 | tf_op jit(solution)/shard_map/all_to_all | solution.py:279
  251.0 5.8 %add_up.1 = bf16[8,32,512]{2,1,0:T(8,128)(2,1)} custom-call(bf16[16,32,4096]{2,1,0:T(8,128)(2,1)} %all-to-all-done.2.x_ref), custom_call_target="tpu_custom_call" | custom-call | tf_op jit(solution)/shard_map/add_up/pallas_call | solution.py:196
  256.8 6.6 %all-to-all-start.3 = ((bf16[8,32,512]{2,1,0:T(8,128)(2,1)}), bf16[8,32,512]{2,1,0:T(8,128)(2,1)S(1)}, u32[]{:S(2)}, u32[]{:S(2)}) async-start(bf16[8,32,512]{2,1,0:T(8,128)(2,1)} %add_up.1), calls=%async_computation.3 | async-start | bytes 524288 | tf_op jit(solution)/shard_map/all_to_all | solution.py:283
  264.4 5.5 %all-to-all-done.3 = bf16[8,32,512]{2,1,0:T(8,128)(2,1)S(1)} async-done(((bf16[8,32,512]{2,1,0:T(8,128)(2,1)}), bf16[8,32,512]{2,1,0:T(8,128)(2,1)S(1)}, u32[]{:S(2)}, u32[]{:S(2)}) %all-to-all-start.3) | async-done | bytes 262176 | tf_op jit(solution)/shard_map/all_to_all | solution.py:283
  270.6 1.7 finish.1
  (49 shorter events, 12.0 us)
Async XLA Ops:
  7.2 11.1 %copy-start.5 = (bf16[2304,128]{1,0:T(8,128)(2,1)S(1)}, bf16[2304,128]{1,0:T(8,128)(2,1)}, u32[]{:S(2)}) copy-start(bf16[2304,128]{1,0:T(8,128)(2,1)} %param.16) | copy-start | bytes 1769476
  10.3 8.1 %collective-permute-start = (bf16[1,64,640]{2,1,0:T(8,128)(2,1)S(1)}, bf16[1,64,640]{2,1,0:T(8,128)(2,1)S(1)}, u32[]{:S(2)}, u32[]{:S(2)}) collective-permute-start(bf16[1,64,640]{2,1,0:T(8,128)(2,1)S(1)} %maximum_bitcast_fusion), channel_id=1, source_target_pairs={{0,8},{8,16},{16,24},{24,0},{32,40},{40,48},{48,56},{56,32},{64,72... | collective-permute-start | bytes 245768 | tf_op jit(solution)/shard_map/ppermute | solution.py:33
  12.5 6.0 %collective-permute-start.1 = (bf16[1,64,640]{2,1,0:T(8,128)(2,1)S(1)}, bf16[1,64,640]{2,1,0:T(8,128)(2,1)S(1)}, u32[]{:S(2)}, u32[]{:S(2)}) collective-permute-start(bf16[1,64,640]{2,1,0:T(8,128)(2,1)S(1)} %maximum_bitcast_fusion), channel_id=1, source_target_pairs={{0,16},{8,24},{16,0},{24,8},{32,48},{40,56},{48,32},{56,40},{64,80... | collective-permute-start | bytes 245768 | tf_op jit(solution)/shard_map/ppermute | solution.py:33
  15.1 3.4 %collective-permute-start.2 = (bf16[1,64,640]{2,1,0:T(8,128)(2,1)S(1)}, bf16[1,64,640]{2,1,0:T(8,128)(2,1)S(1)}, u32[]{:S(2)}, u32[]{:S(2)}) collective-permute-start(bf16[1,64,640]{2,1,0:T(8,128)(2,1)S(1)} %maximum_bitcast_fusion), channel_id=1, source_target_pairs={{0,24},{8,0},{16,8},{24,16},{32,56},{40,32},{48,40},{56,48},{64,88... | collective-permute-start | bytes 245768 | tf_op jit(solution)/shard_map/ppermute | solution.py:33
  18.5 8.5 %collective-permute-start.3 = (bf16[4,64,640]{2,1,0:T(8,128)(2,1)S(1)}, bf16[4,64,640]{2,1,0:T(8,128)(2,1)S(1)}, u32[]{:S(2)}, u32[]{:S(2)}) collective-permute-start(bf16[4,64,640]{2,1,0:T(8,128)(2,1)S(1)} %pad_maximum_fusion.1.q0), channel_id=1, source_target_pairs={{0,32},{8,40},{16,48},{24,56},{32,64},{40,72},{48,80},{56,88},{64,... | collective-permute-start | bytes 983048 | tf_op jit(solution)/shard_map/ppermute | solution.py:33
  20.2 15.3 %collective-permute-start.4 = (bf16[4,64,640]{2,1,0:T(8,128)(2,1)S(1)}, bf16[4,64,640]{2,1,0:T(8,128)(2,1)S(1)}, u32[]{:S(2)}, u32[]{:S(2)}) collective-permute-start(bf16[4,64,640]{2,1,0:T(8,128)(2,1)S(1)} %pad_maximum_fusion.1.q0), channel_id=1, source_target_pairs={{0,64},{8,72},{16,80},{24,88},{32,96},{40,104},{48,112},{56,120},{... | collective-permute-start | bytes 983048 | tf_op jit(solution)/shard_map/ppermute | solution.py:33
  22.6 13.3 %collective-permute-start.5 = (bf16[4,64,640]{2,1,0:T(8,128)(2,1)S(1)}, bf16[4,64,640]{2,1,0:T(8,128)(2,1)S(1)}, u32[]{:S(2)}, u32[]{:S(2)}) collective-permute-start(bf16[4,64,640]{2,1,0:T(8,128)(2,1)S(1)} %pad_maximum_fusion.1.q0), channel_id=1, source_target_pairs={{0,96},{8,104},{16,112},{24,120},{32,0},{40,8},{48,16},{56,24},{64... | collective-permute-start | bytes 983048 | tf_op jit(solution)/shard_map/ppermute | solution.py:33
  62.2 6.7 %copy-start.7 = (s32[64,2]{0,1:T(2,128)S(1)}, s32[64,2]{0,1:T(2,128)}, u32[]{:S(2)}) copy-start(s32[64,2]{0,1:T(2,128)} %param.20) | copy-start | bytes 1540
  62.2 38.0 %copy-start.6 = (bf16[4096]{0:T(1024)(128)(2,1)S(1)}, bf16[4096]{0:T(1024)(128)(2,1)}, u32[]{:S(2)}) copy-start(bf16[4096]{0:T(1024)(128)(2,1)} %param.22) | copy-start | bytes 24580
  62.2 24.4 %all-to-all-start = ((bf16[16,64,640]{2,1,0:T(8,128)(2,1)}), bf16[16,64,640]{2,1,0:T(8,128)(2,1)S(1)}, u32[]{:S(2)}, u32[]{:S(2)}) async-start(bf16[16,64,640]{2,1,0:T(8,128)(2,1)} %attend.1), calls=%async_computation | async-start | bytes 2621440 | tf_op jit(solution)/shard_map/all_to_all | solution.py:272
  86.6 1.1 copy-start.2
  90.9 15.8 %all-to-all-start.1 = ((bf16[8,32,512]{2,1,0:T(8,128)(2,1)}), bf16[8,32,512]{2,1,0:T(8,128)(2,1)S(1)}, u32[]{:S(2)}, u32[]{:S(2)}) async-start(bf16[8,32,512]{2,1,0:T(8,128)(2,1)} %bitcast.24), calls=%async_computation.1 | async-start | bytes 524288 | tf_op jit(solution)/shard_map/all_to_all | solution.py:275
  100.2 56.5 %all-gather.2.cloned.1.call-start = ((), (), s32[]{:S(2)}) async-start(), calls=%async_computation.4 | async-start | bytes 4456448 | tf_op jit(solution)/shard_map/all_gather | solution.py:277
  106.7 0.7 copy-start.3
  156.7 2.2 copy-start.1
  182.4 2.0 copy-start
  184.3 5.2 %copy-start.8 = (bf16[64,2]{0,1:T(2,128)(2,1)S(1)}, bf16[64,2]{0,1:T(2,128)(2,1)}, u32[]{:S(2)}) copy-start(bf16[64,2]{0,1:T(2,128)(2,1)} %param.21) | copy-start | bytes 772
  184.3 66.7 %all-to-all-start.2 = ((bf16[16,32,4096]{2,1,0:T(8,128)(2,1)}), bf16[16,32,4096]{2,1,0:T(8,128)(2,1)}, u32[]{:S(2)}, u32[]{:S(2)}) async-start(bf16[16,32,4096]{2,1,0:T(8,128)(2,1)} %bitcast.20), calls=%async_computation.2 | async-start | bytes 8388608 | tf_op jit(solution)/shard_map/all_to_all | solution.py:279
  256.8 13.1 %all-to-all-start.3 = ((bf16[8,32,512]{2,1,0:T(8,128)(2,1)}), bf16[8,32,512]{2,1,0:T(8,128)(2,1)S(1)}, u32[]{:S(2)}, u32[]{:S(2)}) async-start(bf16[8,32,512]{2,1,0:T(8,128)(2,1)} %add_up.1), calls=%async_computation.3 | async-start | bytes 524288 | tf_op jit(solution)/shard_map/all_to_all | solution.py:283
  269.9 0.7 copy-start.4
Sparse Core Ops, SparseCore 0:
  109.3 47.3 all-gather.1

commit v2 on v1

--- a/solution.py
+++ b/solution.py
@@ -37,32 +37,36 @@
     step = pl.program_id(0)
     for k, ref in enumerate((q0, q1, q2, q3)):
 
-        @pl.when(step // 4 == k)
+        @pl.when(step // 2 == k)
         def _(ref=ref):
-            q_scr[...] = ref[step % 4]
-
-    bias = q_scr[:, 512:640]
-    rows = [
-        jnp.concatenate([q_scr[:, 128 * h : 128 * h + 128], bias], axis=1) for h in range(4)
-    ]
-    q_wide = jnp.concatenate(rows, axis=0)
-    scores = jnp.dot(q_wide, kt_ref[...], preferred_element_type=F32)
-    top = jnp.max(scores, axis=1, keepdims=True) * SCALE2
-    top = top.astype(BF).astype(F32)
-    probs = jnp.exp2(scores * SCALE2 - top).astype(BF)
-    both = jnp.dot(probs, v_ref[...], preferred_element_type=F32)
+            q_scr[...] = ref[pl.ds(2 * (step % 2), 2)]
+
     lane = lax.broadcasted_iota(jnp.int32, (64, 128), 1)
-    stats = jnp.zeros((64, 128), F32)
-    for h in range(4):
-        part = both[64 * h : 64 * h + 64]
-        out_ref[0, :, 128 * h : 128 * h + 128] = part[:, :128].astype(BF)
-        total = part[:, 128:256]
-        high = total.astype(BF).astype(F32)
-        low = total - high
-        stats = jnp.where(lane == h, top[64 * h : 64 * h + 64], stats)
-        stats = jnp.where(lane == 4 + h, high, stats)
-        stats = jnp.where(lane == 8 + h, low, stats)
-    out_ref[0, :, 512:640] = stats.astype(BF)
+    for b in range(2):
+        bias = q_scr[b, :, 512:640]
+        place = order_ref[2 * step + b]
+        stats = jnp.zeros((64, 128), F32)
+        for pair in range(2):
+            rows = [
+                jnp.concatenate([q_scr[b, :, 128 * h : 128 * h + 128], bias], axis=1)
+                for h in (2 * pair, 2 * pair + 1)
+            ]
+            q_wide = jnp.concatenate(rows, axis=0)
+            scores = jnp.dot(q_wide, kt_ref[...], preferred_element_type=F32)
+            top = jnp.max(scores, axis=1, keepdims=True) * SCALE2
+            top = top.astype(BF).astype(F32)
+            probs = jnp.exp2(scores * SCALE2 - top).astype(BF)
+            both = jnp.dot(probs, v_ref[...], preferred_element_type=F32)
+            for k in range(2):
+                h = 2 * pair + k
+                part = both[64 * k : 64 * k + 64]
+                out_ref[place, :, 128 * h : 128 * h + 128] = part[:, :128].astype(BF)
+                total = part[:, 128:256]
+                high = total.astype(BF).astype(F32)
+                stats = jnp.where(lane == h, top[64 * k : 64 * k + 64], stats)
+                stats = jnp.where(lane == 4 + h, high, stats)
+                stats = jnp.where(lane == 8 + h, total - high, stats)
+        out_ref[place, :, 512:640] = stats.astype(BF)
 
 
 def attend(order, blocks, kt_wide, v_wide):
@@ -72,11 +76,11 @@
         out_shape=jax.ShapeDtypeStruct((16, 64, 640), BF),
         grid_spec=pltpu.PrefetchScalarGridSpec(
             num_scalar_prefetch=1,
-            grid=(16,),
+            grid=(8,),
             in_specs=[whole((4, 64, 640)) for _ in range(4)]
             + [whole(kt_wide.shape), whole(v_wide.shape)],
-            out_specs=pl.BlockSpec((1, 64, 640), lambda g, order: (order[g], 0, 0)),
-            scratch_shapes=[pltpu.VMEM((64, 640), BF)],
+            out_specs=whole((16, 64, 640)),
+            scratch_shapes=[pltpu.VMEM((2, 64, 640), BF)],
         ),
         compiler_params=pltpu.CompilerParams(vmem_limit_bytes=40 << 20),
         name="attend",
@@ -114,7 +118,7 @@
     )(got, residual, disp)
 
 
-def norm_kernel(x_ref, gain_ref, out_ref):
+def norm_kernel(x_ref, gain_ref, low_ref, high_ref):
     total = jnp.zeros((32, 512), F32)
     for f in range(8):
         wide = x_ref[f].astype(F32)
@@ -122,85 +126,132 @@
     mean = jnp.sum(total, axis=1, keepdims=True) * (1.0 / 4096.0)
     inverse = lax.rsqrt(mean + EPS)
     for f in range(8):
-        cols = slice(512 * f, 512 * f + 512)
-        out_ref[:, cols] = (x_ref[f].astype(F32) * inverse * gain_ref[:, cols].astype(F32)).astype(BF)
+        gain = gain_ref[:, 512 * f : 512 * f + 512].astype(F32)
+        value = (x_ref[f].astype(F32) * inverse * gain).astype(BF)
+        half = low_ref if f < 4 else high_ref
+        half[:, 512 * (f % 4) : 512 * (f % 4) + 512] = value
 
 
 def norm(x, gain):
     return pl.pallas_call(
         norm_kernel,
-        out_shape=jax.ShapeDtypeStruct((32, 4096), BF),
+        out_shape=(jax.ShapeDtypeStruct((32, 2048), BF), jax.ShapeDtypeStruct((32, 2048), BF)),
         name="norm",
     )(x, gain)
 
 
-def moe_kernel(x_ref, wg_ref, wu_ref, wd_ref, out_ref, gate_acc, up_acc, hid):
-    step = pl.program_id(0)
-
-    @pl.when(step < 8)
+def hidden_kernel(*refs):
+    low, high = refs[0:4], refs[4:8]
+    wg_ref, wu_ref, out_ref, x_scr = refs[8:]
+
+    @pl.when(pl.program_id(0) == 0)
     def _():
-        x = x_ref[...]
-        gate = jnp.dot(x, wg_ref[0], preferred_element_type=F32)
-        up = jnp.dot(x, wu_ref[0], preferred_element_type=F32)
-
-        @pl.when(step == 0)
-        def _():
-            gate_acc[...] = gate
-            up_acc[...] = up
-
-        @pl.when(step > 0)
-        def _():
-            gate_acc[...] += gate
-            up_acc[...] += up
-
-        @pl.when(step == 7)
-        def _():
-            g = gate_acc[...]
-            hid[...] = (g / (1.0 + jnp.exp(-g)) * up_acc[...]).astype(BF)
-
-    @pl.when(step >= 8)
+        for a in range(4):
+            for b in range(4):
+                r = 32 * (4 * a + b)
+                x_scr[r : r + 32, :2048] = low[a][b]
+                x_scr[r : r + 32, 2048:] = high[b][a]
+
+    both = jnp.concatenate([wg_ref[0], wu_ref[0]], axis=1)
+    result = jnp.dot(x_scr[...], both, preferred_element_type=F32)
+    gate = result[:, :128]
+    out_ref[...] = (gate / (1.0 + jnp.exp(-gate)) * result[:, 128:]).astype(BF)
+
+
+def hidden_units(low, high, w_gate, w_up):
+    part = pl.BlockSpec((4, 32, 2048), lambda i: (0, 0, 0), pipeline_mode=pl.Buffered(1))
+    tile = pl.BlockSpec((1, 4096, 128), lambda i: (0, 0, i))
+    return pl.pallas_call(
+        hidden_kernel,
+        out_shape=jax.ShapeDtypeStruct((512, 896), BF),
+        grid=(7,),
+        in_specs=[part] * 8 + [tile, tile],
+        out_specs=pl.BlockSpec((512, 128), lambda i: (0, i)),
+        scratch_shapes=[pltpu.VMEM((512, 4096), BF)],
+        compiler_params=pltpu.CompilerParams(vmem_limit_bytes=40 << 20),
+        name="hidden_units",
+    )(*low, *high, w_gate, w_up)
+
+
+def down_kernel(swap, h_ref, wd_ref, o0, o1, o2, o3, h_scr):
+    @pl.when(pl.program_id(0) == 0)
     def _():
-        out_ref[...] = jnp.dot(hid[...], wd_ref[0], preferred_element_type=F32).astype(BF)
-
-
-def moe(x, w_gate, w_up, w_down):
-    return pl.pallas_call(
-        moe_kernel,
-        out_shape=jax.ShapeDtypeStruct((512, 4096), BF),
-        grid=(16,),
+        for a in range(4):
+            for b in range(4):
+                r = 32 * (4 * a + b)
+                t = 32 * (4 * b + a) if swap else r
+                h_scr[t : t + 32] = h_ref[r : r + 32]
+
+    result = jnp.dot(h_scr[...], wd_ref[0], preferred_element_type=F32)
+    for k, ref in enumerate((o0, o1, o2, o3)):
+        ref[...] = result[128 * k : 128 * k + 128].astype(BF)
+
+
+def down(hidden, w_down, swap):
+    offset = 4 if swap else 0
+    return pl.pallas_call(
+        functools.partial(down_kernel, swap),
+        out_shape=[jax.ShapeDtypeStruct((128, 2048), BF)] * 4,
+        grid=(4,),
         in_specs=[
-            pl.BlockSpec((512, 512), lambda i: (0, jnp.minimum(i, 7))),
-            pl.BlockSpec((1, 512, 896), lambda i: (0, jnp.minimum(i, 7), 0)),
-            pl.BlockSpec((1, 512, 896), lambda i: (0, jnp.minimum(i, 7), 0)),
-            pl.BlockSpec((1, 896, 512), lambda i: (0, 0, jnp.maximum(i - 8, 0))),
+            pl.BlockSpec((512, 896), lambda i: (0, 0)),
+            pl.BlockSpec((1, 896, 512), lambda i: (0, 0, i + offset)),
         ],
-        out_specs=pl.BlockSpec((512, 512), lambda i: (0, jnp.maximum(i - 8, 0))),
-        scratch_shapes=[
-            pltpu.VMEM((512, 896), F32),
-            pltpu.VMEM((512, 896), F32),
-            pltpu.VMEM((512, 896), BF),
-        ],
+        out_specs=[pl.BlockSpec((128, 512), lambda i: (0, i))] * 4,
+        scratch_shapes=[pltpu.VMEM((512, 896), BF)],
         compiler_params=pltpu.CompilerParams(vmem_limit_bytes=40 << 20),
-        name="moe",
-    )(x, w_gate, w_up, w_down)
-
-
-def add_kernel(x_ref, out_ref):
-    total = jnp.zeros((32, 512), F32)
-    for j in range(16):
-        total = total + x_ref[j].astype(F32)
-    out_ref[0] = total.astype(BF)
-
-
-def add_up(x):
+        name="down_high" if swap else "down_low",
+    )(hidden, w_down)
+
+
+def add_kernel(a, b, c, d, o0, o1, o2, o3):
+    total = a[...].astype(F32) + b[...].astype(F32) + c[...].astype(F32) + d[...].astype(F32)
+    for k, ref in enumerate((o0, o1, o2, o3)):
+        ref[...] = total[32 * k : 32 * k + 32].astype(BF)
+
+
+def add_first(parts):
     return pl.pallas_call(
         add_kernel,
-        out_shape=jax.ShapeDtypeStruct((8, 32, 512), BF),
-        grid=(8,),
-        in_specs=[pl.BlockSpec((16, 32, 512), lambda f: (0, 0, f))],
-        out_specs=pl.BlockSpec((1, 32, 512), lambda f: (f, 0, 0)),
-        name="add_up",
-    )(x)
+        out_shape=[jax.ShapeDtypeStruct((32, 2048), BF)] * 4,
+        grid=(2,),
+        in_specs=[pl.BlockSpec((128, 1024), lambda i: (0, i))] * 4,
+        out_specs=[pl.BlockSpec((32, 1024), lambda i: (0, i))] * 4,
+        name="add_first",
+    )(*parts)
+
+
+def last_kernel(*refs):
+    out_ref = refs[8]
+    for half in range(2):
+        a, b, c, d = refs[4 * half : 4 * half + 4]
+        for f in range(4):
+            cols = slice(512 * f, 512 * f + 512)
+            total = (
+                a[:, cols].astype(F32)
+                + b[:, cols].astype(F32)
+                + c[:, cols].astype(F32)
+                + d[:, cols].astype(F32)
+            )
+            out_ref[4 * half + f] = total.astype(BF)
+
+
+def add_last(low, high):
+    return pl.pallas_call(
+        last_kernel, out_shape=jax.ShapeDtypeStruct((8, 32, 512), BF), name="add_last"
+    )(*low, *high)
+
+
+def spread_near(value, axis):
+    return [value] + [shift_dp(value, axis, s) for s in (1, 2, 3)]
+
+
+def spread_far(near, axis):
+    return [near] + [shift_dp(near, axis, s) for s in (1, 2, 3)]
+
+
+def collect(parts, axis):
+    return [parts[0]] + [shift_dp(parts[s], axis, -s) for s in (1, 2, 3)]
 
 
 def finish_kernel(mix_ref, y_ref, stream_ref, out_ref):
@@ -273,13 +324,13 @@
     attention_out, stream, slots = combine(got, residual, disp)
 
     mine = lax.all_to_all(slots.reshape(8, 32, 512), "expert", split_axis=0, concat_axis=0, tiled=True)
-    normed = norm(mine, norm_gain[None, :])
-    gathered = lax.all_gather(normed, "dp", axis=0, tiled=True)
-    expert_y = moe(gathered, w_gate, w_up, w_down)
-    spread = lax.all_to_all(
-        expert_y.reshape(16, 32, 4096), "dp", split_axis=0, concat_axis=0, tiled=True
-    )
-    summed = add_up(spread)
+    low, high = norm(mine, norm_gain[None, :])
+    low, high = lax.optimization_barrier((spread_near(low, 1), spread_near(high, 0)))
+    low, high = spread_far(jnp.stack(low), 0), spread_far(jnp.stack(high), 1)
+    hidden = hidden_units(low, high, w_gate, w_up)
+    low = add_first(collect(down(hidden, w_down, False), 0))
+    high = add_first(collect(down(hidden, w_down, True), 1))
+    summed = add_last(collect(low, 1), collect(high, 0))
     back = lax.all_to_all(summed, "expert", split_axis=0, concat_axis=0, tiled=True)
     layer_out = finish(mix, back.reshape(256, 512), stream)
     return (attention_out, layer_out)

time: 283 us -> 226 us (0.80)
  waiting for transfers between devices: 149 us -> 84.3 us
  starting transfers between devices: 38.7 us -> 68.5 us
  between operations: 14.2 us -> 1.01 us
  Pallas kernels: 62.3 us -> 51.1 us
  local copies, waits for them, and re-layouts: 9.04 us -> 12.2 us
    all_to_all x1 -> x0, waiting for transfers between devices: 61.5 us -> none  [body(): lax.all_to_all(expert_y.reshape(16, 32, 4096), 'dp', split_axis=0, concat...]
    all_gather x1 -> x0, waiting for transfers between devices: 47.5 us -> none  [body(): gathered = lax.all_gather(normed, 'dp', axis=0, tiled=True)]
    ppermute x6 -> x30, waiting for transfers between devices: 12.1 us -> 56.1 us  [shift_dp(): return lax.ppermute(value, 'dp', ring_pairs(axis, shift))]
    ppermute x6 -> x30, starting transfers between devices: 11.1 us -> 40 us  [shift_dp(): return lax.ppermute(value, 'dp', ring_pairs(axis, shift))]
    pallas_call x1, Pallas kernels: 26.3 us -> 19.2 us  [attend(): pl.pallas_call(attend_kernel, out_shape=jax.ShapeDtypeStruct((16, 64, 640...]
    all_to_all x1, starting transfers between devices: 6.62 us -> 12.7 us  [body(): lax.all_to_all(summed, 'expert', split_axis=0, concat_axis=0, tiled=True)]
    all_to_all x1 -> x0, starting transfers between devices: 5.16 us -> none  [body(): lax.all_to_all(expert_y.reshape(16, 32, 4096), 'dp', split_axis=0, concat...]
    pallas_call x3 -> x7, Pallas kernels: 31.1 us -> 26.9 us  [the longest x1 11.7 us: hidden_units(): pl.pallas_call(hidden_kernel, out_shape=jax.ShapeDtypeStruct((512, 896),...]
  transfers between devices with their start and end apart: 11 -> 33, of which waited for: 8 -> 21; matrix products, arithmetic and copies ran while one was open for 2% -> 3% of each run, Pallas kernels for 0% -> 4%
where the time goes in v2:
time: 226 us; the launch traced here: 225 us
  waiting for transfers between devices  84.3 us (37%)
  starting transfers between devices  68.5 us (30%)
  Pallas kernels  51.1 us (23%)
  local copies, waits for them, and re-layouts  12.2 us (5%)
  other arithmetic  7.6 us (3%)
    ppermute x30, waiting for transfers between devices, shift_dp(): return lax.ppermute(value, 'dp', ring_pairs(axis, shift))  56.1 us
    ppermute x30, starting transfers between devices, shift_dp(): return lax.ppermute(value, 'dp', ring_pairs(axis, shift))  40 us
    pallas_call x1, Pallas kernels, attend(): pl.pallas_call(attend_kernel, out_shape=jax.ShapeDtypeStruct((16, 64, 640...  19.2 us
    all_to_all x1, waiting for transfers between devices, body(): got = lax.all_to_all(partial, 'dp', split_axis=0, concat_axis=0, tiled=True)  16.8 us
    all_to_all x1, starting transfers between devices, body(): lax.all_to_all(summed, 'expert', split_axis=0, concat_axis=0, tiled=True)  12.7 us
    pallas_call x1, Pallas kernels, hidden_units(): pl.pallas_call(hidden_kernel, out_shape=jax.ShapeDtypeStruct((512, 896),...  11.7 us
    unnamed x49, local copies, waits for them, and re-layouts  11.1 us
    all_to_all x1, starting transfers between devices, body(): lax.all_to_all(slots.reshape(8, 32, 512), 'expert', split_axis=0, concat_...  9.27 us
  transfers between devices with their start and end apart: 33, of which 21 were waited for; matrix products, arithmetic and copies ran while one was open for 3% of the time, Pallas kernels for 4%

profile of v2, /device:TPU:1, one launch (start us, length us, event | category | flops | bytes accessed | tf_op | source)
XLA Modules:
  0.0 224.8 jit_solution(5094326652465794505)
XLA Ops:
  5.9 2.6 %collective-permute-start.1 = (bf16[1,64,640]{2,1,0:T(8,128)(2,1)S(1)}, bf16[1,64,640]{2,1,0:T(8,128)(2,1)S(1)}, u32[]{:S(2)}, u32[]{:S(2)}) collective-permute-start(bf16[1,64,640]{2,1,0:T(8,128)(2,1)S(1)} %maximum_bitcast_fusion), channel_id=1, source_target_pairs={{0,16},{8,24},{16,0},{24,8},{32,48},{40,56},{48,32},{56,40},{64,80... | collective-permute-start | bytes 245768 | tf_op jit(solution)/shard_map/ppermute | solution.py:33
  13.6 2.5 %collective-permute-start.4 = (bf16[4,64,640]{2,1,0:T(8,128)(2,1)S(1)}, bf16[4,64,640]{2,1,0:T(8,128)(2,1)S(1)}, u32[]{:S(2)}, u32[]{:S(2)}) collective-permute-start(bf16[4,64,640]{2,1,0:T(8,128)(2,1)S(1)} %pad_maximum_fusion.3.q0), channel_id=1, source_target_pairs={{0,64},{8,72},{16,80},{24,88},{32,96},{40,104},{48,112},{56,120},{... | collective-permute-start | bytes 983048 | tf_op jit(solution)/shard_map/ppermute | solution.py:33
  17.3 3.2 %collective-permute-done.3.q1 = bf16[4,64,640]{2,1,0:T(8,128)(2,1)S(1)} collective-permute-done((bf16[4,64,640]{2,1,0:T(8,128)(2,1)S(1)}, bf16[4,64,640]{2,1,0:T(8,128)(2,1)S(1)}, u32[]{:S(2)}, u32[]{:S(2)}) %collective-permute-start.3) | collective-permute-done | bytes 327712 | tf_op jit(solution)/shard_map/ppermute | solution.py:33
  20.5 8.4 %collective-permute-done.4.q2 = bf16[4,64,640]{2,1,0:T(8,128)(2,1)S(1)} collective-permute-done((bf16[4,64,640]{2,1,0:T(8,128)(2,1)S(1)}, bf16[4,64,640]{2,1,0:T(8,128)(2,1)S(1)}, u32[]{:S(2)}, u32[]{:S(2)}) %collective-permute-start.4) | collective-permute-done | bytes 327712 | tf_op jit(solution)/shard_map/ppermute | solution.py:33
  29.4 19.2 %attend.1 = bf16[16,64,640]{2,1,0:T(8,128)(2,1)} custom-call(s32[16]{0:T(128)S(1)} %fusion.7.order_ref, bf16[4,64,640]{2,1,0:T(8,128)(2,1)S(1)} %pad_maximum_fusion.3.q0, bf16[4,64,640]{2,1,0:T(8,128)(2,1)S(1)} %collective-permute-done.3.q1, bf16[4,64,640]{2,1,0:T(8,128)(2,1)S(1)} %collective-permute-done.4.q2, ...), custom_call_target="tpu_custom_call" | custom-call | tf_op jit(solution)/shard_map/attend/pallas_call | solution.py:74
  48.6 6.6 %all-to-all-start = ((bf16[16,64,640]{2,1,0:T(8,128)(2,1)}), bf16[16,64,640]{2,1,0:T(8,128)(2,1)S(1)}, u32[]{:S(2)}, u32[]{:S(2)}) async-start(bf16[16,64,640]{2,1,0:T(8,128)(2,1)} %attend.1), calls=%async_computation | async-start | bytes 2621440 | tf_op jit(solution)/shard_map/all_to_all | solution.py:323
  56.2 16.8 %all-to-all-done.got_ref = bf16[16,64,640]{2,1,0:T(8,128)(2,1)S(1)} async-done(((bf16[16,64,640]{2,1,0:T(8,128)(2,1)}), bf16[16,64,640]{2,1,0:T(8,128)(2,1)S(1)}, u32[]{:S(2)}, u32[]{:S(2)}) %all-to-all-start) | async-done | bytes 1310752 | tf_op jit(solution)/shard_map/all_to_all | solution.py:323
  74.1 3.2 %combine.1 = (bf16[64,512]{1,0:T(8,128)(2,1)}, bf16[64,512]{1,0:T(8,128)(2,1)}, bf16[256,512]{1,0:T(8,128)(2,1)}) custom-call(bf16[16,64,640]{2,1,0:T(8,128)(2,1)} %copy-done.3, bf16[64,512]{1,0:T(8,128)(2,1)} %res_ref.1, bf16[256,64]{1,0:T(8,128)(2,1)} %fusion.2.disp_ref), custom_call_target="tpu_custom_call" | custom-call | tf_op jit(solution)/shard_map/combine/pallas_call | solution.py:110
  77.3 9.3 %all-to-all-start.1 = ((bf16[8,32,512]{2,1,0:T(8,128)(2,1)}), bf16[8,32,512]{2,1,0:T(8,128)(2,1)S(1)}, u32[]{:S(2)}, u32[]{:S(2)}) async-start(bf16[8,32,512]{2,1,0:T(8,128)(2,1)} %bitcast.32), calls=%async_computation.1 | async-start | bytes 524288 | tf_op jit(solution)/shard_map/all_to_all | solution.py:326
  87.2 5.9 %all-to-all-done.1.x_ref = bf16[8,32,512]{2,1,0:T(8,128)(2,1)S(1)} async-done(((bf16[8,32,512]{2,1,0:T(8,128)(2,1)}), bf16[8,32,512]{2,1,0:T(8,128)(2,1)S(1)}, u32[]{:S(2)}, u32[]{:S(2)}) %all-to-all-start.1) | async-done | bytes 262176 | tf_op jit(solution)/shard_map/all_to_all | solution.py:326
  112.0 2.4 %collective-permute-start.13 = (bf16[4,32,2048]{2,1,0:T(8,128)(2,1)S(1)}, bf16[4,32,2048]{2,1,0:T(8,128)(2,1)S(1)}, u32[]{:S(2)}, u32[]{:S(2)}) collective-permute-start(bf16[4,32,2048]{2,1,0:T(8,128)(2,1)S(1)} %pad_maximum_fusion.1.refs_0_), channel_id=1, source_target_pairs={{0,64},{8,72},{16,80},{24,88},{32,96},{40,104},{48,112},{56,120},{... | collective-permute-start | bytes 1572872 | tf_op jit(solution)/shard_map/ppermute | solution.py:33
  114.3 5.2 %collective-permute-done.15.refs_5_ = bf16[4,32,2048]{2,1,0:T(8,128)(2,1)S(1)} collective-permute-done((bf16[4,32,2048]{2,1,0:T(8,128)(2,1)S(1)}, bf16[4,32,2048]{2,1,0:T(8,128)(2,1)S(1)}, u32[]{:S(2)}, u32[]{:S(2)}) %collective-permute-start.15) | collective-permute-done | bytes 524320 | tf_op jit(solution)/shard_map/ppermute | solution.py:33
  119.6 10.6 %collective-permute-done.16.refs_6_ = bf16[4,32,2048]{2,1,0:T(8,128)(2,1)S(1)} collective-permute-done((bf16[4,32,2048]{2,1,0:T(8,128)(2,1)S(1)}, bf16[4,32,2048]{2,1,0:T(8,128)(2,1)S(1)}, u32[]{:S(2)}, u32[]{:S(2)}) %collective-permute-start.16) | collective-permute-done | bytes 524320 | tf_op jit(solution)/shard_map/ppermute | solution.py:33
  130.2 3.4 %collective-permute-done.17.refs_7_ = bf16[4,32,2048]{2,1,0:T(8,128)(2,1)S(1)} collective-permute-done((bf16[4,32,2048]{2,1,0:T(8,128)(2,1)S(1)}, bf16[4,32,2048]{2,1,0:T(8,128)(2,1)S(1)}, u32[]{:S(2)}, u32[]{:S(2)}) %collective-permute-start.17) | collective-permute-done | bytes 524320 | tf_op jit(solution)/shard_map/ppermute | solution.py:33
  134.0 3.1 %copy-done = bf16[1,4096,896]{2,1,0:T(8,128)(2,1)S(1)} copy-done((bf16[1,4096,896]{2,1,0:T(8,128)(2,1)S(1)}, bf16[1,4096,896]{2,1,0:T(8,128)(2,1)}, u32[]{:S(2)}) %copy-start) | copy-done | bytes 7340056
  137.1 11.7 %hidden_units.1.h_ref = bf16[512,896]{1,0:T(8,128)(2,1)S(1)} custom-call(bf16[4,32,2048]{2,1,0:T(8,128)(2,1)S(1)} %pad_maximum_fusion.1.refs_0_, bf16[4,32,2048]{2,1,0:T(8,128)(2,1)S(1)} %collective-permute-done.12.refs_1_, bf16[4,32,2048]{2,1,0:T(8,128)(2,1)S(1)} %collective-permute-done.13.refs_2_, ...), custom_call_target="tpu_custom_call" | custom-call | tf_op jit(solution)/shard_map/hidden_units/pallas_call | solution.py:164
  148.8 3.4 %down_high.1 = (bf16[128,2048]{1,0:T(8,128)(2,1)S(1)}, bf16[128,2048]{1,0:T(8,128)(2,1)S(1)}, bf16[128,2048]{1,0:T(8,128)(2,1)S(1)}, bf16[128,2048]{1,0:T(8,128)(2,1)S(1)}) custom-call(bf16[512,896]{1,0:T(8,128)(2,1)S(1)} %hidden_units.1.h_ref, bf16[1,896,4096]{2,1,0:T(8,128)(2,1)S(1)} %bitcast.28), custom_call_target="tpu_custom_call" | custom-call | tf_op jit(solution)/shard_map/down_high/pallas_call | solution.py:192
  153.0 3.0 %collective-permute-start.24 = (bf16[128,2048]{1,0:T(8,128)(2,1)S(1)}, bf16[128,2048]{1,0:T(8,128)(2,1)S(1)}, u32[]{:S(2)}, u32[]{:S(2)}) collective-permute-start(bf16[128,2048]{1,0:T(8,128)(2,1)S(1)} %get-tuple-element.52), channel_id=1, source_target_pairs={{0,24},{8,0},{16,8},{24,16},{32,56},{40,32},{48,40},{56,48},{64,88... | collective-permute-start | bytes 1572872 | tf_op jit(solution)/shard_map/ppermute | solution.py:33
  157.6 3.4 %down_low.1 = (bf16[128,2048]{1,0:T(8,128)(2,1)S(1)}, bf16[128,2048]{1,0:T(8,128)(2,1)S(1)}, bf16[128,2048]{1,0:T(8,128)(2,1)S(1)}, bf16[128,2048]{1,0:T(8,128)(2,1)S(1)}) custom-call(bf16[512,896]{1,0:T(8,128)(2,1)S(1)} %hidden_units.1.h_ref, bf16[1,896,4096]{2,1,0:T(8,128)(2,1)S(1)} %bitcast.28), custom_call_target="tpu_custom_call" | custom-call | tf_op jit(solution)/shard_map/down_low/pallas_call | solution.py:192
  161.8 3.4 %collective-permute-start.18 = (bf16[128,2048]{1,0:T(8,128)(2,1)S(1)}, bf16[128,2048]{1,0:T(8,128)(2,1)S(1)}, u32[]{:S(2)}, u32[]{:S(2)}) collective-permute-start(bf16[128,2048]{1,0:T(8,128)(2,1)S(1)} %get-tuple-element.44), channel_id=1, source_target_pairs={{0,96},{8,104},{16,112},{24,120},{32,0},{40,8},{48,16},{56,24},{64... | collective-permute-start | bytes 1572872 | tf_op jit(solution)/shard_map/ppermute | solution.py:33
  168.5 12.0 %collective-permute-done.26.d = bf16[128,2048]{1,0:T(8,128)(2,1)S(1)} collective-permute-done((bf16[128,2048]{1,0:T(8,128)(2,1)S(1)}, bf16[128,2048]{1,0:T(8,128)(2,1)S(1)}, u32[]{:S(2)}, u32[]{:S(2)}) %collective-permute-start.26) | collective-permute-done | bytes 524320 | tf_op jit(solution)/shard_map/ppermute | solution.py:33
  185.1 4.9 %collective-permute-start.28 = (bf16[32,2048]{1,0:T(8,128)(2,1)}, bf16[32,2048]{1,0:T(8,128)(2,1)S(1)}, u32[]{:S(2)}, u32[]{:S(2)}) collective-permute-start(bf16[32,2048]{1,0:T(8,128)(2,1)} %get-tuple-element.57), channel_id=1, source_target_pairs={{0,64},{8,72},{16,80},{24,88},{32,96},{40,104},{48,112},{56,120},{... | collective-permute-start | bytes 393224 | tf_op jit(solution)/shard_map/ppermute | solution.py:33
  203.2 12.7 %all-to-all-start.2 = ((bf16[8,32,512]{2,1,0:T(8,128)(2,1)}), bf16[8,32,512]{2,1,0:T(8,128)(2,1)S(1)}, u32[]{:S(2)}, u32[]{:S(2)}) async-start(bf16[8,32,512]{2,1,0:T(8,128)(2,1)} %add_last.1), calls=%async_computation.2 | async-start | bytes 524288 | tf_op jit(solution)/shard_map/all_to_all | solution.py:334
  216.8 5.5 %all-to-all-done.2 = bf16[8,32,512]{2,1,0:T(8,128)(2,1)S(1)} async-done(((bf16[8,32,512]{2,1,0:T(8,128)(2,1)}), bf16[8,32,512]{2,1,0:T(8,128)(2,1)S(1)}, u32[]{:S(2)}, u32[]{:S(2)}) %all-to-all-start.2) | async-done | bytes 262176 | tf_op jit(solution)/shard_map/all_to_all | solution.py:334
  (129 shorter events, 61.7 us)
Async XLA Ops:
  3.8 8.1 %collective-permute-start = (bf16[1,64,640]{2,1,0:T(8,128)(2,1)S(1)}, bf16[1,64,640]{2,1,0:T(8,128)(2,1)S(1)}, u32[]{:S(2)}, u32[]{:S(2)}) collective-permute-start(bf16[1,64,640]{2,1,0:T(8,128)(2,1)S(1)} %maximum_bitcast_fusion), channel_id=1, source_target_pairs={{0,8},{8,16},{16,24},{24,0},{32,40},{40,48},{48,56},{56,32},{64,72... | collective-permute-start | bytes 245768 | tf_op jit(solution)/shard_map/ppermute | solution.py:33
  12.0 8.5 %collective-permute-start.3 = (bf16[4,64,640]{2,1,0:T(8,128)(2,1)S(1)}, bf16[4,64,640]{2,1,0:T(8,128)(2,1)S(1)}, u32[]{:S(2)}, u32[]{:S(2)}) collective-permute-start(bf16[4,64,640]{2,1,0:T(8,128)(2,1)S(1)} %pad_maximum_fusion.3.q0), channel_id=1, source_target_pairs={{0,32},{8,40},{16,48},{24,56},{32,64},{40,72},{48,80},{56,88},{64,... | collective-permute-start | bytes 983048 | tf_op jit(solution)/shard_map/ppermute | solution.py:33
  13.6 15.3 %collective-permute-start.4 = (bf16[4,64,640]{2,1,0:T(8,128)(2,1)S(1)}, bf16[4,64,640]{2,1,0:T(8,128)(2,1)S(1)}, u32[]{:S(2)}, u32[]{:S(2)}) collective-permute-start(bf16[4,64,640]{2,1,0:T(8,128)(2,1)S(1)} %pad_maximum_fusion.3.q0), channel_id=1, source_target_pairs={{0,64},{8,72},{16,80},{24,88},{32,96},{40,104},{48,112},{56,120},{... | collective-permute-start | bytes 983048 | tf_op jit(solution)/shard_map/ppermute | solution.py:33
  16.1 13.3 %collective-permute-start.5 = (bf16[4,64,640]{2,1,0:T(8,128)(2,1)S(1)}, bf16[4,64,640]{2,1,0:T(8,128)(2,1)S(1)}, u32[]{:S(2)}, u32[]{:S(2)}) collective-permute-start(bf16[4,64,640]{2,1,0:T(8,128)(2,1)S(1)} %pad_maximum_fusion.3.q0), channel_id=1, source_target_pairs={{0,96},{8,104},{16,112},{24,120},{32,0},{40,8},{48,16},{56,24},{64... | collective-permute-start | bytes 983048 | tf_op jit(solution)/shard_map/ppermute | solution.py:33
  48.6 24.4 %all-to-all-start = ((bf16[16,64,640]{2,1,0:T(8,128)(2,1)}), bf16[16,64,640]{2,1,0:T(8,128)(2,1)S(1)}, u32[]{:S(2)}, u32[]{:S(2)}) async-start(bf16[16,64,640]{2,1,0:T(8,128)(2,1)} %attend.1), calls=%async_computation | async-start | bytes 2621440 | tf_op jit(solution)/shard_map/all_to_all | solution.py:323
  77.3 15.8 %all-to-all-start.1 = ((bf16[8,32,512]{2,1,0:T(8,128)(2,1)}), bf16[8,32,512]{2,1,0:T(8,128)(2,1)S(1)}, u32[]{:S(2)}, u32[]{:S(2)}) async-start(bf16[8,32,512]{2,1,0:T(8,128)(2,1)} %bitcast.32), calls=%async_computation.1 | async-start | bytes 524288 | tf_op jit(solution)/shard_map/all_to_all | solution.py:326
  97.2 7.0 %collective-permute-start.6 = (bf16[32,2048]{1,0:T(8,128)(2,1)}, bf16[32,2048]{1,0:T(8,128)(2,1)S(1)}, u32[]{:S(2)}, u32[]{:S(2)}) collective-permute-start(bf16[32,2048]{1,0:T(8,128)(2,1)} %get-tuple-element.35), channel_id=1, source_target_pairs={{0,8},{8,16},{16,24},{24,0},{32,40},{40,48},{48,56},{56,32},{64,72... | collective-permute-start | bytes 393224 | tf_op jit(solution)/shard_map/ppermute | solution.py:33
  97.5 6.7 %collective-permute-start.7 = (bf16[32,2048]{1,0:T(8,128)(2,1)}, bf16[32,2048]{1,0:T(8,128)(2,1)S(1)}, u32[]{:S(2)}, u32[]{:S(2)}) collective-permute-start(bf16[32,2048]{1,0:T(8,128)(2,1)} %get-tuple-element.35), channel_id=1, source_target_pairs={{0,16},{8,24},{16,0},{24,8},{32,48},{40,56},{48,32},{56,40},{64,80... | collective-permute-start | bytes 393224 | tf_op jit(solution)/shard_map/ppermute | solution.py:33
  107.7 11.9 %collective-permute-start.15 = (bf16[4,32,2048]{2,1,0:T(8,128)(2,1)S(1)}, bf16[4,32,2048]{2,1,0:T(8,128)(2,1)S(1)}, u32[]{:S(2)}, u32[]{:S(2)}) collective-permute-start(bf16[4,32,2048]{2,1,0:T(8,128)(2,1)S(1)} %pad_maximum_fusion.2.refs_4_), channel_id=1, source_target_pairs={{0,8},{8,16},{16,24},{24,0},{32,40},{40,48},{48,56},{56,32},{64,72... | collective-permute-start | bytes 1572872 | tf_op jit(solution)/shard_map/ppermute | solution.py:33
  107.9 22.3 %collective-permute-start.16 = (bf16[4,32,2048]{2,1,0:T(8,128)(2,1)S(1)}, bf16[4,32,2048]{2,1,0:T(8,128)(2,1)S(1)}, u32[]{:S(2)}, u32[]{:S(2)}) collective-permute-start(bf16[4,32,2048]{2,1,0:T(8,128)(2,1)S(1)} %pad_maximum_fusion.2.refs_4_), channel_id=1, source_target_pairs={{0,16},{8,24},{16,0},{24,8},{32,48},{40,56},{48,32},{56,40},{64,80... | collective-permute-start | bytes 1572872 | tf_op jit(solution)/shard_map/ppermute | solution.py:33
  109.7 23.8 %collective-permute-start.17 = (bf16[4,32,2048]{2,1,0:T(8,128)(2,1)S(1)}, bf16[4,32,2048]{2,1,0:T(8,128)(2,1)S(1)}, u32[]{:S(2)}, u32[]{:S(2)}) collective-permute-start(bf16[4,32,2048]{2,1,0:T(8,128)(2,1)S(1)} %pad_maximum_fusion.2.refs_4_), channel_id=1, source_target_pairs={{0,24},{8,0},{16,8},{24,16},{32,56},{40,32},{48,40},{56,48},{64,88... | collective-permute-start | bytes 1572872 | tf_op jit(solution)/shard_map/ppermute | solution.py:33
  111.9 21.7 %collective-permute-start.12 = (bf16[4,32,2048]{2,1,0:T(8,128)(2,1)S(1)}, bf16[4,32,2048]{2,1,0:T(8,128)(2,1)S(1)}, u32[]{:S(2)}, u32[]{:S(2)}) collective-permute-start(bf16[4,32,2048]{2,1,0:T(8,128)(2,1)S(1)} %pad_maximum_fusion.1.refs_0_), channel_id=1, source_target_pairs={{0,32},{8,40},{16,48},{24,56},{32,64},{40,72},{48,80},{56,88},{64,... | collective-permute-start | bytes 1572872 | tf_op jit(solution)/shard_map/ppermute | solution.py:33
  112.0 22.1 %collective-permute-start.13 = (bf16[4,32,2048]{2,1,0:T(8,128)(2,1)S(1)}, bf16[4,32,2048]{2,1,0:T(8,128)(2,1)S(1)}, u32[]{:S(2)}, u32[]{:S(2)}) collective-permute-start(bf16[4,32,2048]{2,1,0:T(8,128)(2,1)S(1)} %pad_maximum_fusion.1.refs_0_), channel_id=1, source_target_pairs={{0,64},{8,72},{16,80},{24,88},{32,96},{40,104},{48,112},{56,120},{... | collective-permute-start | bytes 1572872 | tf_op jit(solution)/shard_map/ppermute | solution.py:33
  119.6 14.4 %collective-permute-start.14 = (bf16[4,32,2048]{2,1,0:T(8,128)(2,1)S(1)}, bf16[4,32,2048]{2,1,0:T(8,128)(2,1)S(1)}, u32[]{:S(2)}, u32[]{:S(2)}) collective-permute-start(bf16[4,32,2048]{2,1,0:T(8,128)(2,1)S(1)} %pad_maximum_fusion.1.refs_0_), channel_id=1, source_target_pairs={{0,96},{8,104},{16,112},{24,120},{32,0},{40,8},{48,16},{56,24},{64... | collective-permute-start | bytes 1572872 | tf_op jit(solution)/shard_map/ppermute | solution.py:33
  153.0 15.5 %collective-permute-start.24 = (bf16[128,2048]{1,0:T(8,128)(2,1)S(1)}, bf16[128,2048]{1,0:T(8,128)(2,1)S(1)}, u32[]{:S(2)}, u32[]{:S(2)}) collective-permute-start(bf16[128,2048]{1,0:T(8,128)(2,1)S(1)} %get-tuple-element.52), channel_id=1, source_target_pairs={{0,24},{8,0},{16,8},{24,16},{32,56},{40,32},{48,40},{56,48},{64,88... | collective-permute-start | bytes 1572872 | tf_op jit(solution)/shard_map/ppermute | solution.py:33
  156.0 12.5 %collective-permute-start.25 = (bf16[128,2048]{1,0:T(8,128)(2,1)S(1)}, bf16[128,2048]{1,0:T(8,128)(2,1)S(1)}, u32[]{:S(2)}, u32[]{:S(2)}) collective-permute-start(bf16[128,2048]{1,0:T(8,128)(2,1)S(1)} %get-tuple-element.53), channel_id=1, source_target_pairs={{0,16},{8,24},{16,0},{24,8},{32,48},{40,56},{48,32},{56,40},{64,80... | collective-permute-start | bytes 1572872 | tf_op jit(solution)/shard_map/ppermute | solution.py:33
  156.9 23.5 %collective-permute-start.26 = (bf16[128,2048]{1,0:T(8,128)(2,1)S(1)}, bf16[128,2048]{1,0:T(8,128)(2,1)S(1)}, u32[]{:S(2)}, u32[]{:S(2)}) collective-permute-start(bf16[128,2048]{1,0:T(8,128)(2,1)S(1)} %get-tuple-element.54), channel_id=1, source_target_pairs={{0,8},{8,16},{16,24},{24,0},{32,40},{40,48},{48,56},{56,32},{64,72... | collective-permute-start | bytes 1572872 | tf_op jit(solution)/shard_map/ppermute | solution.py:33
  161.8 28.2 %collective-permute-start.18 = (bf16[128,2048]{1,0:T(8,128)(2,1)S(1)}, bf16[128,2048]{1,0:T(8,128)(2,1)S(1)}, u32[]{:S(2)}, u32[]{:S(2)}) collective-permute-start(bf16[128,2048]{1,0:T(8,128)(2,1)S(1)} %get-tuple-element.44), channel_id=1, source_target_pairs={{0,96},{8,104},{16,112},{24,120},{32,0},{40,8},{48,16},{56,24},{64... | collective-permute-start | bytes 1572872 | tf_op jit(solution)/shard_map/ppermute | solution.py:33
  165.2 24.8 %collective-permute-start.19 = (bf16[128,2048]{1,0:T(8,128)(2,1)S(1)}, bf16[128,2048]{1,0:T(8,128)(2,1)S(1)}, u32[]{:S(2)}, u32[]{:S(2)}) collective-permute-start(bf16[128,2048]{1,0:T(8,128)(2,1)S(1)} %get-tuple-element.45), channel_id=1, source_target_pairs={{0,64},{8,72},{16,80},{24,88},{32,96},{40,104},{48,112},{56,120},{... | collective-permute-start | bytes 1572872 | tf_op jit(solution)/shard_map/ppermute | solution.py:33
  168.5 21.5 %collective-permute-start.20 = (bf16[128,2048]{1,0:T(8,128)(2,1)S(1)}, bf16[128,2048]{1,0:T(8,128)(2,1)S(1)}, u32[]{:S(2)}, u32[]{:S(2)}) collective-permute-start(bf16[128,2048]{1,0:T(8,128)(2,1)S(1)} %get-tuple-element.46), channel_id=1, source_target_pairs={{0,32},{8,40},{16,48},{24,56},{32,64},{40,72},{48,80},{56,88},{64,... | collective-permute-start | bytes 1572872 | tf_op jit(solution)/shard_map/ppermute | solution.py:33
  183.6 11.3 %collective-permute-start.27 = (bf16[32,2048]{1,0:T(8,128)(2,1)}, bf16[32,2048]{1,0:T(8,128)(2,1)S(1)}, u32[]{:S(2)}, u32[]{:S(2)}) collective-permute-start(bf16[32,2048]{1,0:T(8,128)(2,1)} %get-tuple-element.56), channel_id=1, source_target_pairs={{0,96},{8,104},{16,112},{24,120},{32,0},{40,8},{48,16},{56,24},{64... | collective-permute-start | bytes 393224 | tf_op jit(solution)/shard_map/ppermute | solution.py:33
  185.1 9.9 %collective-permute-start.28 = (bf16[32,2048]{1,0:T(8,128)(2,1)}, bf16[32,2048]{1,0:T(8,128)(2,1)S(1)}, u32[]{:S(2)}, u32[]{:S(2)}) collective-permute-start(bf16[32,2048]{1,0:T(8,128)(2,1)} %get-tuple-element.57), channel_id=1, source_target_pairs={{0,64},{8,72},{16,80},{24,88},{32,96},{40,104},{48,112},{56,120},{... | collective-permute-start | bytes 393224 | tf_op jit(solution)/shard_map/ppermute | solution.py:33
  189.9 6.7 %collective-permute-start.29 = (bf16[32,2048]{1,0:T(8,128)(2,1)}, bf16[32,2048]{1,0:T(8,128)(2,1)S(1)}, u32[]{:S(2)}, u32[]{:S(2)}) collective-permute-start(bf16[32,2048]{1,0:T(8,128)(2,1)} %get-tuple-element.58), channel_id=1, source_target_pairs={{0,32},{8,40},{16,48},{24,56},{32,64},{40,72},{48,80},{56,88},{64,... | collective-permute-start | bytes 393224 | tf_op jit(solution)/shard_map/ppermute | solution.py:33
  203.2 19.2 %all-to-all-start.2 = ((bf16[8,32,512]{2,1,0:T(8,128)(2,1)}), bf16[8,32,512]{2,1,0:T(8,128)(2,1)S(1)}, u32[]{:S(2)}, u32[]{:S(2)}) async-start(bf16[8,32,512]{2,1,0:T(8,128)(2,1)} %add_last.1), calls=%async_computation.2 | async-start | bytes 524288 | tf_op jit(solution)/shard_map/all_to_all | solution.py:334
  (33 other events, 238.0 us)

commit v3 on v2

--- a/solution.py
+++ b/solution.py
@@ -16,6 +16,10 @@
 SCALE2 = math.log2(math.e) / math.sqrt(HEAD_DIM)
 BF = jnp.bfloat16
 F32 = jnp.float32
+
+
+def room(mib):
+    return pltpu.CompilerParams(vmem_limit_bytes=mib << 20)
 
 
 def ring_pairs(axis, shift):
@@ -33,22 +37,16 @@
     return lax.ppermute(value, "dp", ring_pairs(axis, shift))
 
 
-def attend_kernel(order_ref, q0, q1, q2, q3, kt_ref, v_ref, out_ref, q_scr):
-    step = pl.program_id(0)
-    for k, ref in enumerate((q0, q1, q2, q3)):
-
-        @pl.when(step // 2 == k)
-        def _(ref=ref):
-            q_scr[...] = ref[pl.ds(2 * (step % 2), 2)]
-
+def attend_kernel(q_ref, table_ref, kt_ref, v_ref, out_ref):
     lane = lax.broadcasted_iota(jnp.int32, (64, 128), 1)
     for b in range(2):
-        bias = q_scr[b, :, 512:640]
-        place = order_ref[2 * step + b]
+        leaf = q_ref[b, :, 512:640].astype(F32)
+        leaf_hot = jnp.where(leaf == lane.astype(F32), 1.0, 0.0).astype(BF)
+        bias = jnp.dot(leaf_hot, table_ref[...], preferred_element_type=F32).astype(BF)
         stats = jnp.zeros((64, 128), F32)
         for pair in range(2):
             rows = [
-                jnp.concatenate([q_scr[b, :, 128 * h : 128 * h + 128], bias], axis=1)
+                jnp.concatenate([q_ref[b, :, 128 * h : 128 * h + 128], bias], axis=1)
                 for h in (2 * pair, 2 * pair + 1)
             ]
             q_wide = jnp.concatenate(rows, axis=0)
@@ -60,45 +58,71 @@
             for k in range(2):
                 h = 2 * pair + k
                 part = both[64 * k : 64 * k + 64]
-                out_ref[place, :, 128 * h : 128 * h + 128] = part[:, :128].astype(BF)
+                out_ref[b, :, 128 * h : 128 * h + 128] = part[:, :128].astype(BF)
                 total = part[:, 128:256]
                 high = total.astype(BF).astype(F32)
                 stats = jnp.where(lane == h, top[64 * k : 64 * k + 64], stats)
                 stats = jnp.where(lane == 4 + h, high, stats)
                 stats = jnp.where(lane == 8 + h, total - high, stats)
-        out_ref[place, :, 512:640] = stats.astype(BF)
-
-
-def attend(order, blocks, kt_wide, v_wide):
-    whole = lambda shape: pl.BlockSpec(shape, lambda g, order: tuple(0 for _ in shape))
+        out_ref[b, :, 512:640] = stats.astype(BF)
+
+
+def attend(group, table, kt_wide, v_wide):
+    whole = lambda shape: pl.BlockSpec(
+        shape, lambda g: tuple(0 for _ in shape), pipeline_mode=pl.Buffered(1)
+    )
+    pair = pl.BlockSpec((2, 64, 640), lambda g: (g, 0, 0))
     return pl.pallas_call(
         attend_kernel,
-        out_shape=jax.ShapeDtypeStruct((16, 64, 640), BF),
-        grid_spec=pltpu.PrefetchScalarGridSpec(
-            num_scalar_prefetch=1,
-            grid=(8,),
-            in_specs=[whole((4, 64, 640)) for _ in range(4)]
-            + [whole(kt_wide.shape), whole(v_wide.shape)],
-            out_specs=whole((16, 64, 640)),
-            scratch_shapes=[pltpu.VMEM((2, 64, 640), BF)],
-        ),
-        compiler_params=pltpu.CompilerParams(vmem_limit_bytes=40 << 20),
+        out_shape=jax.ShapeDtypeStruct((4, 64, 640), BF),
+        grid=(2,),
+        in_specs=[pair, whole(table.shape), whole(kt_wide.shape), whole(v_wide.shape)],
+        out_specs=pair,
+        compiler_params=room(16),
         name="attend",
-    )(order, *blocks, kt_wide, v_wide)
-
-
-def combine_kernel(got_ref, res_ref, disp_ref, att_ref, stream_ref, slot_ref):
-    stats = got_ref[:, :, 512:640].astype(F32)
-    top = jnp.max(stats, axis=0)
-    factor = jnp.exp2(stats - top[None])
+    )(group, table, kt_wide, v_wide)
+
+
+def merged(refs, pick):
+    stats = [r[pick + (slice(512, 640),)].astype(F32) for r in refs]
+    top = jnp.maximum(jnp.maximum(stats[0], stats[1]), jnp.maximum(stats[2], stats[3]))
+    factor = [jnp.exp2(s - top) for s in stats]
     for h in range(4):
-        weight = factor[:, :, h : h + 1]
-        total = stats[:, :, 4 + h : 5 + h] + stats[:, :, 8 + h : 9 + h]
-        part = got_ref[:, :, 128 * h : 128 * h + 128].astype(F32)
-        upper = jnp.sum(part * weight, axis=0)
-        lower = jnp.sum(total * weight, axis=0)
+        cols = slice(128 * h, 128 * h + 128)
+        upper = 0.0
+        lower = 0.0
+        for r, s, f in zip(refs, stats, factor):
+            weight = f[:, h : h + 1]
+            upper = upper + r[pick + (cols,)].astype(F32) * weight
+            lower = lower + (s[:, 4 + h : 5 + h] + s[:, 8 + h : 9 + h]) * weight
+        yield h, cols, top[:, h : h + 1], upper, lower
+
+
+def merge_kernel(a, b, c, d, o0, o1, o2, o3):
+    lane = lax.broadcasted_iota(jnp.int32, (64, 128), 1)
+    for k, ref in enumerate((o0, o1, o2, o3)):
+        stats = jnp.zeros((64, 128), F32)
+        for h, cols, top, upper, lower in merged((a, b, c, d), (k, slice(None))):
+            ref[:, cols] = upper.astype(BF)
+            high = lower.astype(BF).astype(F32)
+            stats = jnp.where(lane == h, top, stats)
+            stats = jnp.where(lane == 4 + h, high, stats)
+            stats = jnp.where(lane == 8 + h, lower - high, stats)
+        ref[:, 512:640] = stats.astype(BF)
+
+
+def merge(parts):
+    return pl.pallas_call(
+        merge_kernel,
+        out_shape=[jax.ShapeDtypeStruct((64, 640), BF)] * 4,
+        compiler_params=room(8),
+        name="merge",
+    )(*parts)
+
+
+def combine_kernel(a, b, c, d, res_ref, disp_ref, att_ref, stream_ref, slot_ref):
+    for h, cols, top, upper, lower in merged((a, b, c, d), (slice(None),)):
         att = upper / lower
-        cols = slice(128 * h, 128 * h + 128)
         att_ref[:, cols] = att.astype(BF)
         stream_ref[:, cols] = (res_ref[:, cols].astype(F32) + att).astype(BF)
     slot_ref[...] = jnp.dot(
@@ -106,7 +130,7 @@
     ).astype(BF)
 
 
-def combine(got, residual, disp):
+def combine(parts, residual, disp):
     return pl.pallas_call(
         combine_kernel,
         out_shape=(
@@ -114,8 +138,9 @@
             jax.ShapeDtypeStruct((64, 512), BF),
             jax.ShapeDtypeStruct((256, 512), BF),
         ),
+        compiler_params=room(8),
         name="combine",
-    )(got, residual, disp)
+    )(*parts, residual, disp)
 
 
 def norm_kernel(x_ref, gain_ref, low_ref, high_ref):
@@ -136,6 +161,7 @@
     return pl.pallas_call(
         norm_kernel,
         out_shape=(jax.ShapeDtypeStruct((32, 2048), BF), jax.ShapeDtypeStruct((32, 2048), BF)),
+        compiler_params=room(4),
         name="norm",
     )(x, gain)
 
@@ -168,7 +194,7 @@
         in_specs=[part] * 8 + [tile, tile],
         out_specs=pl.BlockSpec((512, 128), lambda i: (0, i)),
         scratch_shapes=[pltpu.VMEM((512, 4096), BF)],
-        compiler_params=pltpu.CompilerParams(vmem_limit_bytes=40 << 20),
+        compiler_params=room(20),
         name="hidden_units",
     )(*low, *high, w_gate, w_up)
 
@@ -199,7 +225,7 @@
         ],
         out_specs=[pl.BlockSpec((128, 512), lambda i: (0, i))] * 4,
         scratch_shapes=[pltpu.VMEM((512, 896), BF)],
-        compiler_params=pltpu.CompilerParams(vmem_limit_bytes=40 << 20),
+        compiler_params=room(12),
         name="down_high" if swap else "down_low",
     )(hidden, w_down)
 
@@ -217,6 +243,7 @@
         grid=(2,),
         in_specs=[pl.BlockSpec((128, 1024), lambda i: (0, i))] * 4,
         out_specs=[pl.BlockSpec((32, 1024), lambda i: (0, i))] * 4,
+        compiler_params=room(8),
         name="add_first",
     )(*parts)
 
@@ -238,7 +265,10 @@
 
 def add_last(low, high):
     return pl.pallas_call(
-        last_kernel, out_shape=jax.ShapeDtypeStruct((8, 32, 512), BF), name="add_last"
+        last_kernel,
+        out_shape=jax.ShapeDtypeStruct((8, 32, 512), BF),
+        compiler_params=room(8),
+        name="add_last",
     )(*low, *high)
 
 
@@ -261,7 +291,10 @@
 
 def finish(mix, y, stream):
     return pl.pallas_call(
-        finish_kernel, out_shape=jax.ShapeDtypeStruct((64, 512), BF), name="finish"
+        finish_kernel,
+        out_shape=jax.ShapeDtypeStruct((64, 512), BF),
+        compiler_params=room(4),
+        name="finish",
     )(mix, y, stream)
 
 
@@ -282,20 +315,21 @@
 ):
     rows = queries.shape[0]
     node_count = parent.shape[0]
+    leaf_wide = jnp.broadcast_to(leaf_ids.astype(BF)[:, None], (rows, 128))
+    q_own = jnp.concatenate([queries, leaf_wide], axis=1)
+    near = jnp.stack(spread_near(q_own, 1))
+    groups = spread_far(near, 0)
+
     lane = jnp.arange(128, dtype=jnp.int32)
-    leaf_hot = leaf_ids[:, None] == jnp.arange(node_count, dtype=jnp.int32)[None, :]
-    middle = jnp.sum(jnp.where(leaf_hot, parent[None, :], 0), axis=1)
-    middle_hot = middle[:, None] == jnp.arange(node_count, dtype=jnp.int32)[None, :]
+    node = jnp.arange(node_count, dtype=jnp.int32)
+    middle_hot = parent[:, None] == node[None, :]
     upper = jnp.sum(jnp.where(middle_hot, parent[None, :], 0), axis=1)
     seen = (
-        (lane[None, :] == leaf_ids[:, None])
-        | (lane[None, :] == middle[:, None])
+        (lane[None, :] == node[:, None])
+        | (lane[None, :] == parent[:, None])
         | (lane[None, :] == upper[:, None])
     )
-    bias = jnp.where(seen, 0.0, HIDE).astype(BF)
-    q_own = jnp.concatenate([queries, bias], axis=1)[None]
-    stage = jnp.concatenate([q_own] + [shift_dp(q_own, 1, s) for s in (1, 2, 3)], axis=0)
-    blocks = [stage] + [shift_dp(stage, 0, s) for s in (1, 2, 3)]
+    table = jnp.pad(jnp.where(seen, 0.0, HIDE).astype(BF), ((0, 128 - node_count), (0, 0)))
 
     kt_hot = (
         jnp.where(node_of_position < 0, 127, node_of_position)[None, :] == lane[:, None]
@@ -316,12 +350,12 @@
     place_t = named[:, :, None] & (rank[:, :, None] == slot[None, None, :])
     mix = jnp.where(place_t, weight[:, :, None], 0.0).reshape(rows, EXPERTS * CAP).astype(BF)
 
-    me = lax.axis_index("dp")
-    rel = jnp.arange(16, dtype=jnp.int32)
-    order = ((me // 4 - rel // 4) % 4) * 4 + (me % 4 - rel % 4) % 4
-    partial = attend(order, blocks, kt_wide, v_wide)
-    got = lax.all_to_all(partial, "dp", split_axis=0, concat_axis=0, tiled=True)
-    attention_out, stream, slots = combine(got, residual, disp)
+    partial = [attend(groups[0], table, kt_wide, v_wide), None, None, None]
+    partial[0], *groups[1:] = lax.optimization_barrier((partial[0], *groups[1:]))
+    for turn in (1, 3, 2):
+        partial[turn] = attend(groups[turn], table, kt_wide, v_wide)
+    parts = collect(merge(collect(partial, 0)), 1)
+    attention_out, stream, slots = combine(parts, residual, disp)
 
     mine = lax.all_to_all(slots.reshape(8, 32, 512), "expert", split_axis=0, concat_axis=0, tiled=True)
     low, high = norm(mine, norm_gain[None, :])

time: 226 us -> 204 us (0.903)
  waiting for transfers between devices: 84.3 us -> 75.1 us
  Pallas kernels: 51.1 us -> 42.4 us
  local copies, waits for them, and re-layouts: 12.2 us -> 7.06 us
  starting transfers between devices: 68.5 us -> 73.3 us
  other arithmetic: 7.6 us -> 4.49 us
    all_to_all x1 -> x0, waiting for transfers between devices: 16.8 us -> none  [body(): got = lax.all_to_all(partial, 'dp', split_axis=0, concat_axis=0, tiled=True)]
    ppermute x30 -> x36, starting transfers between devices: 40 us -> 50.9 us  [shift_dp(): return lax.ppermute(value, 'dp', ring_pairs(axis, shift))]
    all_to_all x1 -> x0, starting transfers between devices: 6.6 us -> none  [body(): got = lax.all_to_all(partial, 'dp', split_axis=0, concat_axis=0, tiled=True)]
    ppermute x30 -> x36, waiting for transfers between devices: 56.1 us -> 62.5 us  [shift_dp(): return lax.ppermute(value, 'dp', ring_pairs(axis, shift))]
    unnamed x49 -> x21, local copies, waits for them, and re-layouts: 11.1 us -> 6.46 us
    pallas_call x2, Pallas kernels: 4.61 us -> 0.99 us  [add_first(): pl.pallas_call(add_kernel, out_shape=[jax.ShapeDtypeStruct((32, 2048), BF...]
    pallas_call x1 -> x5, Pallas kernels: 19.2 us -> 19.7 us  [the longest x4 18 us: attend(): pl.pallas_call(attend_kernel, out_shape=jax.ShapeDtypeStruct((4, 64, 640)...]
  transfers between devices with their start and end apart: 33 -> 38, of which waited for: 21 -> 21; matrix products, arithmetic and copies ran while one was open for 3% -> 2% of each run, Pallas kernels for 4% -> 9%
where the time goes in v3:
time: 204 us
  waiting for transfers between devices  75.1 us (37%)
  starting transfers between devices  73.3 us (36%)
  Pallas kernels  42.4 us (21%)
  local copies, waits for them, and re-layouts  7.06 us (3%)
  other arithmetic  4.49 us (2%)
    ppermute x36, waiting for transfers between devices, shift_dp(): return lax.ppermute(value, 'dp', ring_pairs(axis, shift))  62.5 us
    ppermute x36, starting transfers between devices, shift_dp(): return lax.ppermute(value, 'dp', ring_pairs(axis, shift))  50.9 us
    pallas_call x4, Pallas kernels, attend(): pl.pallas_call(attend_kernel, out_shape=jax.ShapeDtypeStruct((4, 64, 640)...  18 us
    all_to_all x1, starting transfers between devices, body(): lax.all_to_all(summed, 'expert', split_axis=0, concat_axis=0, tiled=True)  14.1 us
    pallas_call x1, Pallas kernels, hidden_units(): pl.pallas_call(hidden_kernel, out_shape=jax.ShapeDtypeStruct((512, 896),...  11.9 us
    all_to_all x1, starting transfers between devices, body(): lax.all_to_all(slots.reshape(8, 32, 512), 'expert', split_axis=0, concat_...  8.4 us
    pallas_call x2, Pallas kernels, down(): pl.pallas_call(functools.partial(down_kernel, swap), out_shape=[jax.Shape...  6.76 us
    all_to_all x1, waiting for transfers between devices, body(): lax.all_to_all(slots.reshape(8, 32, 512), 'expert', split_axis=0, concat_...  6.49 us
  transfers between devices with their start and end apart: 38, of which 21 were waited for; matrix products, arithmetic and copies ran while one was open for 2% of the time, Pallas kernels for 9%

profile of v3, /device:TPU:1, one launch (start us, length us, event | category | flops | bytes accessed | tf_op | source)
XLA Modules:
  0.0 203.6 jit_solution(10704260024810852576)
XLA Ops:
  16.2 4.5 %attend.4.a = bf16[4,64,640]{2,1,0:T(8,128)(2,1)S(1)} custom-call(bf16[4,64,640]{2,1,0:T(8,128)(2,1)S(1)} %pad_maximum_fusion.3.q_ref, bf16[128,128]{1,0:T(8,128)(2,1)S(1)} %pad.5.table_ref, bf16[256,2304]{1,0:T(8,128)(2,1)S(1)} %pad_maximum_fusion.kt_ref, bf16[2304,256]{1,0:T(8,128)(2,1)S(1)} %concatenate.11.v_ref), custom_call_target="tpu_custom_call" | custom-call | tf_op jit(solution)/shard_map/attend/pallas_call | solution.py:75
  20.7 7.3 %collective-permute-done.4.q_ref = bf16[4,64,640]{2,1,0:T(8,128)(2,1)S(1)} collective-permute-done((bf16[4,64,640]{2,1,0:T(8,128)(2,1)S(1)}, bf16[4,64,640]{2,1,0:T(8,128)(2,1)S(1)}, u32[]{:S(2)}, u32[]{:S(2)}) %collective-permute-start.4) | collective-permute-done | bytes 327712 | tf_op jit(solution)/shard_map/ppermute | solution.py:37
  28.7 4.5 %attend.7 = bf16[4,64,640]{2,1,0:T(8,128)(2,1)S(1)} custom-call(bf16[4,64,640]{2,1,0:T(8,128)(2,1)S(1)} %collective-permute-done.5.q_ref, bf16[128,128]{1,0:T(8,128)(2,1)S(1)} %pad.5.table_ref, bf16[256,2304]{1,0:T(8,128)(2,1)S(1)} %pad_maximum_fusion.kt_ref, bf16[2304,256]{1,0:T(8,128)(2,1)S(1)} %concatenate.11.v_ref), custom_call_target="tpu_custom_call" | custom-call | tf_op jit(solution)/shard_map/attend/pallas_call | solution.py:75
  35.0 4.5 %attend.6 = bf16[4,64,640]{2,1,0:T(8,128)(2,1)S(1)} custom-call(bf16[4,64,640]{2,1,0:T(8,128)(2,1)S(1)} %collective-permute-done.4.q_ref, bf16[128,128]{1,0:T(8,128)(2,1)S(1)} %pad.5.table_ref, bf16[256,2304]{1,0:T(8,128)(2,1)S(1)} %pad_maximum_fusion.kt_ref, bf16[2304,256]{1,0:T(8,128)(2,1)S(1)} %concatenate.11.v_ref), custom_call_target="tpu_custom_call" | custom-call | tf_op jit(solution)/shard_map/attend/pallas_call | solution.py:75
  39.5 2.9 %collective-permute-start.7 = (bf16[4,64,640]{2,1,0:T(8,128)(2,1)S(1)}, bf16[4,64,640]{2,1,0:T(8,128)(2,1)S(1)}, u32[]{:S(2)}, u32[]{:S(2)}) collective-permute-start(bf16[4,64,640]{2,1,0:T(8,128)(2,1)S(1)} %attend.6), channel_id=1, source_target_pairs={{0,64},{8,72},{16,80},{24,88},{32,96},{40,104},{48,112},{56,120},{... | collective-permute-start | bytes 983048 | tf_op jit(solution)/shard_map/ppermute | solution.py:37
  42.4 4.5 %attend.5 = bf16[4,64,640]{2,1,0:T(8,128)(2,1)S(1)} custom-call(bf16[4,64,640]{2,1,0:T(8,128)(2,1)S(1)} %collective-permute-done.3.q_ref, bf16[128,128]{1,0:T(8,128)(2,1)S(1)} %pad.5.table_ref, bf16[256,2304]{1,0:T(8,128)(2,1)S(1)} %pad_maximum_fusion.kt_ref, bf16[2304,256]{1,0:T(8,128)(2,1)S(1)} %concatenate.11.v_ref), custom_call_target="tpu_custom_call" | custom-call | tf_op jit(solution)/shard_map/attend/pallas_call | solution.py:75
  47.2 4.9 %collective-permute-done.7.c = bf16[4,64,640]{2,1,0:T(8,128)(2,1)S(1)} collective-permute-done((bf16[4,64,640]{2,1,0:T(8,128)(2,1)S(1)}, bf16[4,64,640]{2,1,0:T(8,128)(2,1)S(1)}, u32[]{:S(2)}, u32[]{:S(2)}) %collective-permute-start.7) | collective-permute-done | bytes 327712 | tf_op jit(solution)/shard_map/ppermute | solution.py:37
  52.2 3.6 %collective-permute-done.6.b = bf16[4,64,640]{2,1,0:T(8,128)(2,1)S(1)} collective-permute-done((bf16[4,64,640]{2,1,0:T(8,128)(2,1)S(1)}, bf16[4,64,640]{2,1,0:T(8,128)(2,1)S(1)}, u32[]{:S(2)}, u32[]{:S(2)}) %collective-permute-start.6) | collective-permute-done | bytes 327712 | tf_op jit(solution)/shard_map/ppermute | solution.py:37
  64.6 8.4 %all-to-all-start = ((bf16[8,32,512]{2,1,0:T(8,128)(2,1)}), bf16[8,32,512]{2,1,0:T(8,128)(2,1)S(1)}, u32[]{:S(2)}, u32[]{:S(2)}) async-start(bf16[8,32,512]{2,1,0:T(8,128)(2,1)} %bitcast.12), calls=%async_computation | async-start | bytes 524288 | tf_op jit(solution)/shard_map/all_to_all | solution.py:360
  73.0 6.5 %all-to-all-done.x_ref = bf16[8,32,512]{2,1,0:T(8,128)(2,1)S(1)} async-done(((bf16[8,32,512]{2,1,0:T(8,128)(2,1)}), bf16[8,32,512]{2,1,0:T(8,128)(2,1)S(1)}, u32[]{:S(2)}, u32[]{:S(2)}) %all-to-all-start) | async-done | bytes 262176 | tf_op jit(solution)/shard_map/all_to_all | solution.py:360
  80.4 3.2 %collective-permute-start.13 = (bf16[32,2048]{1,0:T(8,128)(2,1)S(1)}, bf16[32,2048]{1,0:T(8,128)(2,1)S(1)}, u32[]{:S(2)}, u32[]{:S(2)}) collective-permute-start(bf16[32,2048]{1,0:T(8,128)(2,1)S(1)} %get-tuple-element.51), channel_id=1, source_target_pairs={{0,16},{8,24},{16,0},{24,8},{32,48},{40,56},{48,32},{56,40},{64,80... | collective-permute-start | bytes 393224 | tf_op jit(solution)/shard_map/ppermute | solution.py:37
  98.9 6.2 %collective-permute-done.21.refs_5_ = bf16[4,32,2048]{2,1,0:T(8,128)(2,1)S(1)} collective-permute-done((bf16[4,32,2048]{2,1,0:T(8,128)(2,1)S(1)}, bf16[4,32,2048]{2,1,0:T(8,128)(2,1)S(1)}, u32[]{:S(2)}, u32[]{:S(2)}) %collective-permute-start.21) | collective-permute-done | bytes 524320 | tf_op jit(solution)/shard_map/ppermute | solution.py:37
  105.8 8.6 %collective-permute-done.22.refs_6_ = bf16[4,32,2048]{2,1,0:T(8,128)(2,1)S(1)} collective-permute-done((bf16[4,32,2048]{2,1,0:T(8,128)(2,1)S(1)}, bf16[4,32,2048]{2,1,0:T(8,128)(2,1)S(1)}, u32[]{:S(2)}, u32[]{:S(2)}) %collective-permute-start.22) | collective-permute-done | bytes 524320 | tf_op jit(solution)/shard_map/ppermute | solution.py:37
  114.5 3.6 %collective-permute-done.23.refs_7_ = bf16[4,32,2048]{2,1,0:T(8,128)(2,1)S(1)} collective-permute-done((bf16[4,32,2048]{2,1,0:T(8,128)(2,1)S(1)}, bf16[4,32,2048]{2,1,0:T(8,128)(2,1)S(1)}, u32[]{:S(2)}, u32[]{:S(2)}) %collective-permute-start.23) | collective-permute-done | bytes 524320 | tf_op jit(solution)/shard_map/ppermute | solution.py:37
  118.1 3.1 %copy-done = bf16[1,4096,896]{2,1,0:T(8,128)(2,1)S(1)} copy-done((bf16[1,4096,896]{2,1,0:T(8,128)(2,1)S(1)}, bf16[1,4096,896]{2,1,0:T(8,128)(2,1)}, u32[]{:S(2)}) %copy-start) | copy-done | bytes 7340056
  121.2 3.1 %copy-done.1 = bf16[1,4096,896]{2,1,0:T(8,128)(2,1)S(1)} copy-done((bf16[1,4096,896]{2,1,0:T(8,128)(2,1)S(1)}, bf16[1,4096,896]{2,1,0:T(8,128)(2,1)}, u32[]{:S(2)}) %copy-start.1) | copy-done | bytes 7340056
  124.3 11.9 %hidden_units.1.h_ref = bf16[512,896]{1,0:T(8,128)(2,1)S(1)} custom-call(bf16[4,32,2048]{2,1,0:T(8,128)(2,1)S(1)} %pad_maximum_fusion.1.refs_0_, bf16[4,32,2048]{2,1,0:T(8,128)(2,1)S(1)} %collective-permute-done.18.refs_1_, bf16[4,32,2048]{2,1,0:T(8,128)(2,1)S(1)} %collective-permute-done.19.refs_2_, ...), custom_call_target="tpu_custom_call" | custom-call | tf_op jit(solution)/shard_map/hidden_units/pallas_call | solution.py:190
  136.2 3.4 %down_high.1 = (bf16[128,2048]{1,0:T(8,128)(2,1)S(1)}, bf16[128,2048]{1,0:T(8,128)(2,1)S(1)}, bf16[128,2048]{1,0:T(8,128)(2,1)S(1)}, bf16[128,2048]{1,0:T(8,128)(2,1)S(1)}) custom-call(bf16[512,896]{1,0:T(8,128)(2,1)S(1)} %hidden_units.1.h_ref, bf16[1,896,4096]{2,1,0:T(8,128)(2,1)S(1)} %bitcast.31), custom_call_target="tpu_custom_call" | custom-call | tf_op jit(solution)/shard_map/down_high/pallas_call | solution.py:218
  139.6 3.4 %collective-permute-start.30 = (bf16[128,2048]{1,0:T(8,128)(2,1)S(1)}, bf16[128,2048]{1,0:T(8,128)(2,1)S(1)}, u32[]{:S(2)}, u32[]{:S(2)}) collective-permute-start(bf16[128,2048]{1,0:T(8,128)(2,1)S(1)} %get-tuple-element.68), channel_id=1, source_target_pairs={{0,24},{8,0},{16,8},{24,16},{32,56},{40,32},{48,40},{56,48},{64,88... | collective-permute-start | bytes 1572872 | tf_op jit(solution)/shard_map/ppermute | solution.py:37
  143.7 3.4 %down_low.1 = (bf16[128,2048]{1,0:T(8,128)(2,1)S(1)}, bf16[128,2048]{1,0:T(8,128)(2,1)S(1)}, bf16[128,2048]{1,0:T(8,128)(2,1)S(1)}, bf16[128,2048]{1,0:T(8,128)(2,1)S(1)}) custom-call(bf16[512,896]{1,0:T(8,128)(2,1)S(1)} %hidden_units.1.h_ref, bf16[1,896,4096]{2,1,0:T(8,128)(2,1)S(1)} %bitcast.31), custom_call_target="tpu_custom_call" | custom-call | tf_op jit(solution)/shard_map/down_low/pallas_call | solution.py:218
  150.9 5.3 %collective-permute-done.30.b = bf16[128,2048]{1,0:T(8,128)(2,1)S(1)} collective-permute-done((bf16[128,2048]{1,0:T(8,128)(2,1)S(1)}, bf16[128,2048]{1,0:T(8,128)(2,1)S(1)}, u32[]{:S(2)}, u32[]{:S(2)}) %collective-permute-start.30) | collective-permute-done | bytes 524320 | tf_op jit(solution)/shard_map/ppermute | solution.py:37
  156.2 11.2 %collective-permute-done.32.d = bf16[128,2048]{1,0:T(8,128)(2,1)S(1)} collective-permute-done((bf16[128,2048]{1,0:T(8,128)(2,1)S(1)}, bf16[128,2048]{1,0:T(8,128)(2,1)S(1)}, u32[]{:S(2)}, u32[]{:S(2)}) %collective-permute-start.32) | collective-permute-done | bytes 524320 | tf_op jit(solution)/shard_map/ppermute | solution.py:37
  182.2 14.1 %all-to-all-start.1 = ((bf16[8,32,512]{2,1,0:T(8,128)(2,1)}), bf16[8,32,512]{2,1,0:T(8,128)(2,1)S(1)}, u32[]{:S(2)}, u32[]{:S(2)}) async-start(bf16[8,32,512]{2,1,0:T(8,128)(2,1)} %add_last.1), calls=%async_computation.1 | async-start | bytes 524288 | tf_op jit(solution)/shard_map/all_to_all | solution.py:368
  196.6 6.1 %all-to-all-done.1 = bf16[8,32,512]{2,1,0:T(8,128)(2,1)S(1)} async-done(((bf16[8,32,512]{2,1,0:T(8,128)(2,1)}), bf16[8,32,512]{2,1,0:T(8,128)(2,1)S(1)}, u32[]{:S(2)}, u32[]{:S(2)}) %all-to-all-start.1) | async-done | bytes 262176 | tf_op jit(solution)/shard_map/all_to_all | solution.py:368
  (116 shorter events, 64.4 us)
Async XLA Ops:
  2.3 8.8 %collective-permute-start = (bf16[64,640]{1,0:T(8,128)(2,1)S(1)}, bf16[64,640]{1,0:T(8,128)(2,1)S(1)}, u32[]{:S(2)}, u32[]{:S(2)}) collective-permute-start(bf16[64,640]{1,0:T(8,128)(2,1)S(1)} %get-tuple-element.77), channel_id=1, source_target_pairs={{0,8},{8,16},{16,24},{24,0},{32,40},{40,48},{48,56},{56,32},{64,72... | collective-permute-start | bytes 245768 | tf_op jit(solution)/shard_map/ppermute | solution.py:37
  11.2 9.5 %collective-permute-start.3 = (bf16[4,64,640]{2,1,0:T(8,128)(2,1)S(1)}, bf16[4,64,640]{2,1,0:T(8,128)(2,1)S(1)}, u32[]{:S(2)}, u32[]{:S(2)}) collective-permute-start(bf16[4,64,640]{2,1,0:T(8,128)(2,1)S(1)} %pad_maximum_fusion.3.q_ref), channel_id=1, source_target_pairs={{0,32},{8,40},{16,48},{24,56},{32,64},{40,72},{48,80},{56,88},{64,... | collective-permute-start | bytes 983048 | tf_op jit(solution)/shard_map/ppermute | solution.py:37
  12.5 15.5 %collective-permute-start.4 = (bf16[4,64,640]{2,1,0:T(8,128)(2,1)S(1)}, bf16[4,64,640]{2,1,0:T(8,128)(2,1)S(1)}, u32[]{:S(2)}, u32[]{:S(2)}) collective-permute-start(bf16[4,64,640]{2,1,0:T(8,128)(2,1)S(1)} %pad_maximum_fusion.3.q_ref), channel_id=1, source_target_pairs={{0,64},{8,72},{16,80},{24,88},{32,96},{40,104},{48,112},{56,120},{... | collective-permute-start | bytes 983048 | tf_op jit(solution)/shard_map/ppermute | solution.py:37
  14.9 13.8 %collective-permute-start.5 = (bf16[4,64,640]{2,1,0:T(8,128)(2,1)S(1)}, bf16[4,64,640]{2,1,0:T(8,128)(2,1)S(1)}, u32[]{:S(2)}, u32[]{:S(2)}) collective-permute-start(bf16[4,64,640]{2,1,0:T(8,128)(2,1)S(1)} %pad_maximum_fusion.3.q_ref), channel_id=1, source_target_pairs={{0,96},{8,104},{16,112},{24,120},{32,0},{40,8},{48,16},{56,24},{64... | collective-permute-start | bytes 983048 | tf_op jit(solution)/shard_map/ppermute | solution.py:37
  33.2 14.0 %collective-permute-start.8 = (bf16[4,64,640]{2,1,0:T(8,128)(2,1)S(1)}, bf16[4,64,640]{2,1,0:T(8,128)(2,1)S(1)}, u32[]{:S(2)}, u32[]{:S(2)}) collective-permute-start(bf16[4,64,640]{2,1,0:T(8,128)(2,1)S(1)} %attend.7), channel_id=1, source_target_pairs={{0,32},{8,40},{16,48},{24,56},{32,64},{40,72},{48,80},{56,88},{64,... | collective-permute-start | bytes 983048 | tf_op jit(solution)/shard_map/ppermute | solution.py:37
  39.5 12.7 %collective-permute-start.7 = (bf16[4,64,640]{2,1,0:T(8,128)(2,1)S(1)}, bf16[4,64,640]{2,1,0:T(8,128)(2,1)S(1)}, u32[]{:S(2)}, u32[]{:S(2)}) collective-permute-start(bf16[4,64,640]{2,1,0:T(8,128)(2,1)S(1)} %attend.6), channel_id=1, source_target_pairs={{0,64},{8,72},{16,80},{24,88},{32,96},{40,104},{48,112},{56,120},{... | collective-permute-start | bytes 983048 | tf_op jit(solution)/shard_map/ppermute | solution.py:37
  46.9 8.9 %collective-permute-start.6 = (bf16[4,64,640]{2,1,0:T(8,128)(2,1)S(1)}, bf16[4,64,640]{2,1,0:T(8,128)(2,1)S(1)}, u32[]{:S(2)}, u32[]{:S(2)}) collective-permute-start(bf16[4,64,640]{2,1,0:T(8,128)(2,1)S(1)} %attend.5), channel_id=1, source_target_pairs={{0,96},{8,104},{16,112},{24,120},{32,0},{40,8},{48,16},{56,24},{64... | collective-permute-start | bytes 983048 | tf_op jit(solution)/shard_map/ppermute | solution.py:37
  64.6 14.9 %all-to-all-start = ((bf16[8,32,512]{2,1,0:T(8,128)(2,1)}), bf16[8,32,512]{2,1,0:T(8,128)(2,1)S(1)}, u32[]{:S(2)}, u32[]{:S(2)}) async-start(bf16[8,32,512]{2,1,0:T(8,128)(2,1)} %bitcast.12), calls=%async_computation | async-start | bytes 524288 | tf_op jit(solution)/shard_map/all_to_all | solution.py:360
  80.4 8.2 %collective-permute-start.13 = (bf16[32,2048]{1,0:T(8,128)(2,1)S(1)}, bf16[32,2048]{1,0:T(8,128)(2,1)S(1)}, u32[]{:S(2)}, u32[]{:S(2)}) collective-permute-start(bf16[32,2048]{1,0:T(8,128)(2,1)S(1)} %get-tuple-element.51), channel_id=1, source_target_pairs={{0,16},{8,24},{16,0},{24,8},{32,48},{40,56},{48,32},{56,40},{64,80... | collective-permute-start | bytes 393224 | tf_op jit(solution)/shard_map/ppermute | solution.py:37
  92.1 12.9 %collective-permute-start.21 = (bf16[4,32,2048]{2,1,0:T(8,128)(2,1)S(1)}, bf16[4,32,2048]{2,1,0:T(8,128)(2,1)S(1)}, u32[]{:S(2)}, u32[]{:S(2)}) collective-permute-start(bf16[4,32,2048]{2,1,0:T(8,128)(2,1)S(1)} %pad_maximum_fusion.2.refs_4_), channel_id=1, source_target_pairs={{0,8},{8,16},{16,24},{24,0},{32,40},{40,48},{48,56},{56,32},{64,72... | collective-permute-start | bytes 1572872 | tf_op jit(solution)/shard_map/ppermute | solution.py:37
  93.5 21.0 %collective-permute-start.22 = (bf16[4,32,2048]{2,1,0:T(8,128)(2,1)S(1)}, bf16[4,32,2048]{2,1,0:T(8,128)(2,1)S(1)}, u32[]{:S(2)}, u32[]{:S(2)}) collective-permute-start(bf16[4,32,2048]{2,1,0:T(8,128)(2,1)S(1)} %pad_maximum_fusion.2.refs_4_), channel_id=1, source_target_pairs={{0,16},{8,24},{16,0},{24,8},{32,48},{40,56},{48,32},{56,40},{64,80... | collective-permute-start | bytes 1572872 | tf_op jit(solution)/shard_map/ppermute | solution.py:37
  93.7 24.3 %collective-permute-start.23 = (bf16[4,32,2048]{2,1,0:T(8,128)(2,1)S(1)}, bf16[4,32,2048]{2,1,0:T(8,128)(2,1)S(1)}, u32[]{:S(2)}, u32[]{:S(2)}) collective-permute-start(bf16[4,32,2048]{2,1,0:T(8,128)(2,1)S(1)} %pad_maximum_fusion.2.refs_4_), channel_id=1, source_target_pairs={{0,24},{8,0},{16,8},{24,16},{32,56},{40,32},{48,40},{56,48},{64,88... | collective-permute-start | bytes 1572872 | tf_op jit(solution)/shard_map/ppermute | solution.py:37
  96.0 22.0 %collective-permute-start.18 = (bf16[4,32,2048]{2,1,0:T(8,128)(2,1)S(1)}, bf16[4,32,2048]{2,1,0:T(8,128)(2,1)S(1)}, u32[]{:S(2)}, u32[]{:S(2)}) collective-permute-start(bf16[4,32,2048]{2,1,0:T(8,128)(2,1)S(1)} %pad_maximum_fusion.1.refs_0_), channel_id=1, source_target_pairs={{0,32},{8,40},{16,48},{24,56},{32,64},{40,72},{48,80},{56,88},{64,... | collective-permute-start | bytes 1572872 | tf_op jit(solution)/shard_map/ppermute | solution.py:37
  96.4 21.7 %collective-permute-start.19 = (bf16[4,32,2048]{2,1,0:T(8,128)(2,1)S(1)}, bf16[4,32,2048]{2,1,0:T(8,128)(2,1)S(1)}, u32[]{:S(2)}, u32[]{:S(2)}) collective-permute-start(bf16[4,32,2048]{2,1,0:T(8,128)(2,1)S(1)} %pad_maximum_fusion.1.refs_0_), channel_id=1, source_target_pairs={{0,64},{8,72},{16,80},{24,88},{32,96},{40,104},{48,112},{56,120},{... | collective-permute-start | bytes 1572872 | tf_op jit(solution)/shard_map/ppermute | solution.py:37
  105.1 13.1 %collective-permute-start.20 = (bf16[4,32,2048]{2,1,0:T(8,128)(2,1)S(1)}, bf16[4,32,2048]{2,1,0:T(8,128)(2,1)S(1)}, u32[]{:S(2)}, u32[]{:S(2)}) collective-permute-start(bf16[4,32,2048]{2,1,0:T(8,128)(2,1)S(1)} %pad_maximum_fusion.1.refs_0_), channel_id=1, source_target_pairs={{0,96},{8,104},{16,112},{24,120},{32,0},{40,8},{48,16},{56,24},{64... | collective-permute-start | bytes 1572872 | tf_op jit(solution)/shard_map/ppermute | solution.py:37
  139.6 16.6 %collective-permute-start.30 = (bf16[128,2048]{1,0:T(8,128)(2,1)S(1)}, bf16[128,2048]{1,0:T(8,128)(2,1)S(1)}, u32[]{:S(2)}, u32[]{:S(2)}) collective-permute-start(bf16[128,2048]{1,0:T(8,128)(2,1)S(1)} %get-tuple-element.68), channel_id=1, source_target_pairs={{0,24},{8,0},{16,8},{24,16},{32,56},{40,32},{48,40},{56,48},{64,88... | collective-permute-start | bytes 1572872 | tf_op jit(solution)/shard_map/ppermute | solution.py:37
  143.0 13.2 %collective-permute-start.31 = (bf16[128,2048]{1,0:T(8,128)(2,1)S(1)}, bf16[128,2048]{1,0:T(8,128)(2,1)S(1)}, u32[]{:S(2)}, u32[]{:S(2)}) collective-permute-start(bf16[128,2048]{1,0:T(8,128)(2,1)S(1)} %get-tuple-element.69), channel_id=1, source_target_pairs={{0,16},{8,24},{16,0},{24,8},{32,48},{40,56},{48,32},{56,40},{64,80... | collective-permute-start | bytes 1572872 | tf_op jit(solution)/shard_map/ppermute | solution.py:37
  143.5 23.9 %collective-permute-start.32 = (bf16[128,2048]{1,0:T(8,128)(2,1)S(1)}, bf16[128,2048]{1,0:T(8,128)(2,1)S(1)}, u32[]{:S(2)}, u32[]{:S(2)}) collective-permute-start(bf16[128,2048]{1,0:T(8,128)(2,1)S(1)} %get-tuple-element.70), channel_id=1, source_target_pairs={{0,8},{8,16},{16,24},{24,0},{32,40},{40,48},{48,56},{56,32},{64,72... | collective-permute-start | bytes 1572872 | tf_op jit(solution)/shard_map/ppermute | solution.py:37
  147.0 23.2 %collective-permute-start.24 = (bf16[128,2048]{1,0:T(8,128)(2,1)S(1)}, bf16[128,2048]{1,0:T(8,128)(2,1)S(1)}, u32[]{:S(2)}, u32[]{:S(2)}) collective-permute-start(bf16[128,2048]{1,0:T(8,128)(2,1)S(1)} %get-tuple-element.60), channel_id=1, source_target_pairs={{0,96},{8,104},{16,112},{24,120},{32,0},{40,8},{48,16},{56,24},{64... | collective-permute-start | bytes 1572872 | tf_op jit(solution)/shard_map/ppermute | solution.py:37
  149.7 20.7 %collective-permute-start.25 = (bf16[128,2048]{1,0:T(8,128)(2,1)S(1)}, bf16[128,2048]{1,0:T(8,128)(2,1)S(1)}, u32[]{:S(2)}, u32[]{:S(2)}) collective-permute-start(bf16[128,2048]{1,0:T(8,128)(2,1)S(1)} %get-tuple-element.61), channel_id=1, source_target_pairs={{0,64},{8,72},{16,80},{24,88},{32,96},{40,104},{48,112},{56,120},{... | collective-permute-start | bytes 1572872 | tf_op jit(solution)/shard_map/ppermute | solution.py:37
  156.2 14.2 %collective-permute-start.26 = (bf16[128,2048]{1,0:T(8,128)(2,1)S(1)}, bf16[128,2048]{1,0:T(8,128)(2,1)S(1)}, u32[]{:S(2)}, u32[]{:S(2)}) collective-permute-start(bf16[128,2048]{1,0:T(8,128)(2,1)S(1)} %get-tuple-element.62), channel_id=1, source_target_pairs={{0,32},{8,40},{16,48},{24,56},{32,64},{40,72},{48,80},{56,88},{64,... | collective-permute-start | bytes 1572872 | tf_op jit(solution)/shard_map/ppermute | solution.py:37
  167.9 8.1 %collective-permute-start.33 = (bf16[32,2048]{1,0:T(8,128)(2,1)S(1)}, bf16[32,2048]{1,0:T(8,128)(2,1)S(1)}, u32[]{:S(2)}, u32[]{:S(2)}) collective-permute-start(bf16[32,2048]{1,0:T(8,128)(2,1)S(1)} %get-tuple-element.72), channel_id=1, source_target_pairs={{0,96},{8,104},{16,112},{24,120},{32,0},{40,8},{48,16},{56,24},{64... | collective-permute-start | bytes 393224 | tf_op jit(solution)/shard_map/ppermute | solution.py:37
  168.4 9.0 %collective-permute-start.34 = (bf16[32,2048]{1,0:T(8,128)(2,1)S(1)}, bf16[32,2048]{1,0:T(8,128)(2,1)S(1)}, u32[]{:S(2)}, u32[]{:S(2)}) collective-permute-start(bf16[32,2048]{1,0:T(8,128)(2,1)S(1)} %get-tuple-element.73), channel_id=1, source_target_pairs={{0,64},{8,72},{16,80},{24,88},{32,96},{40,104},{48,112},{56,120},{... | collective-permute-start | bytes 393224 | tf_op jit(solution)/shard_map/ppermute | solution.py:37
  182.2 20.6 %all-to-all-start.1 = ((bf16[8,32,512]{2,1,0:T(8,128)(2,1)}), bf16[8,32,512]{2,1,0:T(8,128)(2,1)S(1)}, u32[]{:S(2)}, u32[]{:S(2)}) async-start(bf16[8,32,512]{2,1,0:T(8,128)(2,1)} %add_last.1), calls=%async_computation.1 | async-start | bytes 524288 | tf_op jit(solution)/shard_map/all_to_all | solution.py:368
  (24 other events, 246.4 us)

commit v4 on v3

--- a/solution.py
+++ b/solution.py
@@ -13,6 +13,7 @@
 CAP = 32
 EPS = 1e-05
 HIDE = -1e30
+FIRST_ROOM = 24
 SCALE2 = math.log2(math.e) / math.sqrt(HEAD_DIM)
 BF = jnp.bfloat16
 F32 = jnp.float32
@@ -166,68 +167,110 @@
     )(x, gain)
 
 
-def hidden_kernel(*refs):
-    low, high = refs[0:4], refs[4:8]
-    wg_ref, wu_ref, out_ref, x_scr = refs[8:]
-
-    @pl.when(pl.program_id(0) == 0)
-    def _():
-        for a in range(4):
-            for b in range(4):
-                r = 32 * (4 * a + b)
-                x_scr[r : r + 32, :2048] = low[a][b]
-                x_scr[r : r + 32, 2048:] = high[b][a]
-
-    both = jnp.concatenate([wg_ref[0], wu_ref[0]], axis=1)
+EARLY = [(a, b) for a in (0, 1, 3) for b in (0, 1, 3)]
+LATE = [(a, b) for a in range(4) for b in range(4) if a == 2 or b == 2]
+
+
+def gate_and_up(x_scr, both, out_ref):
     result = jnp.dot(x_scr[...], both, preferred_element_type=F32)
     gate = result[:, :128]
     out_ref[...] = (gate / (1.0 + jnp.exp(-gate)) * result[:, 128:]).astype(BF)
 
 
-def hidden_units(low, high, w_gate, w_up):
-    part = pl.BlockSpec((4, 32, 2048), lambda i: (0, 0, 0), pipeline_mode=pl.Buffered(1))
-    tile = pl.BlockSpec((1, 4096, 128), lambda i: (0, 0, i))
-    return pl.pallas_call(
-        hidden_kernel,
-        out_shape=jax.ShapeDtypeStruct((512, 896), BF),
-        grid=(7,),
-        in_specs=[part] * 8 + [tile, tile],
-        out_specs=pl.BlockSpec((512, 128), lambda i: (0, i)),
-        scratch_shapes=[pltpu.VMEM((512, 4096), BF)],
-        compiler_params=room(20),
-        name="hidden_units",
-    )(*low, *high, w_gate, w_up)
-
-
-def down_kernel(swap, h_ref, wd_ref, o0, o1, o2, o3, h_scr):
+def first_kernel(l0, l1, l3, h0, h1, h3, wg_ref, wu_ref, out_ref, both_ref, x_scr):
     @pl.when(pl.program_id(0) == 0)
     def _():
-        for a in range(4):
-            for b in range(4):
-                r = 32 * (4 * a + b)
-                t = 32 * (4 * b + a) if swap else r
-                h_scr[t : t + 32] = h_ref[r : r + 32]
+        low, high = (l0, l1, None, l3), (h0, h1, None, h3)
+        for k, (a, b) in enumerate(EARLY):
+            rows = slice(32 * k, 32 * k + 32)
+            x_scr[rows, :2048] = low[a][b]
+            x_scr[rows, 2048:] = high[b][a]
+
+    both = jnp.concatenate([wg_ref[0], wu_ref[0]], axis=1)
+    both_ref[0] = both
+    gate_and_up(x_scr, both, out_ref)
+
+
+def second_kernel(l0, l1, l3, h0, h1, h3, la, lb, ha, hb, both_ref, out_ref, x_scr):
+    @pl.when(pl.program_id(0) == 0)
+    def _():
+        low, high = (l0, l1, None, l3), (h0, h1, None, h3)
+        low_far, high_far = (la, la, lb, lb), (ha, ha, hb, hb)
+        for k, (a, b) in enumerate(LATE):
+            rows = slice(32 * k, 32 * k + 32)
+            x_scr[rows, :2048] = low_far[b][b % 2] if a == 2 else low[a][b]
+            x_scr[rows, 2048:] = high_far[a][a % 2] if b == 2 else high[b][a]
+
+    gate_and_up(x_scr, both_ref[0], out_ref)
+
+
+def whole_once(shape):
+    return pl.BlockSpec(shape, lambda i: tuple(0 for _ in shape), pipeline_mode=pl.Buffered(1))
+
+
+def hidden_first(parts, w_gate, w_up):
+    tile = pl.BlockSpec((1, 4096, 128), lambda i: (0, 0, i))
+    return pl.pallas_call(
+        first_kernel,
+        out_shape=(
+            jax.ShapeDtypeStruct((288, 896), BF),
+            pltpu.VMEM((7, 4096, 256), BF),
+        ),
+        grid=(7,),
+        in_specs=[whole_once(p.shape) for p in parts] + [tile, tile],
+        out_specs=(
+            pl.BlockSpec((288, 128), lambda i: (0, i)),
+            pl.BlockSpec((1, 4096, 256), lambda i: (i, 0, 0)),
+        ),
+        scratch_shapes=[pltpu.VMEM((288, 4096), BF)],
+        compiler_params=room(FIRST_ROOM),
+        name="hidden_first",
+    )(*parts, *[pltpu.with_memory_space_constraint(w, pltpu.HBM) for w in (w_gate, w_up)])
+
+
+def hidden_second(parts, both):
+    return pl.pallas_call(
+        second_kernel,
+        out_shape=jax.ShapeDtypeStruct((224, 896), BF),
+        grid=(7,),
+        in_specs=[whole_once(p.shape) for p in parts]
+        + [pl.BlockSpec((1, 4096, 256), lambda i: (i, 0, 0))],
+        out_specs=pl.BlockSpec((224, 128), lambda i: (0, i)),
+        scratch_shapes=[pltpu.VMEM((224, 4096), BF)],
+        compiler_params=room(16),
+        name="hidden_second",
+    )(*parts, pltpu.with_memory_space_constraint(both, pltpu.VMEM))
+
+
+def down_kernel(swap, early_ref, late_ref, wd_ref, o0, o1, o2, o3, h_scr):
+    @pl.when(pl.program_id(0) == 0)
+    def _():
+        for ref, places in ((early_ref, EARLY), (late_ref, LATE)):
+            for k, (a, b) in enumerate(places):
+                t = 32 * (4 * b + a) if swap else 32 * (4 * a + b)
+                h_scr[t : t + 32] = ref[32 * k : 32 * k + 32]
 
     result = jnp.dot(h_scr[...], wd_ref[0], preferred_element_type=F32)
     for k, ref in enumerate((o0, o1, o2, o3)):
         ref[...] = result[128 * k : 128 * k + 128].astype(BF)
 
 
-def down(hidden, w_down, swap):
+def down(early, late, w_down, swap):
     offset = 4 if swap else 0
     return pl.pallas_call(
         functools.partial(down_kernel, swap),
         out_shape=[jax.ShapeDtypeStruct((128, 2048), BF)] * 4,
         grid=(4,),
         in_specs=[
-            pl.BlockSpec((512, 896), lambda i: (0, 0)),
+            whole_once(early.shape),
+            whole_once(late.shape),
             pl.BlockSpec((1, 896, 512), lambda i: (0, 0, i + offset)),
         ],
         out_specs=[pl.BlockSpec((128, 512), lambda i: (0, i))] * 4,
         scratch_shapes=[pltpu.VMEM((512, 896), BF)],
         compiler_params=room(12),
         name="down_high" if swap else "down_low",
-    )(hidden, w_down)
+    )(early, late, w_down)
 
 
 def add_kernel(a, b, c, d, o0, o1, o2, o3):
@@ -360,10 +403,17 @@
     mine = lax.all_to_all(slots.reshape(8, 32, 512), "expert", split_axis=0, concat_axis=0, tiled=True)
     low, high = norm(mine, norm_gain[None, :])
     low, high = lax.optimization_barrier((spread_near(low, 1), spread_near(high, 0)))
-    low, high = spread_far(jnp.stack(low), 0), spread_far(jnp.stack(high), 1)
-    hidden = hidden_units(low, high, w_gate, w_up)
-    low = add_first(collect(down(hidden, w_down, False), 0))
-    high = add_first(collect(down(hidden, w_down, True), 1))
+    low, high = jnp.stack(low), jnp.stack(high)
+    low = [low, shift_dp(low, 0, 1), shift_dp(low, 0, -1)]
+    high = [high, shift_dp(high, 1, 1), shift_dp(high, 1, -1)]
+    low_far = [shift_dp(low[1][:2], 0, 1), shift_dp(low[2][2:], 0, -1)]
+    high_far = [shift_dp(high[1][:2], 1, 1), shift_dp(high[2][2:], 1, -1)]
+    parts = low + high
+    early, both = hidden_first(parts, w_gate, w_up)
+    parts = parts + low_far + high_far
+    late = hidden_second(parts, both)
+    low = add_first(collect(down(early, late, w_down, False), 0))
+    high = add_first(collect(down(early, late, w_down, True), 1))
     summed = add_last(collect(low, 1), collect(high, 0))
     back = lax.all_to_all(summed, "expert", split_axis=0, concat_axis=0, tiled=True)
     layer_out = finish(mix, back.reshape(256, 512), stream)

time: 204 us -> 188 us (0.922)
  starting transfers between devices: 73.3 us -> 66.1 us
  waiting for transfers between devices: 75.1 us -> 68 us
  local copies, waits for them, and re-layouts: 7.06 us -> 2.01 us
  Pallas kernels: 42.4 us -> 45.7 us
    ppermute x36 -> x38, waiting for transfers between devices: 62.5 us -> 55.4 us  [shift_dp(): return lax.ppermute(value, 'dp', ring_pairs(axis, shift))]
    unnamed x21 -> x15, local copies, waits for them, and re-layouts: 6.46 us -> 1.34 us
    ppermute x36 -> x38, starting transfers between devices: 50.9 us -> 46.4 us  [shift_dp(): return lax.ppermute(value, 'dp', ring_pairs(axis, shift))]
    pallas_call x1 -> x2, Pallas kernels: 11.9 us -> 15.2 us  [the longest x1 9.94 us: hidden_first(): pl.pallas_call(first_kernel, out_shape=(jax.ShapeDtypeStruct((288, 896),...]
    all_to_all x1, starting transfers between devices: 14.1 us -> 11.5 us  [body(): lax.all_to_all(summed, 'expert', split_axis=0, concat_axis=0, tiled=True)]
  transfers between devices with their start and end apart: 38 -> 40, of which waited for: 21 -> 18; matrix products, arithmetic and copies ran while one was open for 2% -> 3% of each run, Pallas kernels for 9% -> 15%
where the time goes in v4:
time: 188 us
  waiting for transfers between devices  68 us (36%)
  starting transfers between devices  66.1 us (35%)
  Pallas kernels  45.7 us (24%)
  other arithmetic  4.46 us (2%)
  local copies, waits for them, and re-layouts  2.01 us (1%)
    ppermute x38, waiting for transfers between devices, shift_dp(): return lax.ppermute(value, 'dp', ring_pairs(axis, shift))  55.4 us
    ppermute x38, starting transfers between devices, shift_dp(): return lax.ppermute(value, 'dp', ring_pairs(axis, shift))  46.4 us
    pallas_call x4, Pallas kernels, attend(): pl.pallas_call(attend_kernel, out_shape=jax.ShapeDtypeStruct((4, 64, 640)...  17.9 us
    all_to_all x1, starting transfers between devices, body(): lax.all_to_all(summed, 'expert', split_axis=0, concat_axis=0, tiled=True)  11.5 us
    pallas_call x1, Pallas kernels, hidden_first(): pl.pallas_call(first_kernel, out_shape=(jax.ShapeDtypeStruct((288, 896),...  9.94 us
    all_to_all x1, starting transfers between devices, body(): lax.all_to_all(slots.reshape(8, 32, 512), 'expert', split_axis=0, concat_...  8.19 us
    pallas_call x2, Pallas kernels, down(): pl.pallas_call(functools.partial(down_kernel, swap), out_shape=[jax.Shape...  6.76 us
    all_to_all x1, waiting for transfers between devices, body(): lax.all_to_all(slots.reshape(8, 32, 512), 'expert', split_axis=0, concat_...  6.49 us
  transfers between devices with their start and end apart: 40, of which 18 were waited for; matrix products, arithmetic and copies ran while one was open for 3% of the time, Pallas kernels for 15%

profile of v4, /device:TPU:1, one launch (start us, length us, event | category | flops | bytes accessed | tf_op | source)
XLA Modules:
  0.0 187.5 jit_solution(13408675134459193257)
XLA Ops:
  17.2 4.5 %attend.4.a = bf16[4,64,640]{2,1,0:T(8,128)(2,1)S(1)} custom-call(bf16[4,64,640]{2,1,0:T(8,128)(2,1)S(1)} %pad_maximum_fusion.3.q_ref, bf16[128,128]{1,0:T(8,128)(2,1)S(1)} %pad.5.table_ref, bf16[256,2304]{1,0:T(8,128)(2,1)S(1)} %pad_maximum_fusion.kt_ref, bf16[2304,256]{1,0:T(8,128)(2,1)S(1)} %concatenate.11.v_ref), custom_call_target="tpu_custom_call" | custom-call | tf_op jit(solution)/shard_map/attend/pallas_call | solution.py:76
  21.7 7.5 %collective-permute-done.4.q_ref = bf16[4,64,640]{2,1,0:T(8,128)(2,1)S(1)} collective-permute-done((bf16[4,64,640]{2,1,0:T(8,128)(2,1)S(1)}, bf16[4,64,640]{2,1,0:T(8,128)(2,1)S(1)}, u32[]{:S(2)}, u32[]{:S(2)}) %collective-permute-start.4) | collective-permute-done | bytes 327712 | tf_op jit(solution)/shard_map/ppermute | solution.py:38
  29.7 4.5 %attend.7 = bf16[4,64,640]{2,1,0:T(8,128)(2,1)S(1)} custom-call(bf16[4,64,640]{2,1,0:T(8,128)(2,1)S(1)} %collective-permute-done.5.q_ref, bf16[128,128]{1,0:T(8,128)(2,1)S(1)} %pad.5.table_ref, bf16[256,2304]{1,0:T(8,128)(2,1)S(1)} %pad_maximum_fusion.kt_ref, bf16[2304,256]{1,0:T(8,128)(2,1)S(1)} %concatenate.11.v_ref), custom_call_target="tpu_custom_call" | custom-call | tf_op jit(solution)/shard_map/attend/pallas_call | solution.py:76
  36.0 4.5 %attend.6 = bf16[4,64,640]{2,1,0:T(8,128)(2,1)S(1)} custom-call(bf16[4,64,640]{2,1,0:T(8,128)(2,1)S(1)} %collective-permute-done.4.q_ref, bf16[128,128]{1,0:T(8,128)(2,1)S(1)} %pad.5.table_ref, bf16[256,2304]{1,0:T(8,128)(2,1)S(1)} %pad_maximum_fusion.kt_ref, bf16[2304,256]{1,0:T(8,128)(2,1)S(1)} %concatenate.11.v_ref), custom_call_target="tpu_custom_call" | custom-call | tf_op jit(solution)/shard_map/attend/pallas_call | solution.py:76
  40.5 2.9 %collective-permute-start.7 = (bf16[4,64,640]{2,1,0:T(8,128)(2,1)S(1)}, bf16[4,64,640]{2,1,0:T(8,128)(2,1)S(1)}, u32[]{:S(2)}, u32[]{:S(2)}) collective-permute-start(bf16[4,64,640]{2,1,0:T(8,128)(2,1)S(1)} %attend.6), channel_id=1, source_target_pairs={{0,64},{8,72},{16,80},{24,88},{32,96},{40,104},{48,112},{56,120},{... | collective-permute-start | bytes 983048 | tf_op jit(solution)/shard_map/ppermute | solution.py:38
  43.4 4.5 %attend.5 = bf16[4,64,640]{2,1,0:T(8,128)(2,1)S(1)} custom-call(bf16[4,64,640]{2,1,0:T(8,128)(2,1)S(1)} %collective-permute-done.3.q_ref, bf16[128,128]{1,0:T(8,128)(2,1)S(1)} %pad.5.table_ref, bf16[256,2304]{1,0:T(8,128)(2,1)S(1)} %pad_maximum_fusion.kt_ref, bf16[2304,256]{1,0:T(8,128)(2,1)S(1)} %concatenate.11.v_ref), custom_call_target="tpu_custom_call" | custom-call | tf_op jit(solution)/shard_map/attend/pallas_call | solution.py:76
  48.2 5.0 %collective-permute-done.7.c = bf16[4,64,640]{2,1,0:T(8,128)(2,1)S(1)} collective-permute-done((bf16[4,64,640]{2,1,0:T(8,128)(2,1)S(1)}, bf16[4,64,640]{2,1,0:T(8,128)(2,1)S(1)}, u32[]{:S(2)}, u32[]{:S(2)}) %collective-permute-start.7) | collective-permute-done | bytes 327712 | tf_op jit(solution)/shard_map/ppermute | solution.py:38
  53.2 3.6 %collective-permute-done.6.b = bf16[4,64,640]{2,1,0:T(8,128)(2,1)S(1)} collective-permute-done((bf16[4,64,640]{2,1,0:T(8,128)(2,1)S(1)}, bf16[4,64,640]{2,1,0:T(8,128)(2,1)S(1)}, u32[]{:S(2)}, u32[]{:S(2)}) %collective-permute-start.6) | collective-permute-done | bytes 327712 | tf_op jit(solution)/shard_map/ppermute | solution.py:38
  65.4 8.2 %all-to-all-start = ((bf16[8,32,512]{2,1,0:T(8,128)(2,1)}), bf16[8,32,512]{2,1,0:T(8,128)(2,1)S(1)}, u32[]{:S(2)}, u32[]{:S(2)}) async-start(bf16[8,32,512]{2,1,0:T(8,128)(2,1)} %bitcast.12), calls=%async_computation | async-start | bytes 524288 | tf_op jit(solution)/shard_map/all_to_all | solution.py:403
  73.7 6.5 %all-to-all-done.x_ref = bf16[8,32,512]{2,1,0:T(8,128)(2,1)S(1)} async-done(((bf16[8,32,512]{2,1,0:T(8,128)(2,1)}), bf16[8,32,512]{2,1,0:T(8,128)(2,1)S(1)}, u32[]{:S(2)}, u32[]{:S(2)}) %all-to-all-start) | async-done | bytes 262176 | tf_op jit(solution)/shard_map/all_to_all | solution.py:403
  85.5 2.8 %collective-permute-start.16 = (bf16[32,2048]{1,0:T(8,128)(2,1)S(1)}, bf16[32,2048]{1,0:T(8,128)(2,1)S(1)}, u32[]{:S(2)}, u32[]{:S(2)}) collective-permute-start(bf16[32,2048]{1,0:T(8,128)(2,1)S(1)} %get-tuple-element.57), channel_id=1, source_target_pairs={{0,64},{8,72},{16,80},{24,88},{32,96},{40,104},{48,112},{56,120},{... | collective-permute-start | bytes 393224 | tf_op jit(solution)/shard_map/ppermute | solution.py:38
  96.0 2.7 %collective-permute-start.19 = (bf16[4,32,2048]{2,1,0:T(8,128)(2,1)S(1)}, bf16[4,32,2048]{2,1,0:T(8,128)(2,1)S(1)}, u32[]{:S(2)}, u32[]{:S(2)}) collective-permute-start(bf16[4,32,2048]{2,1,0:T(8,128)(2,1)S(1)} %pad_maximum_fusion.1.l0), channel_id=1, source_target_pairs={{0,96},{8,104},{16,112},{24,120},{32,0},{40,8},{48,16},{56,24},{64... | collective-permute-start | bytes 1572872 | tf_op jit(solution)/shard_map/ppermute | solution.py:38
  98.7 6.4 %collective-permute-done.20.h1 = bf16[4,32,2048]{2,1,0:T(8,128)(2,1)S(1)} collective-permute-done((bf16[4,32,2048]{2,1,0:T(8,128)(2,1)S(1)}, bf16[4,32,2048]{2,1,0:T(8,128)(2,1)S(1)}, u32[]{:S(2)}, u32[]{:S(2)}) %collective-permute-start.20) | collective-permute-done | bytes 524320 | tf_op jit(solution)/shard_map/ppermute | solution.py:38
  105.3 2.7 %collective-permute-start.25 = (bf16[2,32,2048]{2,1,0:T(8,128)(2,1)S(1)}, bf16[2,32,2048]{2,1,0:T(8,128)(2,1)S(1)}, u32[]{:S(2)}, u32[]{:S(2)}) collective-permute-start(bf16[2,32,2048]{2,1,0:T(8,128)(2,1)S(1)} %slice.19), channel_id=1, source_target_pairs={{0,24},{8,0},{16,8},{24,16},{32,56},{40,32},{48,40},{56,48},{64,88... | collective-permute-start | bytes 786440 | tf_op jit(solution)/shard_map/ppermute | solution.py:38
  108.1 2.7 %collective-permute-start.23 = (bf16[2,32,2048]{2,1,0:T(8,128)(2,1)S(1)}, bf16[2,32,2048]{2,1,0:T(8,128)(2,1)S(1)}, u32[]{:S(2)}, u32[]{:S(2)}) collective-permute-start(bf16[2,32,2048]{2,1,0:T(8,128)(2,1)S(1)} %slice.17), channel_id=1, source_target_pairs={{0,96},{8,104},{16,112},{24,120},{32,0},{40,8},{48,16},{56,24},{64... | collective-permute-start | bytes 786440 | tf_op jit(solution)/shard_map/ppermute | solution.py:38
  110.9 9.9 %hidden_first.1 = (bf16[288,896]{1,0:T(8,128)(2,1)S(1)}, bf16[7,4096,256]{2,1,0:T(8,128)(2,1)S(1)}) custom-call(bf16[4,32,2048]{2,1,0:T(8,128)(2,1)S(1)} %pad_maximum_fusion.1.l0, bf16[4,32,2048]{2,1,0:T(8,128)(2,1)S(1)} %collective-permute-done.18.l1, bf16[4,32,2048]{2,1,0:T(8,128)(2,1)S(1)} %collective-permute-done.19.l3, ...), custom_call_target="tpu_custom_call" | custom-call | tf_op jit(solution)/shard_map/hidden_first/pallas_call | solution.py:213
  120.9 5.2 %hidden_second.1.late_ref = bf16[224,896]{1,0:T(8,128)(2,1)S(1)} custom-call(bf16[4,32,2048]{2,1,0:T(8,128)(2,1)S(1)} %pad_maximum_fusion.1.l0, bf16[4,32,2048]{2,1,0:T(8,128)(2,1)S(1)} %collective-permute-done.18.l1, bf16[4,32,2048]{2,1,0:T(8,128)(2,1)S(1)} %collective-permute-done.19.l3, bf16[4,32,2048]{2,1,0:T(8,128)(2,1)S(1)} %pad_maximum_fusion.2.h0, ...), custom_call_target="tpu_custom_call" | custom-call | tf_op jit(solution)/shard_map/hidden_second/pallas_call | solution.py:232
  126.1 3.4 %down_high.1 = (bf16[128,2048]{1,0:T(8,128)(2,1)S(1)}, bf16[128,2048]{1,0:T(8,128)(2,1)S(1)}, bf16[128,2048]{1,0:T(8,128)(2,1)S(1)}, bf16[128,2048]{1,0:T(8,128)(2,1)S(1)}) custom-call(bf16[288,896]{1,0:T(8,128)(2,1)S(1)} %get-tuple-element.61.early_ref, bf16[224,896]{1,0:T(8,128)(2,1)S(1)} %hidden_second.1.late_ref, bf16[1,896,4096]{2,1,0:T(8,128)(2,1)S(1)} %bitcast.31), custom_call_target="tpu_custom_call" | custom-call | tf_op jit(solution)/shard_map/down_high/pallas_call | solution.py:260
  131.1 3.4 %down_low.1 = (bf16[128,2048]{1,0:T(8,128)(2,1)S(1)}, bf16[128,2048]{1,0:T(8,128)(2,1)S(1)}, bf16[128,2048]{1,0:T(8,128)(2,1)S(1)}, bf16[128,2048]{1,0:T(8,128)(2,1)S(1)}) custom-call(bf16[288,896]{1,0:T(8,128)(2,1)S(1)} %get-tuple-element.61.early_ref, bf16[224,896]{1,0:T(8,128)(2,1)S(1)} %hidden_second.1.late_ref, bf16[1,896,4096]{2,1,0:T(8,128)(2,1)S(1)} %bitcast.31), custom_call_target="tpu_custom_call" | custom-call | tf_op jit(solution)/shard_map/down_low/pallas_call | solution.py:260
  135.2 3.1 %collective-permute-done.32.b = bf16[128,2048]{1,0:T(8,128)(2,1)S(1)} collective-permute-done((bf16[128,2048]{1,0:T(8,128)(2,1)S(1)}, bf16[128,2048]{1,0:T(8,128)(2,1)S(1)}, u32[]{:S(2)}, u32[]{:S(2)}) %collective-permute-start.32) | collective-permute-done | bytes 524320 | tf_op jit(solution)/shard_map/ppermute | solution.py:38
  140.0 16.3 %collective-permute-done.34.d = bf16[128,2048]{1,0:T(8,128)(2,1)S(1)} collective-permute-done((bf16[128,2048]{1,0:T(8,128)(2,1)S(1)}, bf16[128,2048]{1,0:T(8,128)(2,1)S(1)}, u32[]{:S(2)}, u32[]{:S(2)}) %collective-permute-start.34) | collective-permute-done | bytes 524320 | tf_op jit(solution)/shard_map/ppermute | solution.py:38
  163.7 3.2 %collective-permute-done.37.refs_7_ = bf16[32,2048]{1,0:T(8,128)(2,1)S(1)} collective-permute-done((bf16[32,2048]{1,0:T(8,128)(2,1)S(1)}, bf16[32,2048]{1,0:T(8,128)(2,1)S(1)}, u32[]{:S(2)}, u32[]{:S(2)}) %collective-permute-start.37) | collective-permute-done | bytes 131104 | tf_op jit(solution)/shard_map/ppermute | solution.py:38
  168.7 11.5 %all-to-all-start.1 = ((bf16[8,32,512]{2,1,0:T(8,128)(2,1)}), bf16[8,32,512]{2,1,0:T(8,128)(2,1)S(1)}, u32[]{:S(2)}, u32[]{:S(2)}) async-start(bf16[8,32,512]{2,1,0:T(8,128)(2,1)} %add_last.1), calls=%async_computation.1 | async-start | bytes 524288 | tf_op jit(solution)/shard_map/all_to_all | solution.py:418
  180.6 6.1 %all-to-all-done.1 = bf16[8,32,512]{2,1,0:T(8,128)(2,1)S(1)} async-done(((bf16[8,32,512]{2,1,0:T(8,128)(2,1)}), bf16[8,32,512]{2,1,0:T(8,128)(2,1)S(1)}, u32[]{:S(2)}, u32[]{:S(2)}) %all-to-all-start.1) | async-done | bytes 262176 | tf_op jit(solution)/shard_map/all_to_all | solution.py:418
  (119 shorter events, 55.3 us)
Async XLA Ops:
  2.3 9.8 %collective-permute-start = (bf16[64,640]{1,0:T(8,128)(2,1)S(1)}, bf16[64,640]{1,0:T(8,128)(2,1)S(1)}, u32[]{:S(2)}, u32[]{:S(2)}) collective-permute-start(bf16[64,640]{1,0:T(8,128)(2,1)S(1)} %get-tuple-element.81), channel_id=1, source_target_pairs={{0,8},{8,16},{16,24},{24,0},{32,40},{40,48},{48,56},{56,32},{64,72... | collective-permute-start | bytes 245768 | tf_op jit(solution)/shard_map/ppermute | solution.py:38
  12.2 9.5 %collective-permute-start.3 = (bf16[4,64,640]{2,1,0:T(8,128)(2,1)S(1)}, bf16[4,64,640]{2,1,0:T(8,128)(2,1)S(1)}, u32[]{:S(2)}, u32[]{:S(2)}) collective-permute-start(bf16[4,64,640]{2,1,0:T(8,128)(2,1)S(1)} %pad_maximum_fusion.3.q_ref), channel_id=1, source_target_pairs={{0,32},{8,40},{16,48},{24,56},{32,64},{40,72},{48,80},{56,88},{64,... | collective-permute-start | bytes 983048 | tf_op jit(solution)/shard_map/ppermute | solution.py:38
  13.5 15.7 %collective-permute-start.4 = (bf16[4,64,640]{2,1,0:T(8,128)(2,1)S(1)}, bf16[4,64,640]{2,1,0:T(8,128)(2,1)S(1)}, u32[]{:S(2)}, u32[]{:S(2)}) collective-permute-start(bf16[4,64,640]{2,1,0:T(8,128)(2,1)S(1)} %pad_maximum_fusion.3.q_ref), channel_id=1, source_target_pairs={{0,64},{8,72},{16,80},{24,88},{32,96},{40,104},{48,112},{56,120},{... | collective-permute-start | bytes 983048 | tf_op jit(solution)/shard_map/ppermute | solution.py:38
  15.9 13.8 %collective-permute-start.5 = (bf16[4,64,640]{2,1,0:T(8,128)(2,1)S(1)}, bf16[4,64,640]{2,1,0:T(8,128)(2,1)S(1)}, u32[]{:S(2)}, u32[]{:S(2)}) collective-permute-start(bf16[4,64,640]{2,1,0:T(8,128)(2,1)S(1)} %pad_maximum_fusion.3.q_ref), channel_id=1, source_target_pairs={{0,96},{8,104},{16,112},{24,120},{32,0},{40,8},{48,16},{56,24},{64... | collective-permute-start | bytes 983048 | tf_op jit(solution)/shard_map/ppermute | solution.py:38
  34.2 14.0 %collective-permute-start.8 = (bf16[4,64,640]{2,1,0:T(8,128)(2,1)S(1)}, bf16[4,64,640]{2,1,0:T(8,128)(2,1)S(1)}, u32[]{:S(2)}, u32[]{:S(2)}) collective-permute-start(bf16[4,64,640]{2,1,0:T(8,128)(2,1)S(1)} %attend.7), channel_id=1, source_target_pairs={{0,32},{8,40},{16,48},{24,56},{32,64},{40,72},{48,80},{56,88},{64,... | collective-permute-start | bytes 983048 | tf_op jit(solution)/shard_map/ppermute | solution.py:38
  40.5 12.7 %collective-permute-start.7 = (bf16[4,64,640]{2,1,0:T(8,128)(2,1)S(1)}, bf16[4,64,640]{2,1,0:T(8,128)(2,1)S(1)}, u32[]{:S(2)}, u32[]{:S(2)}) collective-permute-start(bf16[4,64,640]{2,1,0:T(8,128)(2,1)S(1)} %attend.6), channel_id=1, source_target_pairs={{0,64},{8,72},{16,80},{24,88},{32,96},{40,104},{48,112},{56,120},{... | collective-permute-start | bytes 983048 | tf_op jit(solution)/shard_map/ppermute | solution.py:38
  47.9 8.9 %collective-permute-start.6 = (bf16[4,64,640]{2,1,0:T(8,128)(2,1)S(1)}, bf16[4,64,640]{2,1,0:T(8,128)(2,1)S(1)}, u32[]{:S(2)}, u32[]{:S(2)}) collective-permute-start(bf16[4,64,640]{2,1,0:T(8,128)(2,1)S(1)} %attend.5), channel_id=1, source_target_pairs={{0,96},{8,104},{16,112},{24,120},{32,0},{40,8},{48,16},{56,24},{64... | collective-permute-start | bytes 983048 | tf_op jit(solution)/shard_map/ppermute | solution.py:38
  65.4 14.7 %all-to-all-start = ((bf16[8,32,512]{2,1,0:T(8,128)(2,1)}), bf16[8,32,512]{2,1,0:T(8,128)(2,1)S(1)}, u32[]{:S(2)}, u32[]{:S(2)}) async-start(bf16[8,32,512]{2,1,0:T(8,128)(2,1)} %bitcast.12), calls=%async_computation | async-start | bytes 524288 | tf_op jit(solution)/shard_map/all_to_all | solution.py:403
  93.1 12.0 %collective-permute-start.20 = (bf16[4,32,2048]{2,1,0:T(8,128)(2,1)S(1)}, bf16[4,32,2048]{2,1,0:T(8,128)(2,1)S(1)}, u32[]{:S(2)}, u32[]{:S(2)}) collective-permute-start(bf16[4,32,2048]{2,1,0:T(8,128)(2,1)S(1)} %pad_maximum_fusion.2.h0), channel_id=1, source_target_pairs={{0,8},{8,16},{16,24},{24,0},{32,40},{40,48},{48,56},{56,32},{64,72... | collective-permute-start | bytes 1572872 | tf_op jit(solution)/shard_map/ppermute | solution.py:38
  93.5 11.7 %collective-permute-start.21 = (bf16[4,32,2048]{2,1,0:T(8,128)(2,1)S(1)}, bf16[4,32,2048]{2,1,0:T(8,128)(2,1)S(1)}, u32[]{:S(2)}, u32[]{:S(2)}) collective-permute-start(bf16[4,32,2048]{2,1,0:T(8,128)(2,1)S(1)} %pad_maximum_fusion.2.h0), channel_id=1, source_target_pairs={{0,24},{8,0},{16,8},{24,16},{32,56},{40,32},{48,40},{56,48},{64,88... | collective-permute-start | bytes 1572872 | tf_op jit(solution)/shard_map/ppermute | solution.py:38
  96.0 12.0 %collective-permute-start.18 = (bf16[4,32,2048]{2,1,0:T(8,128)(2,1)S(1)}, bf16[4,32,2048]{2,1,0:T(8,128)(2,1)S(1)}, u32[]{:S(2)}, u32[]{:S(2)}) collective-permute-start(bf16[4,32,2048]{2,1,0:T(8,128)(2,1)S(1)} %pad_maximum_fusion.1.l0), channel_id=1, source_target_pairs={{0,32},{8,40},{16,48},{24,56},{32,64},{40,72},{48,80},{56,88},{64,... | collective-permute-start | bytes 1572872 | tf_op jit(solution)/shard_map/ppermute | solution.py:38
  96.0 12.1 %collective-permute-start.19 = (bf16[4,32,2048]{2,1,0:T(8,128)(2,1)S(1)}, bf16[4,32,2048]{2,1,0:T(8,128)(2,1)S(1)}, u32[]{:S(2)}, u32[]{:S(2)}) collective-permute-start(bf16[4,32,2048]{2,1,0:T(8,128)(2,1)S(1)} %pad_maximum_fusion.1.l0), channel_id=1, source_target_pairs={{0,96},{8,104},{16,112},{24,120},{32,0},{40,8},{48,16},{56,24},{64... | collective-permute-start | bytes 1572872 | tf_op jit(solution)/shard_map/ppermute | solution.py:38
  105.2 15.7 %collective-permute-start.24 = (bf16[2,32,2048]{2,1,0:T(8,128)(2,1)S(1)}, bf16[2,32,2048]{2,1,0:T(8,128)(2,1)S(1)}, u32[]{:S(2)}, u32[]{:S(2)}) collective-permute-start(bf16[2,32,2048]{2,1,0:T(8,128)(2,1)S(1)} %slice.18), channel_id=1, source_target_pairs={{0,8},{8,16},{16,24},{24,0},{32,40},{40,48},{48,56},{56,32},{64,72... | collective-permute-start | bytes 786440 | tf_op jit(solution)/shard_map/ppermute | solution.py:38
  105.3 15.5 %collective-permute-start.25 = (bf16[2,32,2048]{2,1,0:T(8,128)(2,1)S(1)}, bf16[2,32,2048]{2,1,0:T(8,128)(2,1)S(1)}, u32[]{:S(2)}, u32[]{:S(2)}) collective-permute-start(bf16[2,32,2048]{2,1,0:T(8,128)(2,1)S(1)} %slice.19), channel_id=1, source_target_pairs={{0,24},{8,0},{16,8},{24,16},{32,56},{40,32},{48,40},{56,48},{64,88... | collective-permute-start | bytes 786440 | tf_op jit(solution)/shard_map/ppermute | solution.py:38
  108.0 12.8 %collective-permute-start.22 = (bf16[2,32,2048]{2,1,0:T(8,128)(2,1)S(1)}, bf16[2,32,2048]{2,1,0:T(8,128)(2,1)S(1)}, u32[]{:S(2)}, u32[]{:S(2)}) collective-permute-start(bf16[2,32,2048]{2,1,0:T(8,128)(2,1)S(1)} %slice.16), channel_id=1, source_target_pairs={{0,32},{8,40},{16,48},{24,56},{32,64},{40,72},{48,80},{56,88},{64,... | collective-permute-start | bytes 786440 | tf_op jit(solution)/shard_map/ppermute | solution.py:38
  108.1 12.7 %collective-permute-start.23 = (bf16[2,32,2048]{2,1,0:T(8,128)(2,1)S(1)}, bf16[2,32,2048]{2,1,0:T(8,128)(2,1)S(1)}, u32[]{:S(2)}, u32[]{:S(2)}) collective-permute-start(bf16[2,32,2048]{2,1,0:T(8,128)(2,1)S(1)} %slice.17), channel_id=1, source_target_pairs={{0,96},{8,104},{16,112},{24,120},{32,0},{40,8},{48,16},{56,24},{64... | collective-permute-start | bytes 786440 | tf_op jit(solution)/shard_map/ppermute | solution.py:38
  129.5 8.7 %collective-permute-start.32 = (bf16[128,2048]{1,0:T(8,128)(2,1)S(1)}, bf16[128,2048]{1,0:T(8,128)(2,1)S(1)}, u32[]{:S(2)}, u32[]{:S(2)}) collective-permute-start(bf16[128,2048]{1,0:T(8,128)(2,1)S(1)} %get-tuple-element.72), channel_id=1, source_target_pairs={{0,24},{8,0},{16,8},{24,16},{32,56},{40,32},{48,40},{56,48},{64,88... | collective-permute-start | bytes 1572872 | tf_op jit(solution)/shard_map/ppermute | solution.py:38
  129.6 10.3 %collective-permute-start.33 = (bf16[128,2048]{1,0:T(8,128)(2,1)S(1)}, bf16[128,2048]{1,0:T(8,128)(2,1)S(1)}, u32[]{:S(2)}, u32[]{:S(2)}) collective-permute-start(bf16[128,2048]{1,0:T(8,128)(2,1)S(1)} %get-tuple-element.73), channel_id=1, source_target_pairs={{0,16},{8,24},{16,0},{24,8},{32,48},{40,56},{48,32},{56,40},{64,80... | collective-permute-start | bytes 1572872 | tf_op jit(solution)/shard_map/ppermute | solution.py:38
  130.2 26.0 %collective-permute-start.34 = (bf16[128,2048]{1,0:T(8,128)(2,1)S(1)}, bf16[128,2048]{1,0:T(8,128)(2,1)S(1)}, u32[]{:S(2)}, u32[]{:S(2)}) collective-permute-start(bf16[128,2048]{1,0:T(8,128)(2,1)S(1)} %get-tuple-element.74), channel_id=1, source_target_pairs={{0,8},{8,16},{16,24},{24,0},{32,40},{40,48},{48,56},{56,32},{64,72... | collective-permute-start | bytes 1572872 | tf_op jit(solution)/shard_map/ppermute | solution.py:38
  134.5 23.1 %collective-permute-start.26 = (bf16[128,2048]{1,0:T(8,128)(2,1)S(1)}, bf16[128,2048]{1,0:T(8,128)(2,1)S(1)}, u32[]{:S(2)}, u32[]{:S(2)}) collective-permute-start(bf16[128,2048]{1,0:T(8,128)(2,1)S(1)} %get-tuple-element.64), channel_id=1, source_target_pairs={{0,96},{8,104},{16,112},{24,120},{32,0},{40,8},{48,16},{56,24},{64... | collective-permute-start | bytes 1572872 | tf_op jit(solution)/shard_map/ppermute | solution.py:38
  134.6 23.7 %collective-permute-start.27 = (bf16[128,2048]{1,0:T(8,128)(2,1)S(1)}, bf16[128,2048]{1,0:T(8,128)(2,1)S(1)}, u32[]{:S(2)}, u32[]{:S(2)}) collective-permute-start(bf16[128,2048]{1,0:T(8,128)(2,1)S(1)} %get-tuple-element.65), channel_id=1, source_target_pairs={{0,64},{8,72},{16,80},{24,88},{32,96},{40,104},{48,112},{56,120},{... | collective-permute-start | bytes 1572872 | tf_op jit(solution)/shard_map/ppermute | solution.py:38
  138.3 20.0 %collective-permute-start.28 = (bf16[128,2048]{1,0:T(8,128)(2,1)S(1)}, bf16[128,2048]{1,0:T(8,128)(2,1)S(1)}, u32[]{:S(2)}, u32[]{:S(2)}) collective-permute-start(bf16[128,2048]{1,0:T(8,128)(2,1)S(1)} %get-tuple-element.66), channel_id=1, source_target_pairs={{0,32},{8,40},{16,48},{24,56},{32,64},{40,72},{48,80},{56,88},{64,... | collective-permute-start | bytes 1572872 | tf_op jit(solution)/shard_map/ppermute | solution.py:38
  157.5 9.3 %collective-permute-start.37 = (bf16[32,2048]{1,0:T(8,128)(2,1)S(1)}, bf16[32,2048]{1,0:T(8,128)(2,1)S(1)}, u32[]{:S(2)}, u32[]{:S(2)}) collective-permute-start(bf16[32,2048]{1,0:T(8,128)(2,1)S(1)} %get-tuple-element.78), channel_id=1, source_target_pairs={{0,32},{8,40},{16,48},{24,56},{32,64},{40,72},{48,80},{56,88},{64,... | collective-permute-start | bytes 393224 | tf_op jit(solution)/shard_map/ppermute | solution.py:38
  168.7 18.0 %all-to-all-start.1 = ((bf16[8,32,512]{2,1,0:T(8,128)(2,1)}), bf16[8,32,512]{2,1,0:T(8,128)(2,1)S(1)}, u32[]{:S(2)}, u32[]{:S(2)}) async-start(bf16[8,32,512]{2,1,0:T(8,128)(2,1)} %add_last.1), calls=%async_computation.1 | async-start | bytes 524288 | tf_op jit(solution)/shard_map/all_to_all | solution.py:418
  (23 other events, 229.9 us)

commit v5 on v4

--- a/solution.py
+++ b/solution.py
@@ -319,10 +319,6 @@
     return [value] + [shift_dp(value, axis, s) for s in (1, 2, 3)]
 
 
-def spread_far(near, axis):
-    return [near] + [shift_dp(near, axis, s) for s in (1, 2, 3)]
-
-
 def collect(parts, axis):
     return [parts[0]] + [shift_dp(parts[s], axis, -s) for s in (1, 2, 3)]
 
@@ -358,10 +354,10 @@
 ):
     rows = queries.shape[0]
     node_count = parent.shape[0]
-    leaf_wide = jnp.broadcast_to(leaf_ids.astype(BF)[:, None], (rows, 128))
+    leaf_wide = jnp.broadcast_to(leaf_ids[:, None], (rows, 128)).astype(BF)
     q_own = jnp.concatenate([queries, leaf_wide], axis=1)
     near = jnp.stack(spread_near(q_own, 1))
-    groups = spread_far(near, 0)
+    plus, minus = shift_dp(near, 0, 1), shift_dp(near, 0, -1)
 
     lane = jnp.arange(128, dtype=jnp.int32)
     node = jnp.arange(node_count, dtype=jnp.int32)
@@ -393,10 +389,12 @@
     place_t = named[:, :, None] & (rank[:, :, None] == slot[None, None, :])
     mix = jnp.where(place_t, weight[:, :, None], 0.0).reshape(rows, EXPERTS * CAP).astype(BF)
 
-    partial = [attend(groups[0], table, kt_wide, v_wide), None, None, None]
-    partial[0], *groups[1:] = lax.optimization_barrier((partial[0], *groups[1:]))
-    for turn in (1, 3, 2):
-        partial[turn] = attend(groups[turn], table, kt_wide, v_wide)
+    partial = [attend(near, table, kt_wide, v_wide), None, None, None]
+    partial[0], plus, minus = lax.optimization_barrier((partial[0], plus, minus))
+    far = (shift_dp(plus[:2], 0, 1), shift_dp(minus[2:], 0, -1))
+    partial[1] = attend(plus, table, kt_wide, v_wide)
+    partial[3] = attend(minus, table, kt_wide, v_wide)
+    partial[2] = attend(jnp.concatenate(far, axis=0), table, kt_wide, v_wide)
     parts = collect(merge(collect(partial, 0)), 1)
     attention_out, stream, slots = combine(parts, residual, disp)
 

time: 188 us -> 185 us (0.984)
  waiting for transfers between devices: 68 us -> 63.1 us
    ppermute x38 -> x39, waiting for transfers between devices: 55.4 us -> 50.5 us  [shift_dp(): return lax.ppermute(value, 'dp', ring_pairs(axis, shift))]
    all_to_all x1, starting transfers between devices: 8.19 us -> 11.7 us  [body(): lax.all_to_all(slots.reshape(8, 32, 512), 'expert', split_axis=0, concat_...]
    all_to_all x1, starting transfers between devices: 11.5 us -> 9.45 us  [body(): lax.all_to_all(summed, 'expert', split_axis=0, concat_axis=0, tiled=True)]
    ppermute x38 -> x39, starting transfers between devices: 46.4 us -> 46.6 us  [shift_dp(): return lax.ppermute(value, 'dp', ring_pairs(axis, shift))]
  transfers between devices with their start and end apart: 40 -> 41, of which waited for: 18 -> 16; matrix products, arithmetic and copies ran while one was open for 3% -> 3% of each run, Pallas kernels for 15% -> 17%
where the time goes in v5:
time: 185 us; the launch traced here: 184 us
  starting transfers between devices  67.8 us (37%)
  waiting for transfers between devices  63.1 us (34%)
  Pallas kernels  45.8 us (25%)
  other arithmetic  4.5 us (2%)
  local copies, waits for them, and re-layouts  2.04 us (1%)
    ppermute x39, waiting for transfers between devices, shift_dp(): return lax.ppermute(value, 'dp', ring_pairs(axis, shift))  50.5 us
    ppermute x39, starting transfers between devices, shift_dp(): return lax.ppermute(value, 'dp', ring_pairs(axis, shift))  46.6 us
    pallas_call x4, Pallas kernels, attend(): pl.pallas_call(attend_kernel, out_shape=jax.ShapeDtypeStruct((4, 64, 640)...  18 us
    all_to_all x1, starting transfers between devices, body(): lax.all_to_all(slots.reshape(8, 32, 512), 'expert', split_axis=0, concat_...  11.7 us
    pallas_call x1, Pallas kernels, hidden_first(): pl.pallas_call(first_kernel, out_shape=(jax.ShapeDtypeStruct((288, 896),...  9.94 us
    all_to_all x1, starting transfers between devices, body(): lax.all_to_all(summed, 'expert', split_axis=0, concat_axis=0, tiled=True)  9.45 us
    pallas_call x2, Pallas kernels, down(): pl.pallas_call(functools.partial(down_kernel, swap), out_shape=[jax.Shape...  6.76 us
    all_to_all x1, waiting for transfers between devices, body(): lax.all_to_all(slots.reshape(8, 32, 512), 'expert', split_axis=0, concat_...  6.49 us
  transfers between devices with their start and end apart: 41, of which 16 were waited for; matrix products, arithmetic and copies ran while one was open for 3% of the time, Pallas kernels for 17%

profile of v5, /device:TPU:1, one launch (start us, length us, event | category | flops | bytes accessed | tf_op | source)
XLA Modules:
  0.0 184.5 jit_solution(18426501850503959860)
XLA Ops:
  15.0 4.5 %attend.4.a = bf16[4,64,640]{2,1,0:T(8,128)(2,1)S(1)} custom-call(bf16[4,64,640]{2,1,0:T(8,128)(2,1)S(1)} %pad_maximum_fusion.3.q_ref, bf16[128,128]{1,0:T(8,128)(2,1)S(1)} %pad.5.table_ref, bf16[256,2304]{1,0:T(8,128)(2,1)S(1)} %pad_maximum_fusion.kt_ref, bf16[2304,256]{1,0:T(8,128)(2,1)S(1)} %concatenate.14.v_ref), custom_call_target="tpu_custom_call" | custom-call | tf_op jit(solution)/shard_map/attend/pallas_call | solution.py:76
  24.0 4.5 %attend.7 = bf16[4,64,640]{2,1,0:T(8,128)(2,1)S(1)} custom-call(bf16[4,64,640]{2,1,0:T(8,128)(2,1)S(1)} %collective-permute-done.4.q_ref, bf16[128,128]{1,0:T(8,128)(2,1)S(1)} %pad.5.table_ref, bf16[256,2304]{1,0:T(8,128)(2,1)S(1)} %pad_maximum_fusion.kt_ref, bf16[2304,256]{1,0:T(8,128)(2,1)S(1)} %concatenate.14.v_ref), custom_call_target="tpu_custom_call" | custom-call | tf_op jit(solution)/shard_map/attend/pallas_call | solution.py:76
  28.5 4.5 %attend.5 = bf16[4,64,640]{2,1,0:T(8,128)(2,1)S(1)} custom-call(bf16[4,64,640]{2,1,0:T(8,128)(2,1)S(1)} %collective-permute-done.3.q_ref, bf16[128,128]{1,0:T(8,128)(2,1)S(1)} %pad.5.table_ref, bf16[256,2304]{1,0:T(8,128)(2,1)S(1)} %pad_maximum_fusion.kt_ref, bf16[2304,256]{1,0:T(8,128)(2,1)S(1)} %concatenate.14.v_ref), custom_call_target="tpu_custom_call" | custom-call | tf_op jit(solution)/shard_map/attend/pallas_call | solution.py:76
  33.1 2.7 %collective-permute-start.5 = (bf16[4,64,640]{2,1,0:T(8,128)(2,1)S(1)}, bf16[4,64,640]{2,1,0:T(8,128)(2,1)S(1)}, u32[]{:S(2)}, u32[]{:S(2)}) collective-permute-start(bf16[4,64,640]{2,1,0:T(8,128)(2,1)S(1)} %attend.5), channel_id=1, source_target_pairs={{0,96},{8,104},{16,112},{24,120},{32,0},{40,8},{48,16},{56,24},{64... | collective-permute-start | bytes 983048 | tf_op jit(solution)/shard_map/ppermute | solution.py:38
  35.8 4.5 %attend.6 = bf16[4,64,640]{2,1,0:T(8,128)(2,1)S(1)} custom-call(bf16[4,64,640]{2,1,0:T(8,128)(2,1)S(1)} %pad_maximum_fusion.4.q_ref, bf16[128,128]{1,0:T(8,128)(2,1)S(1)} %pad.5.table_ref, bf16[256,2304]{1,0:T(8,128)(2,1)S(1)} %pad_maximum_fusion.kt_ref, bf16[2304,256]{1,0:T(8,128)(2,1)S(1)} %concatenate.14.v_ref), custom_call_target="tpu_custom_call" | custom-call | tf_op jit(solution)/shard_map/attend/pallas_call | solution.py:76
  40.5 7.4 %collective-permute-done.8.c = bf16[4,64,640]{2,1,0:T(8,128)(2,1)S(1)} collective-permute-done((bf16[4,64,640]{2,1,0:T(8,128)(2,1)S(1)}, bf16[4,64,640]{2,1,0:T(8,128)(2,1)S(1)}, u32[]{:S(2)}, u32[]{:S(2)}) %collective-permute-start.8) | collective-permute-done | bytes 327712 | tf_op jit(solution)/shard_map/ppermute | solution.py:38
  57.7 11.7 %all-to-all-start = ((bf16[8,32,512]{2,1,0:T(8,128)(2,1)}), bf16[8,32,512]{2,1,0:T(8,128)(2,1)S(1)}, u32[]{:S(2)}, u32[]{:S(2)}) async-start(bf16[8,32,512]{2,1,0:T(8,128)(2,1)} %bitcast.12), calls=%async_computation | async-start | bytes 524288 | tf_op jit(solution)/shard_map/all_to_all | solution.py:401
  69.4 6.5 %all-to-all-done.x_ref = bf16[8,32,512]{2,1,0:T(8,128)(2,1)S(1)} async-done(((bf16[8,32,512]{2,1,0:T(8,128)(2,1)}), bf16[8,32,512]{2,1,0:T(8,128)(2,1)S(1)}, u32[]{:S(2)}, u32[]{:S(2)}) %all-to-all-start) | async-done | bytes 262176 | tf_op jit(solution)/shard_map/all_to_all | solution.py:401
  79.1 3.0 %collective-permute-start.17 = (bf16[32,2048]{1,0:T(8,128)(2,1)S(1)}, bf16[32,2048]{1,0:T(8,128)(2,1)S(1)}, u32[]{:S(2)}, u32[]{:S(2)}) collective-permute-start(bf16[32,2048]{1,0:T(8,128)(2,1)S(1)} %get-tuple-element.55), channel_id=1, source_target_pairs={{0,64},{8,72},{16,80},{24,88},{32,96},{40,104},{48,112},{56,120},{... | collective-permute-start | bytes 393224 | tf_op jit(solution)/shard_map/ppermute | solution.py:38
  86.2 2.7 %collective-permute-done.18 = bf16[32,2048]{1,0:T(8,128)(2,1)S(1)} collective-permute-done((bf16[32,2048]{1,0:T(8,128)(2,1)S(1)}, bf16[32,2048]{1,0:T(8,128)(2,1)S(1)}, u32[]{:S(2)}, u32[]{:S(2)}) %collective-permute-start.18) | collective-permute-done | bytes 131104 | tf_op jit(solution)/shard_map/ppermute | solution.py:38
  94.6 7.0 %collective-permute-done.21.h1 = bf16[4,32,2048]{2,1,0:T(8,128)(2,1)S(1)} collective-permute-done((bf16[4,32,2048]{2,1,0:T(8,128)(2,1)S(1)}, bf16[4,32,2048]{2,1,0:T(8,128)(2,1)S(1)}, u32[]{:S(2)}, u32[]{:S(2)}) %collective-permute-start.21) | collective-permute-done | bytes 524320 | tf_op jit(solution)/shard_map/ppermute | solution.py:38
  101.8 2.7 %collective-permute-start.26 = (bf16[2,32,2048]{2,1,0:T(8,128)(2,1)S(1)}, bf16[2,32,2048]{2,1,0:T(8,128)(2,1)S(1)}, u32[]{:S(2)}, u32[]{:S(2)}) collective-permute-start(bf16[2,32,2048]{2,1,0:T(8,128)(2,1)S(1)} %slice.27), channel_id=1, source_target_pairs={{0,24},{8,0},{16,8},{24,16},{32,56},{40,32},{48,40},{56,48},{64,88... | collective-permute-start | bytes 786440 | tf_op jit(solution)/shard_map/ppermute | solution.py:38
  104.6 2.9 %collective-permute-start.24 = (bf16[2,32,2048]{2,1,0:T(8,128)(2,1)S(1)}, bf16[2,32,2048]{2,1,0:T(8,128)(2,1)S(1)}, u32[]{:S(2)}, u32[]{:S(2)}) collective-permute-start(bf16[2,32,2048]{2,1,0:T(8,128)(2,1)S(1)} %slice.25), channel_id=1, source_target_pairs={{0,96},{8,104},{16,112},{24,120},{32,0},{40,8},{48,16},{56,24},{64... | collective-permute-start | bytes 786440 | tf_op jit(solution)/shard_map/ppermute | solution.py:38
  107.6 9.9 %hidden_first.1 = (bf16[288,896]{1,0:T(8,128)(2,1)S(1)}, bf16[7,4096,256]{2,1,0:T(8,128)(2,1)S(1)}) custom-call(bf16[4,32,2048]{2,1,0:T(8,128)(2,1)S(1)} %pad_maximum_fusion.1.l0, bf16[4,32,2048]{2,1,0:T(8,128)(2,1)S(1)} %collective-permute-done.19.l1, bf16[4,32,2048]{2,1,0:T(8,128)(2,1)S(1)} %collective-permute-done.20.l3, ...), custom_call_target="tpu_custom_call" | custom-call | tf_op jit(solution)/shard_map/hidden_first/pallas_call | solution.py:213
  117.6 5.2 %hidden_second.1.late_ref = bf16[224,896]{1,0:T(8,128)(2,1)S(1)} custom-call(bf16[4,32,2048]{2,1,0:T(8,128)(2,1)S(1)} %pad_maximum_fusion.1.l0, bf16[4,32,2048]{2,1,0:T(8,128)(2,1)S(1)} %collective-permute-done.19.l1, bf16[4,32,2048]{2,1,0:T(8,128)(2,1)S(1)} %collective-permute-done.20.l3, bf16[4,32,2048]{2,1,0:T(8,128)(2,1)S(1)} %pad_maximum_fusion.2.h0, ...), custom_call_target="tpu_custom_call" | custom-call | tf_op jit(solution)/shard_map/hidden_second/pallas_call | solution.py:232
  122.8 3.4 %down_high.1 = (bf16[128,2048]{1,0:T(8,128)(2,1)S(1)}, bf16[128,2048]{1,0:T(8,128)(2,1)S(1)}, bf16[128,2048]{1,0:T(8,128)(2,1)S(1)}, bf16[128,2048]{1,0:T(8,128)(2,1)S(1)}) custom-call(bf16[288,896]{1,0:T(8,128)(2,1)S(1)} %get-tuple-element.59.early_ref, bf16[224,896]{1,0:T(8,128)(2,1)S(1)} %hidden_second.1.late_ref, bf16[1,896,4096]{2,1,0:T(8,128)(2,1)S(1)} %bitcast.31), custom_call_target="tpu_custom_call" | custom-call | tf_op jit(solution)/shard_map/down_high/pallas_call | solution.py:260
  127.8 3.4 %down_low.1 = (bf16[128,2048]{1,0:T(8,128)(2,1)S(1)}, bf16[128,2048]{1,0:T(8,128)(2,1)S(1)}, bf16[128,2048]{1,0:T(8,128)(2,1)S(1)}, bf16[128,2048]{1,0:T(8,128)(2,1)S(1)}) custom-call(bf16[288,896]{1,0:T(8,128)(2,1)S(1)} %get-tuple-element.59.early_ref, bf16[224,896]{1,0:T(8,128)(2,1)S(1)} %hidden_second.1.late_ref, bf16[1,896,4096]{2,1,0:T(8,128)(2,1)S(1)} %bitcast.31), custom_call_target="tpu_custom_call" | custom-call | tf_op jit(solution)/shard_map/down_low/pallas_call | solution.py:260
  132.0 3.6 %collective-permute-done.33.b = bf16[128,2048]{1,0:T(8,128)(2,1)S(1)} collective-permute-done((bf16[128,2048]{1,0:T(8,128)(2,1)S(1)}, bf16[128,2048]{1,0:T(8,128)(2,1)S(1)}, u32[]{:S(2)}, u32[]{:S(2)}) %collective-permute-start.33) | collective-permute-done | bytes 524320 | tf_op jit(solution)/shard_map/ppermute | solution.py:38
  137.3 15.7 %collective-permute-done.35.d = bf16[128,2048]{1,0:T(8,128)(2,1)S(1)} collective-permute-done((bf16[128,2048]{1,0:T(8,128)(2,1)S(1)}, bf16[128,2048]{1,0:T(8,128)(2,1)S(1)}, u32[]{:S(2)}, u32[]{:S(2)}) %collective-permute-start.35) | collective-permute-done | bytes 524320 | tf_op jit(solution)/shard_map/ppermute | solution.py:38
  155.6 3.2 %collective-permute-start.30 = (bf16[32,2048]{1,0:T(8,128)(2,1)S(1)}, bf16[32,2048]{1,0:T(8,128)(2,1)S(1)}, u32[]{:S(2)}, u32[]{:S(2)}) collective-permute-start(bf16[32,2048]{1,0:T(8,128)(2,1)S(1)} %get-tuple-element.66), channel_id=1, source_target_pairs={{0,24},{8,0},{16,8},{24,16},{32,56},{40,32},{48,40},{56,48},{64,88... | collective-permute-start | bytes 393224 | tf_op jit(solution)/shard_map/ppermute | solution.py:38
  158.8 3.1 %collective-permute-start.31 = (bf16[32,2048]{1,0:T(8,128)(2,1)S(1)}, bf16[32,2048]{1,0:T(8,128)(2,1)S(1)}, u32[]{:S(2)}, u32[]{:S(2)}) collective-permute-start(bf16[32,2048]{1,0:T(8,128)(2,1)S(1)} %get-tuple-element.67), channel_id=1, source_target_pairs={{0,16},{8,24},{16,0},{24,8},{32,48},{40,56},{48,32},{56,40},{64,80... | collective-permute-start | bytes 393224 | tf_op jit(solution)/shard_map/ppermute | solution.py:38
  164.2 2.7 %collective-permute-done.32.refs_3_ = bf16[32,2048]{1,0:T(8,128)(2,1)S(1)} collective-permute-done((bf16[32,2048]{1,0:T(8,128)(2,1)S(1)}, bf16[32,2048]{1,0:T(8,128)(2,1)S(1)}, u32[]{:S(2)}, u32[]{:S(2)}) %collective-permute-start.32) | collective-permute-done | bytes 131104 | tf_op jit(solution)/shard_map/ppermute | solution.py:38
  167.7 9.4 %all-to-all-start.1 = ((bf16[8,32,512]{2,1,0:T(8,128)(2,1)}), bf16[8,32,512]{2,1,0:T(8,128)(2,1)S(1)}, u32[]{:S(2)}, u32[]{:S(2)}) async-start(bf16[8,32,512]{2,1,0:T(8,128)(2,1)} %add_last.1), calls=%async_computation.1 | async-start | bytes 524288 | tf_op jit(solution)/shard_map/all_to_all | solution.py:416
  177.6 6.1 %all-to-all-done.1 = bf16[8,32,512]{2,1,0:T(8,128)(2,1)S(1)} async-done(((bf16[8,32,512]{2,1,0:T(8,128)(2,1)}), bf16[8,32,512]{2,1,0:T(8,128)(2,1)S(1)}, u32[]{:S(2)}, u32[]{:S(2)}) %all-to-all-start.1) | async-done | bytes 262176 | tf_op jit(solution)/shard_map/all_to_all | solution.py:416
  (124 shorter events, 52.9 us)
Async XLA Ops:
  2.3 9.8 %collective-permute-start = (bf16[64,640]{1,0:T(8,128)(2,1)S(1)}, bf16[64,640]{1,0:T(8,128)(2,1)S(1)}, u32[]{:S(2)}, u32[]{:S(2)}) collective-permute-start(bf16[64,640]{1,0:T(8,128)(2,1)S(1)} %get-tuple-element.79), channel_id=1, source_target_pairs={{0,8},{8,16},{16,24},{24,0},{32,40},{40,48},{48,56},{56,32},{64,72... | collective-permute-start | bytes 245768 | tf_op jit(solution)/shard_map/ppermute | solution.py:38
  12.2 9.0 %collective-permute-start.3 = (bf16[4,64,640]{2,1,0:T(8,128)(2,1)S(1)}, bf16[4,64,640]{2,1,0:T(8,128)(2,1)S(1)}, u32[]{:S(2)}, u32[]{:S(2)}) collective-permute-start(bf16[4,64,640]{2,1,0:T(8,128)(2,1)S(1)} %pad_maximum_fusion.3.q_ref), channel_id=1, source_target_pairs={{0,32},{8,40},{16,48},{24,56},{32,64},{40,72},{48,80},{56,88},{64,... | collective-permute-start | bytes 983048 | tf_op jit(solution)/shard_map/ppermute | solution.py:38
  21.2 14.6 %collective-permute-start.6 = (bf16[2,64,640]{2,1,0:T(8,128)(2,1)S(1)}, bf16[2,64,640]{2,1,0:T(8,128)(2,1)S(1)}, u32[]{:S(2)}, u32[]{:S(2)}) collective-permute-start(bf16[2,64,640]{2,1,0:T(8,128)(2,1)S(1)} %slice.18), channel_id=1, source_target_pairs={{0,32},{8,40},{16,48},{24,56},{32,64},{40,72},{48,80},{56,88},{64,... | collective-permute-start | bytes 491528 | tf_op jit(solution)/shard_map/ppermute | solution.py:38
  22.2 13.6 %collective-permute-start.7 = (bf16[2,64,640]{2,1,0:T(8,128)(2,1)S(1)}, bf16[2,64,640]{2,1,0:T(8,128)(2,1)S(1)}, u32[]{:S(2)}, u32[]{:S(2)}) collective-permute-start(bf16[2,64,640]{2,1,0:T(8,128)(2,1)S(1)} %slice.19), channel_id=1, source_target_pairs={{0,96},{8,104},{16,112},{24,120},{32,0},{40,8},{48,16},{56,24},{64... | collective-permute-start | bytes 491528 | tf_op jit(solution)/shard_map/ppermute | solution.py:38
  57.7 18.2 %all-to-all-start = ((bf16[8,32,512]{2,1,0:T(8,128)(2,1)}), bf16[8,32,512]{2,1,0:T(8,128)(2,1)S(1)}, u32[]{:S(2)}, u32[]{:S(2)}) async-start(bf16[8,32,512]{2,1,0:T(8,128)(2,1)} %bitcast.12), calls=%async_computation | async-start | bytes 524288 | tf_op jit(solution)/shard_map/all_to_all | solution.py:401
  76.2 9.3 %collective-permute-start.14 = (bf16[32,2048]{1,0:T(8,128)(2,1)S(1)}, bf16[32,2048]{1,0:T(8,128)(2,1)S(1)}, u32[]{:S(2)}, u32[]{:S(2)}) collective-permute-start(bf16[32,2048]{1,0:T(8,128)(2,1)S(1)} %get-tuple-element.51), channel_id=1, source_target_pairs={{0,16},{8,24},{16,0},{24,8},{32,48},{40,56},{48,32},{56,40},{64,80... | collective-permute-start | bytes 393224 | tf_op jit(solution)/shard_map/ppermute | solution.py:38
  89.0 12.6 %collective-permute-start.21 = (bf16[4,32,2048]{2,1,0:T(8,128)(2,1)S(1)}, bf16[4,32,2048]{2,1,0:T(8,128)(2,1)S(1)}, u32[]{:S(2)}, u32[]{:S(2)}) collective-permute-start(bf16[4,32,2048]{2,1,0:T(8,128)(2,1)S(1)} %pad_maximum_fusion.2.h0), channel_id=1, source_target_pairs={{0,8},{8,16},{16,24},{24,0},{32,40},{40,48},{48,56},{56,32},{64,72... | collective-permute-start | bytes 1572872 | tf_op jit(solution)/shard_map/ppermute | solution.py:38
  89.1 12.6 %collective-permute-start.22 = (bf16[4,32,2048]{2,1,0:T(8,128)(2,1)S(1)}, bf16[4,32,2048]{2,1,0:T(8,128)(2,1)S(1)}, u32[]{:S(2)}, u32[]{:S(2)}) collective-permute-start(bf16[4,32,2048]{2,1,0:T(8,128)(2,1)S(1)} %pad_maximum_fusion.2.h0), channel_id=1, source_target_pairs={{0,24},{8,0},{16,8},{24,16},{32,56},{40,32},{48,40},{56,48},{64,88... | collective-permute-start | bytes 1572872 | tf_op jit(solution)/shard_map/ppermute | solution.py:38
  91.8 12.6 %collective-permute-start.19 = (bf16[4,32,2048]{2,1,0:T(8,128)(2,1)S(1)}, bf16[4,32,2048]{2,1,0:T(8,128)(2,1)S(1)}, u32[]{:S(2)}, u32[]{:S(2)}) collective-permute-start(bf16[4,32,2048]{2,1,0:T(8,128)(2,1)S(1)} %pad_maximum_fusion.1.l0), channel_id=1, source_target_pairs={{0,32},{8,40},{16,48},{24,56},{32,64},{40,72},{48,80},{56,88},{64,... | collective-permute-start | bytes 1572872 | tf_op jit(solution)/shard_map/ppermute | solution.py:38
  91.9 12.7 %collective-permute-start.20 = (bf16[4,32,2048]{2,1,0:T(8,128)(2,1)S(1)}, bf16[4,32,2048]{2,1,0:T(8,128)(2,1)S(1)}, u32[]{:S(2)}, u32[]{:S(2)}) collective-permute-start(bf16[4,32,2048]{2,1,0:T(8,128)(2,1)S(1)} %pad_maximum_fusion.1.l0), channel_id=1, source_target_pairs={{0,96},{8,104},{16,112},{24,120},{32,0},{40,8},{48,16},{56,24},{64... | collective-permute-start | bytes 1572872 | tf_op jit(solution)/shard_map/ppermute | solution.py:38
  101.6 15.9 %collective-permute-start.25 = (bf16[2,32,2048]{2,1,0:T(8,128)(2,1)S(1)}, bf16[2,32,2048]{2,1,0:T(8,128)(2,1)S(1)}, u32[]{:S(2)}, u32[]{:S(2)}) collective-permute-start(bf16[2,32,2048]{2,1,0:T(8,128)(2,1)S(1)} %slice.26), channel_id=1, source_target_pairs={{0,8},{8,16},{16,24},{24,0},{32,40},{40,48},{48,56},{56,32},{64,72... | collective-permute-start | bytes 786440 | tf_op jit(solution)/shard_map/ppermute | solution.py:38
  101.8 15.8 %collective-permute-start.26 = (bf16[2,32,2048]{2,1,0:T(8,128)(2,1)S(1)}, bf16[2,32,2048]{2,1,0:T(8,128)(2,1)S(1)}, u32[]{:S(2)}, u32[]{:S(2)}) collective-permute-start(bf16[2,32,2048]{2,1,0:T(8,128)(2,1)S(1)} %slice.27), channel_id=1, source_target_pairs={{0,24},{8,0},{16,8},{24,16},{32,56},{40,32},{48,40},{56,48},{64,88... | collective-permute-start | bytes 786440 | tf_op jit(solution)/shard_map/ppermute | solution.py:38
  104.5 13.0 %collective-permute-start.23 = (bf16[2,32,2048]{2,1,0:T(8,128)(2,1)S(1)}, bf16[2,32,2048]{2,1,0:T(8,128)(2,1)S(1)}, u32[]{:S(2)}, u32[]{:S(2)}) collective-permute-start(bf16[2,32,2048]{2,1,0:T(8,128)(2,1)S(1)} %slice.24), channel_id=1, source_target_pairs={{0,32},{8,40},{16,48},{24,56},{32,64},{40,72},{48,80},{56,88},{64,... | collective-permute-start | bytes 786440 | tf_op jit(solution)/shard_map/ppermute | solution.py:38
  104.6 12.9 %collective-permute-start.24 = (bf16[2,32,2048]{2,1,0:T(8,128)(2,1)S(1)}, bf16[2,32,2048]{2,1,0:T(8,128)(2,1)S(1)}, u32[]{:S(2)}, u32[]{:S(2)}) collective-permute-start(bf16[2,32,2048]{2,1,0:T(8,128)(2,1)S(1)} %slice.25), channel_id=1, source_target_pairs={{0,96},{8,104},{16,112},{24,120},{32,0},{40,8},{48,16},{56,24},{64... | collective-permute-start | bytes 786440 | tf_op jit(solution)/shard_map/ppermute | solution.py:38
  126.2 9.3 %collective-permute-start.33 = (bf16[128,2048]{1,0:T(8,128)(2,1)S(1)}, bf16[128,2048]{1,0:T(8,128)(2,1)S(1)}, u32[]{:S(2)}, u32[]{:S(2)}) collective-permute-start(bf16[128,2048]{1,0:T(8,128)(2,1)S(1)} %get-tuple-element.70), channel_id=1, source_target_pairs={{0,24},{8,0},{16,8},{24,16},{32,56},{40,32},{48,40},{56,48},{64,88... | collective-permute-start | bytes 1572872 | tf_op jit(solution)/shard_map/ppermute | solution.py:38
  126.3 10.9 %collective-permute-start.34 = (bf16[128,2048]{1,0:T(8,128)(2,1)S(1)}, bf16[128,2048]{1,0:T(8,128)(2,1)S(1)}, u32[]{:S(2)}, u32[]{:S(2)}) collective-permute-start(bf16[128,2048]{1,0:T(8,128)(2,1)S(1)} %get-tuple-element.71), channel_id=1, source_target_pairs={{0,16},{8,24},{16,0},{24,8},{32,48},{40,56},{48,32},{56,40},{64,80... | collective-permute-start | bytes 1572872 | tf_op jit(solution)/shard_map/ppermute | solution.py:38
  126.9 26.1 %collective-permute-start.35 = (bf16[128,2048]{1,0:T(8,128)(2,1)S(1)}, bf16[128,2048]{1,0:T(8,128)(2,1)S(1)}, u32[]{:S(2)}, u32[]{:S(2)}) collective-permute-start(bf16[128,2048]{1,0:T(8,128)(2,1)S(1)} %get-tuple-element.72), channel_id=1, source_target_pairs={{0,8},{8,16},{16,24},{24,0},{32,40},{40,48},{48,56},{56,32},{64,72... | collective-permute-start | bytes 1572872 | tf_op jit(solution)/shard_map/ppermute | solution.py:38
  131.2 23.2 %collective-permute-start.27 = (bf16[128,2048]{1,0:T(8,128)(2,1)S(1)}, bf16[128,2048]{1,0:T(8,128)(2,1)S(1)}, u32[]{:S(2)}, u32[]{:S(2)}) collective-permute-start(bf16[128,2048]{1,0:T(8,128)(2,1)S(1)} %get-tuple-element.62), channel_id=1, source_target_pairs={{0,96},{8,104},{16,112},{24,120},{32,0},{40,8},{48,16},{56,24},{64... | collective-permute-start | bytes 1572872 | tf_op jit(solution)/shard_map/ppermute | solution.py:38
  132.0 23.0 %collective-permute-start.28 = (bf16[128,2048]{1,0:T(8,128)(2,1)S(1)}, bf16[128,2048]{1,0:T(8,128)(2,1)S(1)}, u32[]{:S(2)}, u32[]{:S(2)}) collective-permute-start(bf16[128,2048]{1,0:T(8,128)(2,1)S(1)} %get-tuple-element.63), channel_id=1, source_target_pairs={{0,64},{8,72},{16,80},{24,88},{32,96},{40,104},{48,112},{56,120},{... | collective-permute-start | bytes 1572872 | tf_op jit(solution)/shard_map/ppermute | solution.py:38
  135.6 19.5 %collective-permute-start.29 = (bf16[128,2048]{1,0:T(8,128)(2,1)S(1)}, bf16[128,2048]{1,0:T(8,128)(2,1)S(1)}, u32[]{:S(2)}, u32[]{:S(2)}) collective-permute-start(bf16[128,2048]{1,0:T(8,128)(2,1)S(1)} %get-tuple-element.64), channel_id=1, source_target_pairs={{0,32},{8,40},{16,48},{24,56},{32,64},{40,72},{48,80},{56,88},{64,... | collective-permute-start | bytes 1572872 | tf_op jit(solution)/shard_map/ppermute | solution.py:38
  153.5 8.4 %collective-permute-start.36 = (bf16[32,2048]{1,0:T(8,128)(2,1)S(1)}, bf16[32,2048]{1,0:T(8,128)(2,1)S(1)}, u32[]{:S(2)}, u32[]{:S(2)}) collective-permute-start(bf16[32,2048]{1,0:T(8,128)(2,1)S(1)} %get-tuple-element.74), channel_id=1, source_target_pairs={{0,96},{8,104},{16,112},{24,120},{32,0},{40,8},{48,16},{56,24},{64... | collective-permute-start | bytes 393224 | tf_op jit(solution)/shard_map/ppermute | solution.py:38
  154.3 9.8 %collective-permute-start.38 = (bf16[32,2048]{1,0:T(8,128)(2,1)S(1)}, bf16[32,2048]{1,0:T(8,128)(2,1)S(1)}, u32[]{:S(2)}, u32[]{:S(2)}) collective-permute-start(bf16[32,2048]{1,0:T(8,128)(2,1)S(1)} %get-tuple-element.76), channel_id=1, source_target_pairs={{0,32},{8,40},{16,48},{24,56},{32,64},{40,72},{48,80},{56,88},{64,... | collective-permute-start | bytes 393224 | tf_op jit(solution)/shard_map/ppermute | solution.py:38
  155.6 8.6 %collective-permute-start.30 = (bf16[32,2048]{1,0:T(8,128)(2,1)S(1)}, bf16[32,2048]{1,0:T(8,128)(2,1)S(1)}, u32[]{:S(2)}, u32[]{:S(2)}) collective-permute-start(bf16[32,2048]{1,0:T(8,128)(2,1)S(1)} %get-tuple-element.66), channel_id=1, source_target_pairs={{0,24},{8,0},{16,8},{24,16},{32,56},{40,32},{48,40},{56,48},{64,88... | collective-permute-start | bytes 393224 | tf_op jit(solution)/shard_map/ppermute | solution.py:38
  167.7 16.0 %all-to-all-start.1 = ((bf16[8,32,512]{2,1,0:T(8,128)(2,1)}), bf16[8,32,512]{2,1,0:T(8,128)(2,1)S(1)}, u32[]{:S(2)}, u32[]{:S(2)}) async-start(bf16[8,32,512]{2,1,0:T(8,128)(2,1)} %add_last.1), calls=%async_computation.1 | async-start | bytes 524288 | tf_op jit(solution)/shard_map/all_to_all | solution.py:416
  (24 other events, 233.0 us)

commit v6 on v5

--- a/solution.py
+++ b/solution.py
@@ -256,19 +256,19 @@
 
 
 def down(early, late, w_down, swap):
-    offset = 4 if swap else 0
+    offset = 2 if swap else 0
     return pl.pallas_call(
         functools.partial(down_kernel, swap),
         out_shape=[jax.ShapeDtypeStruct((128, 2048), BF)] * 4,
-        grid=(4,),
+        grid=(2,),
         in_specs=[
             whole_once(early.shape),
             whole_once(late.shape),
-            pl.BlockSpec((1, 896, 512), lambda i: (0, 0, i + offset)),
+            pl.BlockSpec((1, 896, 1024), lambda i: (0, 0, i + offset)),
         ],
-        out_specs=[pl.BlockSpec((128, 512), lambda i: (0, i))] * 4,
+        out_specs=[pl.BlockSpec((128, 1024), lambda i: (0, i))] * 4,
         scratch_shapes=[pltpu.VMEM((512, 896), BF)],
-        compiler_params=room(12),
+        compiler_params=room(14),
         name="down_high" if swap else "down_low",
     )(early, late, w_down)
 

time: 185 us -> 184 us (level)
  no operation moved by 1% of the time
where the time goes in v6:
time: 184 us
  starting transfers between devices  67.4 us (37%)
  waiting for transfers between devices  63.5 us (35%)
  Pallas kernels  45 us (24%)
  other arithmetic  4.5 us (2%)
  local copies, waits for them, and re-layouts  2.04 us (1%)
    ppermute x39, waiting for transfers between devices, shift_dp(): return lax.ppermute(value, 'dp', ring_pairs(axis, shift))  50.9 us
    ppermute x39, starting transfers between devices, shift_dp(): return lax.ppermute(value, 'dp', ring_pairs(axis, shift))  45.4 us
    pallas_call x4, Pallas kernels, attend(): pl.pallas_call(attend_kernel, out_shape=jax.ShapeDtypeStruct((4, 64, 640)...  18 us
    all_to_all x1, starting transfers between devices, body(): lax.all_to_all(slots.reshape(8, 32, 512), 'expert', split_axis=0, concat_...  11.7 us
    all_to_all x1, starting transfers between devices, body(): lax.all_to_all(summed, 'expert', split_axis=0, concat_axis=0, tiled=True)  10.2 us
    pallas_call x1, Pallas kernels, hidden_first(): pl.pallas_call(first_kernel, out_shape=(jax.ShapeDtypeStruct((288, 896),...  9.94 us
    all_to_all x1, waiting for transfers between devices, body(): lax.all_to_all(slots.reshape(8, 32, 512), 'expert', split_axis=0, concat_...  6.49 us
    all_to_all x1, waiting for transfers between devices, body(): lax.all_to_all(summed, 'expert', split_axis=0, concat_axis=0, tiled=True)  6.14 us
  transfers between devices with their start and end apart: 41, of which 16 were waited for; matrix products, arithmetic and copies ran while one was open for 3% of the time, Pallas kernels for 17%

profile of v6, /device:TPU:1, one launch (start us, length us, event | category | flops | bytes accessed | tf_op | source)
XLA Modules:
  0.0 183.7 jit_solution(7140858599136974155)
XLA Ops:
  15.0 4.5 %attend.4.a = bf16[4,64,640]{2,1,0:T(8,128)(2,1)S(1)} custom-call(bf16[4,64,640]{2,1,0:T(8,128)(2,1)S(1)} %pad_maximum_fusion.3.q_ref, bf16[128,128]{1,0:T(8,128)(2,1)S(1)} %pad.5.table_ref, bf16[256,2304]{1,0:T(8,128)(2,1)S(1)} %pad_maximum_fusion.kt_ref, bf16[2304,256]{1,0:T(8,128)(2,1)S(1)} %concatenate.14.v_ref), custom_call_target="tpu_custom_call" | custom-call | tf_op jit(solution)/shard_map/attend/pallas_call | solution.py:76
  24.0 4.5 %attend.7 = bf16[4,64,640]{2,1,0:T(8,128)(2,1)S(1)} custom-call(bf16[4,64,640]{2,1,0:T(8,128)(2,1)S(1)} %collective-permute-done.4.q_ref, bf16[128,128]{1,0:T(8,128)(2,1)S(1)} %pad.5.table_ref, bf16[256,2304]{1,0:T(8,128)(2,1)S(1)} %pad_maximum_fusion.kt_ref, bf16[2304,256]{1,0:T(8,128)(2,1)S(1)} %concatenate.14.v_ref), custom_call_target="tpu_custom_call" | custom-call | tf_op jit(solution)/shard_map/attend/pallas_call | solution.py:76
  28.5 4.5 %attend.5 = bf16[4,64,640]{2,1,0:T(8,128)(2,1)S(1)} custom-call(bf16[4,64,640]{2,1,0:T(8,128)(2,1)S(1)} %collective-permute-done.3.q_ref, bf16[128,128]{1,0:T(8,128)(2,1)S(1)} %pad.5.table_ref, bf16[256,2304]{1,0:T(8,128)(2,1)S(1)} %pad_maximum_fusion.kt_ref, bf16[2304,256]{1,0:T(8,128)(2,1)S(1)} %concatenate.14.v_ref), custom_call_target="tpu_custom_call" | custom-call | tf_op jit(solution)/shard_map/attend/pallas_call | solution.py:76
  33.1 2.7 %collective-permute-start.5 = (bf16[4,64,640]{2,1,0:T(8,128)(2,1)S(1)}, bf16[4,64,640]{2,1,0:T(8,128)(2,1)S(1)}, u32[]{:S(2)}, u32[]{:S(2)}) collective-permute-start(bf16[4,64,640]{2,1,0:T(8,128)(2,1)S(1)} %attend.5), channel_id=1, source_target_pairs={{0,96},{8,104},{16,112},{24,120},{32,0},{40,8},{48,16},{56,24},{64... | collective-permute-start | bytes 983048 | tf_op jit(solution)/shard_map/ppermute | solution.py:38
  35.8 4.5 %attend.6 = bf16[4,64,640]{2,1,0:T(8,128)(2,1)S(1)} custom-call(bf16[4,64,640]{2,1,0:T(8,128)(2,1)S(1)} %pad_maximum_fusion.4.q_ref, bf16[128,128]{1,0:T(8,128)(2,1)S(1)} %pad.5.table_ref, bf16[256,2304]{1,0:T(8,128)(2,1)S(1)} %pad_maximum_fusion.kt_ref, bf16[2304,256]{1,0:T(8,128)(2,1)S(1)} %concatenate.14.v_ref), custom_call_target="tpu_custom_call" | custom-call | tf_op jit(solution)/shard_map/attend/pallas_call | solution.py:76
  40.5 7.4 %collective-permute-done.8.c = bf16[4,64,640]{2,1,0:T(8,128)(2,1)S(1)} collective-permute-done((bf16[4,64,640]{2,1,0:T(8,128)(2,1)S(1)}, bf16[4,64,640]{2,1,0:T(8,128)(2,1)S(1)}, u32[]{:S(2)}, u32[]{:S(2)}) %collective-permute-start.8) | collective-permute-done | bytes 327712 | tf_op jit(solution)/shard_map/ppermute | solution.py:38
  57.7 11.7 %all-to-all-start = ((bf16[8,32,512]{2,1,0:T(8,128)(2,1)}), bf16[8,32,512]{2,1,0:T(8,128)(2,1)S(1)}, u32[]{:S(2)}, u32[]{:S(2)}) async-start(bf16[8,32,512]{2,1,0:T(8,128)(2,1)} %bitcast.12), calls=%async_computation | async-start | bytes 524288 | tf_op jit(solution)/shard_map/all_to_all | solution.py:401
  69.4 6.5 %all-to-all-done.x_ref = bf16[8,32,512]{2,1,0:T(8,128)(2,1)S(1)} async-done(((bf16[8,32,512]{2,1,0:T(8,128)(2,1)}), bf16[8,32,512]{2,1,0:T(8,128)(2,1)S(1)}, u32[]{:S(2)}, u32[]{:S(2)}) %all-to-all-start) | async-done | bytes 262176 | tf_op jit(solution)/shard_map/all_to_all | solution.py:401
  79.1 3.0 %collective-permute-start.17 = (bf16[32,2048]{1,0:T(8,128)(2,1)S(1)}, bf16[32,2048]{1,0:T(8,128)(2,1)S(1)}, u32[]{:S(2)}, u32[]{:S(2)}) collective-permute-start(bf16[32,2048]{1,0:T(8,128)(2,1)S(1)} %get-tuple-element.55), channel_id=1, source_target_pairs={{0,64},{8,72},{16,80},{24,88},{32,96},{40,104},{48,112},{56,120},{... | collective-permute-start | bytes 393224 | tf_op jit(solution)/shard_map/ppermute | solution.py:38
  86.2 2.7 %collective-permute-done.18 = bf16[32,2048]{1,0:T(8,128)(2,1)S(1)} collective-permute-done((bf16[32,2048]{1,0:T(8,128)(2,1)S(1)}, bf16[32,2048]{1,0:T(8,128)(2,1)S(1)}, u32[]{:S(2)}, u32[]{:S(2)}) %collective-permute-start.18) | collective-permute-done | bytes 131104 | tf_op jit(solution)/shard_map/ppermute | solution.py:38
  89.1 2.7 %collective-permute-start.22 = (bf16[4,32,2048]{2,1,0:T(8,128)(2,1)S(1)}, bf16[4,32,2048]{2,1,0:T(8,128)(2,1)S(1)}, u32[]{:S(2)}, u32[]{:S(2)}) collective-permute-start(bf16[4,32,2048]{2,1,0:T(8,128)(2,1)S(1)} %pad_maximum_fusion.2.h0), channel_id=1, source_target_pairs={{0,24},{8,0},{16,8},{24,16},{32,56},{40,32},{48,40},{56,48},{64,88... | collective-permute-start | bytes 1572872 | tf_op jit(solution)/shard_map/ppermute | solution.py:38
  91.9 2.7 %collective-permute-start.20 = (bf16[4,32,2048]{2,1,0:T(8,128)(2,1)S(1)}, bf16[4,32,2048]{2,1,0:T(8,128)(2,1)S(1)}, u32[]{:S(2)}, u32[]{:S(2)}) collective-permute-start(bf16[4,32,2048]{2,1,0:T(8,128)(2,1)S(1)} %pad_maximum_fusion.1.l0), channel_id=1, source_target_pairs={{0,96},{8,104},{16,112},{24,120},{32,0},{40,8},{48,16},{56,24},{64... | collective-permute-start | bytes 1572872 | tf_op jit(solution)/shard_map/ppermute | solution.py:38
  94.6 7.0 %collective-permute-done.21.h1 = bf16[4,32,2048]{2,1,0:T(8,128)(2,1)S(1)} collective-permute-done((bf16[4,32,2048]{2,1,0:T(8,128)(2,1)S(1)}, bf16[4,32,2048]{2,1,0:T(8,128)(2,1)S(1)}, u32[]{:S(2)}, u32[]{:S(2)}) %collective-permute-start.21) | collective-permute-done | bytes 524320 | tf_op jit(solution)/shard_map/ppermute | solution.py:38
  101.8 2.7 %collective-permute-start.26 = (bf16[2,32,2048]{2,1,0:T(8,128)(2,1)S(1)}, bf16[2,32,2048]{2,1,0:T(8,128)(2,1)S(1)}, u32[]{:S(2)}, u32[]{:S(2)}) collective-permute-start(bf16[2,32,2048]{2,1,0:T(8,128)(2,1)S(1)} %slice.27), channel_id=1, source_target_pairs={{0,24},{8,0},{16,8},{24,16},{32,56},{40,32},{48,40},{56,48},{64,88... | collective-permute-start | bytes 786440 | tf_op jit(solution)/shard_map/ppermute | solution.py:38
  104.6 2.9 %collective-permute-start.24 = (bf16[2,32,2048]{2,1,0:T(8,128)(2,1)S(1)}, bf16[2,32,2048]{2,1,0:T(8,128)(2,1)S(1)}, u32[]{:S(2)}, u32[]{:S(2)}) collective-permute-start(bf16[2,32,2048]{2,1,0:T(8,128)(2,1)S(1)} %slice.25), channel_id=1, source_target_pairs={{0,96},{8,104},{16,112},{24,120},{32,0},{40,8},{48,16},{56,24},{64... | collective-permute-start | bytes 786440 | tf_op jit(solution)/shard_map/ppermute | solution.py:38
  107.6 9.9 %hidden_first.1 = (bf16[288,896]{1,0:T(8,128)(2,1)S(1)}, bf16[7,4096,256]{2,1,0:T(8,128)(2,1)S(1)}) custom-call(bf16[4,32,2048]{2,1,0:T(8,128)(2,1)S(1)} %pad_maximum_fusion.1.l0, bf16[4,32,2048]{2,1,0:T(8,128)(2,1)S(1)} %collective-permute-done.19.l1, bf16[4,32,2048]{2,1,0:T(8,128)(2,1)S(1)} %collective-permute-done.20.l3, ...), custom_call_target="tpu_custom_call" | custom-call | tf_op jit(solution)/shard_map/hidden_first/pallas_call | solution.py:213
  117.6 5.2 %hidden_second.1.late_ref = bf16[224,896]{1,0:T(8,128)(2,1)S(1)} custom-call(bf16[4,32,2048]{2,1,0:T(8,128)(2,1)S(1)} %pad_maximum_fusion.1.l0, bf16[4,32,2048]{2,1,0:T(8,128)(2,1)S(1)} %collective-permute-done.19.l1, bf16[4,32,2048]{2,1,0:T(8,128)(2,1)S(1)} %collective-permute-done.20.l3, bf16[4,32,2048]{2,1,0:T(8,128)(2,1)S(1)} %pad_maximum_fusion.2.h0, ...), custom_call_target="tpu_custom_call" | custom-call | tf_op jit(solution)/shard_map/hidden_second/pallas_call | solution.py:232
  122.8 3.0 %down_high.1 = (bf16[128,2048]{1,0:T(8,128)(2,1)S(1)}, bf16[128,2048]{1,0:T(8,128)(2,1)S(1)}, bf16[128,2048]{1,0:T(8,128)(2,1)S(1)}, bf16[128,2048]{1,0:T(8,128)(2,1)S(1)}) custom-call(bf16[288,896]{1,0:T(8,128)(2,1)S(1)} %get-tuple-element.59.early_ref, bf16[224,896]{1,0:T(8,128)(2,1)S(1)} %hidden_second.1.late_ref, bf16[1,896,4096]{2,1,0:T(8,128)(2,1)S(1)} %bitcast.31), custom_call_target="tpu_custom_call" | custom-call | tf_op jit(solution)/shard_map/down_high/pallas_call | solution.py:260
  127.4 3.0 %down_low.1 = (bf16[128,2048]{1,0:T(8,128)(2,1)S(1)}, bf16[128,2048]{1,0:T(8,128)(2,1)S(1)}, bf16[128,2048]{1,0:T(8,128)(2,1)S(1)}, bf16[128,2048]{1,0:T(8,128)(2,1)S(1)}) custom-call(bf16[288,896]{1,0:T(8,128)(2,1)S(1)} %get-tuple-element.59.early_ref, bf16[224,896]{1,0:T(8,128)(2,1)S(1)} %hidden_second.1.late_ref, bf16[1,896,4096]{2,1,0:T(8,128)(2,1)S(1)} %bitcast.31), custom_call_target="tpu_custom_call" | custom-call | tf_op jit(solution)/shard_map/down_low/pallas_call | solution.py:260
  131.2 4.0 %collective-permute-done.33.b = bf16[128,2048]{1,0:T(8,128)(2,1)S(1)} collective-permute-done((bf16[128,2048]{1,0:T(8,128)(2,1)S(1)}, bf16[128,2048]{1,0:T(8,128)(2,1)S(1)}, u32[]{:S(2)}, u32[]{:S(2)}) %collective-permute-start.33) | collective-permute-done | bytes 524320 | tf_op jit(solution)/shard_map/ppermute | solution.py:38
  136.9 15.7 %collective-permute-done.35.d = bf16[128,2048]{1,0:T(8,128)(2,1)S(1)} collective-permute-done((bf16[128,2048]{1,0:T(8,128)(2,1)S(1)}, bf16[128,2048]{1,0:T(8,128)(2,1)S(1)}, u32[]{:S(2)}, u32[]{:S(2)}) %collective-permute-start.35) | collective-permute-done | bytes 524320 | tf_op jit(solution)/shard_map/ppermute | solution.py:38
  157.7 2.6 %collective-permute-start.31 = (bf16[32,2048]{1,0:T(8,128)(2,1)S(1)}, bf16[32,2048]{1,0:T(8,128)(2,1)S(1)}, u32[]{:S(2)}, u32[]{:S(2)}) collective-permute-start(bf16[32,2048]{1,0:T(8,128)(2,1)S(1)} %get-tuple-element.67), channel_id=1, source_target_pairs={{0,16},{8,24},{16,0},{24,8},{32,48},{40,56},{48,32},{56,40},{64,80... | collective-permute-start | bytes 393224 | tf_op jit(solution)/shard_map/ppermute | solution.py:38
  166.2 10.2 %all-to-all-start.1 = ((bf16[8,32,512]{2,1,0:T(8,128)(2,1)}), bf16[8,32,512]{2,1,0:T(8,128)(2,1)S(1)}, u32[]{:S(2)}, u32[]{:S(2)}) async-start(bf16[8,32,512]{2,1,0:T(8,128)(2,1)} %add_last.1), calls=%async_computation.1 | async-start | bytes 524288 | tf_op jit(solution)/shard_map/all_to_all | solution.py:416
  176.8 6.1 %all-to-all-done.1 = bf16[8,32,512]{2,1,0:T(8,128)(2,1)S(1)} async-done(((bf16[8,32,512]{2,1,0:T(8,128)(2,1)}), bf16[8,32,512]{2,1,0:T(8,128)(2,1)S(1)}, u32[]{:S(2)}, u32[]{:S(2)}) %all-to-all-start.1) | async-done | bytes 262176 | tf_op jit(solution)/shard_map/all_to_all | solution.py:416
  (124 shorter events, 52.8 us)
Async XLA Ops:
  2.3 9.8 %collective-permute-start = (bf16[64,640]{1,0:T(8,128)(2,1)S(1)}, bf16[64,640]{1,0:T(8,128)(2,1)S(1)}, u32[]{:S(2)}, u32[]{:S(2)}) collective-permute-start(bf16[64,640]{1,0:T(8,128)(2,1)S(1)} %get-tuple-element.79), channel_id=1, source_target_pairs={{0,8},{8,16},{16,24},{24,0},{32,40},{40,48},{48,56},{56,32},{64,72... | collective-permute-start | bytes 245768 | tf_op jit(solution)/shard_map/ppermute | solution.py:38
  12.2 9.0 %collective-permute-start.3 = (bf16[4,64,640]{2,1,0:T(8,128)(2,1)S(1)}, bf16[4,64,640]{2,1,0:T(8,128)(2,1)S(1)}, u32[]{:S(2)}, u32[]{:S(2)}) collective-permute-start(bf16[4,64,640]{2,1,0:T(8,128)(2,1)S(1)} %pad_maximum_fusion.3.q_ref), channel_id=1, source_target_pairs={{0,32},{8,40},{16,48},{24,56},{32,64},{40,72},{48,80},{56,88},{64,... | collective-permute-start | bytes 983048 | tf_op jit(solution)/shard_map/ppermute | solution.py:38
  21.2 14.6 %collective-permute-start.6 = (bf16[2,64,640]{2,1,0:T(8,128)(2,1)S(1)}, bf16[2,64,640]{2,1,0:T(8,128)(2,1)S(1)}, u32[]{:S(2)}, u32[]{:S(2)}) collective-permute-start(bf16[2,64,640]{2,1,0:T(8,128)(2,1)S(1)} %slice.18), channel_id=1, source_target_pairs={{0,32},{8,40},{16,48},{24,56},{32,64},{40,72},{48,80},{56,88},{64,... | collective-permute-start | bytes 491528 | tf_op jit(solution)/shard_map/ppermute | solution.py:38
  22.2 13.6 %collective-permute-start.7 = (bf16[2,64,640]{2,1,0:T(8,128)(2,1)S(1)}, bf16[2,64,640]{2,1,0:T(8,128)(2,1)S(1)}, u32[]{:S(2)}, u32[]{:S(2)}) collective-permute-start(bf16[2,64,640]{2,1,0:T(8,128)(2,1)S(1)} %slice.19), channel_id=1, source_target_pairs={{0,96},{8,104},{16,112},{24,120},{32,0},{40,8},{48,16},{56,24},{64... | collective-permute-start | bytes 491528 | tf_op jit(solution)/shard_map/ppermute | solution.py:38
  57.7 18.2 %all-to-all-start = ((bf16[8,32,512]{2,1,0:T(8,128)(2,1)}), bf16[8,32,512]{2,1,0:T(8,128)(2,1)S(1)}, u32[]{:S(2)}, u32[]{:S(2)}) async-start(bf16[8,32,512]{2,1,0:T(8,128)(2,1)} %bitcast.12), calls=%async_computation | async-start | bytes 524288 | tf_op jit(solution)/shard_map/all_to_all | solution.py:401
  76.2 9.3 %collective-permute-start.14 = (bf16[32,2048]{1,0:T(8,128)(2,1)S(1)}, bf16[32,2048]{1,0:T(8,128)(2,1)S(1)}, u32[]{:S(2)}, u32[]{:S(2)}) collective-permute-start(bf16[32,2048]{1,0:T(8,128)(2,1)S(1)} %get-tuple-element.51), channel_id=1, source_target_pairs={{0,16},{8,24},{16,0},{24,8},{32,48},{40,56},{48,32},{56,40},{64,80... | collective-permute-start | bytes 393224 | tf_op jit(solution)/shard_map/ppermute | solution.py:38
  77.8 7.7 %collective-permute-start.15 = (bf16[32,2048]{1,0:T(8,128)(2,1)S(1)}, bf16[32,2048]{1,0:T(8,128)(2,1)S(1)}, u32[]{:S(2)}, u32[]{:S(2)}) collective-permute-start(bf16[32,2048]{1,0:T(8,128)(2,1)S(1)} %get-tuple-element.51), channel_id=1, source_target_pairs={{0,24},{8,0},{16,8},{24,16},{32,56},{40,32},{48,40},{56,48},{64,88... | collective-permute-start | bytes 393224 | tf_op jit(solution)/shard_map/ppermute | solution.py:38
  89.0 12.6 %collective-permute-start.21 = (bf16[4,32,2048]{2,1,0:T(8,128)(2,1)S(1)}, bf16[4,32,2048]{2,1,0:T(8,128)(2,1)S(1)}, u32[]{:S(2)}, u32[]{:S(2)}) collective-permute-start(bf16[4,32,2048]{2,1,0:T(8,128)(2,1)S(1)} %pad_maximum_fusion.2.h0), channel_id=1, source_target_pairs={{0,8},{8,16},{16,24},{24,0},{32,40},{40,48},{48,56},{56,32},{64,72... | collective-permute-start | bytes 1572872 | tf_op jit(solution)/shard_map/ppermute | solution.py:38
  89.1 12.6 %collective-permute-start.22 = (bf16[4,32,2048]{2,1,0:T(8,128)(2,1)S(1)}, bf16[4,32,2048]{2,1,0:T(8,128)(2,1)S(1)}, u32[]{:S(2)}, u32[]{:S(2)}) collective-permute-start(bf16[4,32,2048]{2,1,0:T(8,128)(2,1)S(1)} %pad_maximum_fusion.2.h0), channel_id=1, source_target_pairs={{0,24},{8,0},{16,8},{24,16},{32,56},{40,32},{48,40},{56,48},{64,88... | collective-permute-start | bytes 1572872 | tf_op jit(solution)/shard_map/ppermute | solution.py:38
  91.8 12.6 %collective-permute-start.19 = (bf16[4,32,2048]{2,1,0:T(8,128)(2,1)S(1)}, bf16[4,32,2048]{2,1,0:T(8,128)(2,1)S(1)}, u32[]{:S(2)}, u32[]{:S(2)}) collective-permute-start(bf16[4,32,2048]{2,1,0:T(8,128)(2,1)S(1)} %pad_maximum_fusion.1.l0), channel_id=1, source_target_pairs={{0,32},{8,40},{16,48},{24,56},{32,64},{40,72},{48,80},{56,88},{64,... | collective-permute-start | bytes 1572872 | tf_op jit(solution)/shard_map/ppermute | solution.py:38
  91.9 12.7 %collective-permute-start.20 = (bf16[4,32,2048]{2,1,0:T(8,128)(2,1)S(1)}, bf16[4,32,2048]{2,1,0:T(8,128)(2,1)S(1)}, u32[]{:S(2)}, u32[]{:S(2)}) collective-permute-start(bf16[4,32,2048]{2,1,0:T(8,128)(2,1)S(1)} %pad_maximum_fusion.1.l0), channel_id=1, source_target_pairs={{0,96},{8,104},{16,112},{24,120},{32,0},{40,8},{48,16},{56,24},{64... | collective-permute-start | bytes 1572872 | tf_op jit(solution)/shard_map/ppermute | solution.py:38
  101.6 15.9 %collective-permute-start.25 = (bf16[2,32,2048]{2,1,0:T(8,128)(2,1)S(1)}, bf16[2,32,2048]{2,1,0:T(8,128)(2,1)S(1)}, u32[]{:S(2)}, u32[]{:S(2)}) collective-permute-start(bf16[2,32,2048]{2,1,0:T(8,128)(2,1)S(1)} %slice.26), channel_id=1, source_target_pairs={{0,8},{8,16},{16,24},{24,0},{32,40},{40,48},{48,56},{56,32},{64,72... | collective-permute-start | bytes 786440 | tf_op jit(solution)/shard_map/ppermute | solution.py:38
  101.8 15.8 %collective-permute-start.26 = (bf16[2,32,2048]{2,1,0:T(8,128)(2,1)S(1)}, bf16[2,32,2048]{2,1,0:T(8,128)(2,1)S(1)}, u32[]{:S(2)}, u32[]{:S(2)}) collective-permute-start(bf16[2,32,2048]{2,1,0:T(8,128)(2,1)S(1)} %slice.27), channel_id=1, source_target_pairs={{0,24},{8,0},{16,8},{24,16},{32,56},{40,32},{48,40},{56,48},{64,88... | collective-permute-start | bytes 786440 | tf_op jit(solution)/shard_map/ppermute | solution.py:38
  104.5 13.0 %collective-permute-start.23 = (bf16[2,32,2048]{2,1,0:T(8,128)(2,1)S(1)}, bf16[2,32,2048]{2,1,0:T(8,128)(2,1)S(1)}, u32[]{:S(2)}, u32[]{:S(2)}) collective-permute-start(bf16[2,32,2048]{2,1,0:T(8,128)(2,1)S(1)} %slice.24), channel_id=1, source_target_pairs={{0,32},{8,40},{16,48},{24,56},{32,64},{40,72},{48,80},{56,88},{64,... | collective-permute-start | bytes 786440 | tf_op jit(solution)/shard_map/ppermute | solution.py:38
  104.6 12.9 %collective-permute-start.24 = (bf16[2,32,2048]{2,1,0:T(8,128)(2,1)S(1)}, bf16[2,32,2048]{2,1,0:T(8,128)(2,1)S(1)}, u32[]{:S(2)}, u32[]{:S(2)}) collective-permute-start(bf16[2,32,2048]{2,1,0:T(8,128)(2,1)S(1)} %slice.25), channel_id=1, source_target_pairs={{0,96},{8,104},{16,112},{24,120},{32,0},{40,8},{48,16},{56,24},{64... | collective-permute-start | bytes 786440 | tf_op jit(solution)/shard_map/ppermute | solution.py:38
  125.9 9.3 %collective-permute-start.33 = (bf16[128,2048]{1,0:T(8,128)(2,1)S(1)}, bf16[128,2048]{1,0:T(8,128)(2,1)S(1)}, u32[]{:S(2)}, u32[]{:S(2)}) collective-permute-start(bf16[128,2048]{1,0:T(8,128)(2,1)S(1)} %get-tuple-element.70), channel_id=1, source_target_pairs={{0,24},{8,0},{16,8},{24,16},{32,56},{40,32},{48,40},{56,48},{64,88... | collective-permute-start | bytes 1572872 | tf_op jit(solution)/shard_map/ppermute | solution.py:38
  125.9 10.9 %collective-permute-start.34 = (bf16[128,2048]{1,0:T(8,128)(2,1)S(1)}, bf16[128,2048]{1,0:T(8,128)(2,1)S(1)}, u32[]{:S(2)}, u32[]{:S(2)}) collective-permute-start(bf16[128,2048]{1,0:T(8,128)(2,1)S(1)} %get-tuple-element.71), channel_id=1, source_target_pairs={{0,16},{8,24},{16,0},{24,8},{32,48},{40,56},{48,32},{56,40},{64,80... | collective-permute-start | bytes 1572872 | tf_op jit(solution)/shard_map/ppermute | solution.py:38
  126.5 26.1 %collective-permute-start.35 = (bf16[128,2048]{1,0:T(8,128)(2,1)S(1)}, bf16[128,2048]{1,0:T(8,128)(2,1)S(1)}, u32[]{:S(2)}, u32[]{:S(2)}) collective-permute-start(bf16[128,2048]{1,0:T(8,128)(2,1)S(1)} %get-tuple-element.72), channel_id=1, source_target_pairs={{0,8},{8,16},{16,24},{24,0},{32,40},{40,48},{48,56},{56,32},{64,72... | collective-permute-start | bytes 1572872 | tf_op jit(solution)/shard_map/ppermute | solution.py:38
  130.4 23.6 %collective-permute-start.27 = (bf16[128,2048]{1,0:T(8,128)(2,1)S(1)}, bf16[128,2048]{1,0:T(8,128)(2,1)S(1)}, u32[]{:S(2)}, u32[]{:S(2)}) collective-permute-start(bf16[128,2048]{1,0:T(8,128)(2,1)S(1)} %get-tuple-element.62), channel_id=1, source_target_pairs={{0,96},{8,104},{16,112},{24,120},{32,0},{40,8},{48,16},{56,24},{64... | collective-permute-start | bytes 1572872 | tf_op jit(solution)/shard_map/ppermute | solution.py:38
  131.2 23.4 %collective-permute-start.28 = (bf16[128,2048]{1,0:T(8,128)(2,1)S(1)}, bf16[128,2048]{1,0:T(8,128)(2,1)S(1)}, u32[]{:S(2)}, u32[]{:S(2)}) collective-permute-start(bf16[128,2048]{1,0:T(8,128)(2,1)S(1)} %get-tuple-element.63), channel_id=1, source_target_pairs={{0,64},{8,72},{16,80},{24,88},{32,96},{40,104},{48,112},{56,120},{... | collective-permute-start | bytes 1572872 | tf_op jit(solution)/shard_map/ppermute | solution.py:38
  135.2 19.5 %collective-permute-start.29 = (bf16[128,2048]{1,0:T(8,128)(2,1)S(1)}, bf16[128,2048]{1,0:T(8,128)(2,1)S(1)}, u32[]{:S(2)}, u32[]{:S(2)}) collective-permute-start(bf16[128,2048]{1,0:T(8,128)(2,1)S(1)} %get-tuple-element.64), channel_id=1, source_target_pairs={{0,32},{8,40},{16,48},{24,56},{32,64},{40,72},{48,80},{56,88},{64,... | collective-permute-start | bytes 1572872 | tf_op jit(solution)/shard_map/ppermute | solution.py:38
  154.0 9.7 %collective-permute-start.38 = (bf16[32,2048]{1,0:T(8,128)(2,1)S(1)}, bf16[32,2048]{1,0:T(8,128)(2,1)S(1)}, u32[]{:S(2)}, u32[]{:S(2)}) collective-permute-start(bf16[32,2048]{1,0:T(8,128)(2,1)S(1)} %get-tuple-element.76), channel_id=1, source_target_pairs={{0,32},{8,40},{16,48},{24,56},{32,64},{40,72},{48,80},{56,88},{64,... | collective-permute-start | bytes 393224 | tf_op jit(solution)/shard_map/ppermute | solution.py:38
  155.2 8.5 %collective-permute-start.30 = (bf16[32,2048]{1,0:T(8,128)(2,1)S(1)}, bf16[32,2048]{1,0:T(8,128)(2,1)S(1)}, u32[]{:S(2)}, u32[]{:S(2)}) collective-permute-start(bf16[32,2048]{1,0:T(8,128)(2,1)S(1)} %get-tuple-element.66), channel_id=1, source_target_pairs={{0,24},{8,0},{16,8},{24,16},{32,56},{40,32},{48,40},{56,48},{64,88... | collective-permute-start | bytes 393224 | tf_op jit(solution)/shard_map/ppermute | solution.py:38
  166.2 16.7 %all-to-all-start.1 = ((bf16[8,32,512]{2,1,0:T(8,128)(2,1)}), bf16[8,32,512]{2,1,0:T(8,128)(2,1)S(1)}, u32[]{:S(2)}, u32[]{:S(2)}) async-start(bf16[8,32,512]{2,1,0:T(8,128)(2,1)} %add_last.1), calls=%async_computation.1 | async-start | bytes 524288 | tf_op jit(solution)/shard_map/all_to_all | solution.py:416
  (24 other events, 231.2 us)
